TPU v7x, 32 devices: a whole 2x2x4 slice. The times are simulated.
32 devices in a mesh: dp: 2 (over x), mp: 4 (over z), section: 4 (over y, core).
Axes of the slice: x: 2, y: 2, z: 4, core: 2. Of those that a mesh axis runs over, the one named last changes fastest.
Arguments:
- hidden: bfloat16 [512, 24576], P('dp', ('mp', 'section')), may hold values from -6 to 6
- fc_weight: bfloat16 [4096, 24576], P('dp', ('mp', 'section')), may hold values from -0.0390625 to 0.0390625
- gain_query: float32 [4096], P(('mp', 'section')), may hold values from 0.25 to 2.5
- gain_key: float32 [4096], P(('mp', 'section')), may hold values from 0.25 to 2.5
- block_mask: int32 [8, 4], P('dp'), may hold values 0 or 1
- cotangent: bfloat16 [2, 512, 4096], P(None, 'dp', ('mp', 'section')), may hold values from -6 to 6
Outputs:
- ttt_out: bfloat16 [2, 512, 4096], P(None, 'dp', ('mp', 'section'))
- fc_grad: float32 [4096, 24576], P('dp', ('mp', 'section'))
All inputs are finite; a program needn't handle non-finite values. No bound on the sum of `block_mask` on one device may be relied on, other than what follows from the above.
Results may differ from a plain program's by a relative error of at most 0.015.
Values may be sent and summed in bfloat16 or wider, within the bound.
No kernel may reach another device: no remote copies, remote signals or barrier semaphores. Data moves between devices by JAX's collectives and lax.ppermute only.
A program may use at most 128 MiB of HBM per device.

v0:
```python
from functools import partial

import jax
import jax.numpy as jnp
from jax import lax
from jax.sharding import PartitionSpec as P

HD = 128


EPS = 1e-06


def rms_scale(values):
    return values * lax.rsqrt(jnp.mean(values * values, axis=-1, keepdims=True) + EPS)


def visible_sets(block_mask, length):
    position = jnp.arange(length, dtype=jnp.int32)
    block_of = position // 64
    onehot = (
        block_of[:, None] == jnp.arange(block_mask.shape[0], dtype=jnp.int32)[None, :]
    ).astype(jnp.float32)
    opened = (
        jnp.dot(
            jnp.dot(onehot, block_mask.astype(jnp.float32), precision=lax.Precision.HIGHEST),
            onehot.T,
            precision=lax.Precision.HIGHEST,
        )
        > 0.5
    )
    earlier = block_of[None, :] < block_of[:, None]
    same_block = block_of[None, :] == block_of[:, None]
    causal = position[None, :] <= position[:, None]
    first = causal & (same_block | opened & earlier)
    second = first & (position[None, :] < position[:, None])
    return (first, second)


def head_steps(joined_head, gain_query, gain_key, first, second):
    scale = joined_head.shape[-1] ** (-0.5)
    normed = rms_scale(joined_head.astype(jnp.float32))
    queries = normed * gain_query
    keys_ctx = normed * gain_key
    scores = jnp.dot(queries, keys_ctx.T, precision=lax.Precision.HIGHEST) * scale
    scores = jnp.where(first, scores, -jnp.inf)
    top_one = jnp.max(scores, axis=-1, keepdims=True)
    expo_one = jnp.exp(scores - top_one)
    weights_one = (expo_one / jnp.sum(expo_one, axis=-1, keepdims=True)).astype(jnp.bfloat16)
    step_one = jnp.dot(weights_one, joined_head, preferred_element_type=jnp.float32).astype(
        jnp.bfloat16
    )
    renorm = rms_scale(step_one.astype(jnp.float32))
    queries_two = renorm * gain_query
    own_key = renorm * gain_key
    scores_two = jnp.dot(queries_two, keys_ctx.T, precision=lax.Precision.HIGHEST) * scale
    scores_two = jnp.where(second, scores_two, -jnp.inf)
    own_score = jnp.sum(queries_two * own_key, axis=-1) * scale
    top_two = jnp.maximum(jnp.max(scores_two, axis=-1), own_score)
    expo_two = jnp.exp(scores_two - top_two[:, None])
    own_expo = jnp.exp(own_score - top_two)
    total = jnp.sum(expo_two, axis=-1) + own_expo
    weights_two = (expo_two / total[:, None]).astype(jnp.bfloat16)
    step_two = jnp.dot(weights_two, joined_head, preferred_element_type=jnp.float32) + (
        own_expo / total
    )[:, None] * step_one.astype(jnp.float32)
    return (step_one, step_two.astype(jnp.bfloat16))


def sequence_steps(joined_seq, gain_query, gain_key, block_mask):
    length, width = joined_seq.shape
    heads = width // HD
    first, second = visible_sets(block_mask, length)
    split = joined_seq.reshape(length, heads, HD).transpose(1, 0, 2)
    one_out, two_out = jax.vmap(head_steps, in_axes=(0, 0, 0, None, None))(
        split, gain_query.reshape(heads, HD), gain_key.reshape(heads, HD), first, second
    )
    return (
        one_out.transpose(1, 0, 2).reshape(length, width),
        two_out.transpose(1, 0, 2).reshape(length, width),
    )


def sequence_train(joined_seq, gain_query, gain_key, block_mask, cot_one, cot_two):
    forward = partial(
        sequence_steps, gain_query=gain_query, gain_key=gain_key, block_mask=block_mask
    )
    outputs, pullback = jax.vjp(forward, joined_seq)
    grads = pullback((cot_one, cot_two))
    return (outputs[0], outputs[1], grads[0])


def per_device(hidden, fc_weight, gain_query, gain_key, block_mask, cotangent):
    partial_joined = lax.dot_general(
        hidden,
        lax.all_gather(fc_weight, "dp", axis=0, tiled=True),
        (((1,), (1,)), ((), ())),
        preferred_element_type=jnp.float32,
    )
    joined = lax.psum_scatter(
        partial_joined, ("mp", "section"), scatter_dimension=1, tiled=True
    ).astype(jnp.bfloat16)
    step_one, step_two, d_joined = sequence_train(
        joined, gain_query, gain_key, block_mask, cotangent[0], cotangent[1]
    )
    ttt_out = jnp.stack([step_one, step_two])
    grad_full = lax.all_gather(d_joined, ("mp", "section"), axis=1, tiled=True)
    fc_grad = lax.psum_scatter(
        lax.dot_general(
            grad_full, hidden, (((0,), (0,)), ((), ())), preferred_element_type=jnp.float32
        ),
        "dp",
        scatter_dimension=0,
        tiled=True,
    )
    return (ttt_out, fc_grad)


def solution(mesh):
    in_specs = (
        P("dp", ("mp", "section")),
        P("dp", ("mp", "section")),
        P(("mp", "section")),
        P(("mp", "section")),
        P("dp", None),
        P(None, "dp", ("mp", "section")),
    )
    out_specs = (P(None, "dp", ("mp", "section")), P("dp", ("mp", "section")))
    return jax.shard_map(
        per_device, mesh=mesh, in_specs=in_specs, out_specs=out_specs, check_vma=False
    )
```

profile of v0, /device:TPU:0, one launch (start us, length us, event | category | flops | bytes accessed | tf_op | source)
XLA Modules:
  0.0 597.4 jit_solution(3495537072250453060)
XLA Ops:
  7.2 0.7 all-gather.3.cloned.1.call-update
  8.0 156.8 %all-gather.3.cloned.1.call-done = bf16[4096,1536]{1,0:T(8,128)(2,1)} async-done(((bf16[2048,1536]{1,0:T(8,128)(2,1)}), bf16[4096,1536]{1,0:T(8,128)(2,1)}) %all-gather.3.cloned.1.call-update) | async-done | bytes 12582928 | tf_op jit(solution)/shard_map/all_gather | solution.py:96
  164.8 14.0 %fusion.107 = f32[256,4096]{1,0:T(8,128)} fusion(bf16[256,1536]{1,0:T(8,128)(2,1)S(1)} %copy-done, bf16[4096,1536]{1,0:T(8,128)(2,1)} %all-gather.3.cloned.1.call-done), kind=kOutput, calls=%fused_computation.165 | convolution fusion | flops 3221225472 | bytes 17563648 | tf_op jit(solution)/shard_map/dot_general | solution.py:94
  178.9 0.3 fusion.79
  179.2 0.4 fusion.57
  180.2 71.2 %reduce-scatter.3.cloned.1.call-done = f32[256,256]{1,0:T(8,128)} async-done(((f32[256,4096]{1,0:T(8,128)}), f32[256,256]{1,0:T(8,128)}) %reduce-scatter.3.cloned.1.call-update) | async-done | bytes 262160 | tf_op jit(solution)/shard_map/reduce_scatter | solution.py:100
  251.4 1.0 convert_element_type.83
  252.6 0.8 fusion.105
  253.5 0.2 convert_reduce_fusion
  253.7 0.2 fusion.42
  254.0 0.8 fusion.106
  255.0 0.4 convert_reduce_fusion.1
  255.5 0.8 fusion.19
  256.4 0.7 fusion.44
  257.2 0.2 convolution_convert_fusion.3
  257.4 0.3 multiply_reduce_fusion
  257.9 0.6 convolution_multiply_fusion.2
  258.4 0.9 fusion.39
  259.3 0.9 fusion.12
  260.3 40.6 %all-gather.5.cloned.1.call-done = bf16[256,4096]{0,1:T(8,128)(2,1)} async-done(((bf16[256,256]{0,1:T(8,128)(2,1)}), bf16[256,4096]{0,1:T(8,128)(2,1)}) %all-gather.5.cloned.1.call-update) | async-done | bytes 2097168 | tf_op jit(solution)/shard_map/all_gather | solution.py:107
  300.9 11.7 %fusion.108 = f32[4096,1536]{1,0:T(8,128)} fusion(bf16[256,4096]{0,1:T(8,128)(2,1)} %all-gather.5.cloned.1.call-done, bf16[256,1536]{1,0:T(8,128)(2,1)S(1)} %copy-done), kind=kOutput, calls=%fused_computation.166 | convolution fusion | flops 3221225472 | bytes 28049408 | tf_op jit(solution)/shard_map/dot_general | solution.py:109
  312.8 0.2 fusion.9
  313.2 0.7 pad_maximum_fusion
  313.9 277.0 %reduce-scatter.5.cloned.1.call-done = f32[2048,1536]{1,0:T(8,128)} async-done(((f32[4096,1536]{1,0:T(8,128)}), f32[2048,1536]{1,0:T(8,128)}) %reduce-scatter.5.cloned.1.call-update) | async-done | bytes 12582928 | tf_op jit(solution)/shard_map/reduce_scatter | solution.py:108
  (47 shorter events, 2.0 us)
Async XLA Ops:
  7.2 157.7 %copy-start = (bf16[256,1536]{1,0:T(8,128)(2,1)S(1)}, bf16[256,1536]{1,0:T(8,128)(2,1)}, u32[]{:S(2)}) copy-start(bf16[256,1536]{1,0:T(8,128)(2,1)} %param.6) | copy-start | bytes 2359300
  7.2 157.6 %all-gather.3.cloned.1.call-start = ((), (), s32[]{:S(2)}) async-start(), calls=%async_computation.2 | async-start | bytes 18874368 | tf_op jit(solution)/shard_map/all_gather | solution.py:96
  7.9 171.0 %copy-start.4 = (s32[4,4]{1,0:T(4,128)S(1)}, s32[4,4]{1,0:T(4,128)}, u32[]{:S(2)}) copy-start(s32[4,4]{1,0:T(4,128)} %param.10) | copy-start | bytes 196
  7.9 172.0 %copy-start.1 = (bf16[2,256,256]{2,1,0:T(8,128)(2,1)S(1)}, bf16[2,256,256]{2,1,0:T(8,128)(2,1)}, u32[]{:S(2)}) copy-start(bf16[2,256,256]{2,1,0:T(8,128)(2,1)} %param.11) | copy-start | bytes 786436
  7.9 244.6 %copy-start.2 = (f32[256]{0:T(256)S(1)}, f32[256]{0:T(256)}, u32[]{:S(2)}) copy-start(f32[256]{0:T(256)} %param.9) | copy-start | bytes 3076
  7.9 244.6 %copy-start.3 = (f32[256]{0:T(256)S(1)}, f32[256]{0:T(256)}, u32[]{:S(2)}) copy-start(f32[256]{0:T(256)} %param.8) | copy-start | bytes 3076
  8.0 243.5 %reduce-scatter.3.cloned.1.call-start = ((), (), s32[]{:S(2)}) async-start(), calls=%async_computation.3 | async-start | bytes 4456448 | tf_op jit(solution)/shard_map/reduce_scatter | solution.py:100
  178.9 122.1 %all-gather.5.cloned.1.call-start = ((), (), s32[]{:S(2)}) async-start(), calls=%async_computation.4 | async-start | bytes 2228224 | tf_op jit(solution)/shard_map/all_gather | solution.py:107
  260.3 330.6 %reduce-scatter.5.cloned.1.call-start = ((), (), s32[]{:S(2)}) async-start(), calls=%async_computation.5 | async-start | bytes 37748736 | tf_op jit(solution)/shard_map/reduce_scatter | solution.py:108
Sparse Core Ops, SparseCore 0:
  9.6 155.2 all-gather.2
  179.0 72.3 reduce-scatter.2
  260.4 40.4 all-gather.4
  312.8 278.0 reduce-scatter.4
where the time goes:
time: 598 us; the launch traced here: 597 us
  waiting for transfers between devices  546 us (91%)
  matrix products  33.2 us (6%)
  between operations  14.1 us (2%)
    reduce_scatter x1, waiting for transfers between devices, per_device(): lax.psum_scatter(lax.dot_general(grad_full, hidden, (((0,), (0,)), ((), (...  277 us
    all_gather x1, waiting for transfers between devices, per_device(): lax.all_gather(fc_weight, 'dp', axis=0, tiled=True)  157 us
    reduce_scatter x1, waiting for transfers between devices, per_device(): lax.psum_scatter(partial_joined, ('mp', 'section'), scatter_dimension=1,...  71.2 us
    all_gather x1, waiting for transfers between devices, per_device(): grad_full = lax.all_gather(d_joined, ('mp', 'section'), axis=1, tiled=True)  40.6 us
    dot_general x1, matrix products, per_device(): lax.dot_general(hidden, lax.all_gather(fc_weight, 'dp', axis=0, tiled=Tru...  14 us
  transfers between devices with their start and end apart: 4, of which 4 were waited for; matrix products, arithmetic and copies ran while one was open for 0% of the time, Pallas kernels for 0%

commit v1 on v0

--- a/solution.py
+++ b/solution.py
@@ -3,6 +3,8 @@
 import jax
 import jax.numpy as jnp
 from jax import lax
+from jax.experimental import pallas as pl
+from jax.experimental.pallas import tpu as pltpu
 from jax.sharding import PartitionSpec as P
 
 HD = 128
@@ -90,7 +92,7 @@
     return (outputs[0], outputs[1], grads[0])
 
 
-def per_device(hidden, fc_weight, gain_query, gain_key, block_mask, cotangent):
+def gather_weights_plan(hidden, fc_weight, gain_query, gain_key, block_mask, cotangent):
     partial_joined = lax.dot_general(
         hidden,
         lax.all_gather(fc_weight, "dp", axis=0, tiled=True),
@@ -114,6 +116,218 @@
         tiled=True,
     )
     return (ttt_out, fc_grad)
+
+
+def take(array, index):
+    return lax.dynamic_index_in_dim(array, index, 0, keepdims=False)
+
+
+def swap(axis, size, bit):
+    return lambda array: lax.ppermute(array, axis, [(i, i ^ bit) for i in range(size)])
+
+
+def half_product_kernel(core_ref, hidden_ref, weight_ref, out_ref, rows, sems):
+    core = core_ref[0]
+    copies = []
+    for y in range(2):
+        for z0 in range(2):
+            block = 4 * z0 + 2 * y + core
+            copy = pltpu.make_async_copy(
+                weight_ref.at[pl.ds(block * 2 * HD, 2 * HD)], rows.at[2 * y + z0], sems.at[2 * y + z0]
+            )
+            copy.start()
+            copies.append(copy)
+    for y in range(2):
+        for z0 in range(2):
+            copies[2 * y + z0].wait()
+            product = lax.dot_general(
+                hidden_ref[...],
+                rows[2 * y + z0],
+                (((1,), (1,)), ((), ())),
+                preferred_element_type=jnp.float32,
+            )
+            out_ref[y, z0] = product[:, :HD].astype(out_ref.dtype)
+            out_ref[y, 2 + z0] = product[:, HD:].astype(out_ref.dtype)
+
+
+def half_product(hidden, weight, core, dtype):
+    tokens, features = hidden.shape
+    vmem = pl.BlockSpec(memory_space=pltpu.VMEM)
+    return pl.pallas_call(
+        half_product_kernel,
+        grid_spec=pltpu.PrefetchScalarGridSpec(
+            num_scalar_prefetch=1,
+            grid=(),
+            in_specs=[vmem, pl.BlockSpec(memory_space=pl.ANY)],
+            out_specs=vmem,
+            scratch_shapes=[
+                pltpu.VMEM((4, 2 * HD, features), weight.dtype),
+                pltpu.SemaphoreType.DMA((4,)),
+            ],
+        ),
+        out_shape=jax.ShapeDtypeStruct((2, 4, tokens, HD), dtype),
+        compiler_params=pltpu.CompilerParams(vmem_limit_bytes=24 << 20),
+        cost_estimate=pl.CostEstimate(
+            flops=2 * tokens * features * 8 * HD,
+            bytes_accessed=2 * features * 8 * HD + 2 * tokens * features,
+            transcendentals=0,
+        ),
+    )(core.reshape(1), hidden, weight)
+
+
+def grad_kernel(table_ref, own_ref, other_ref, hidden_ref, hidden_other_ref, *rest):
+    out_ref, total, sems = rest[-3:]
+    groups = own_ref.shape[0] // 4
+    copies = []
+    for g in range(groups):
+        left = jnp.concatenate([own_ref[4 * g + i] for i in range(4)], axis=0)
+        right = jnp.concatenate([other_ref[4 * g + i] for i in range(4)], axis=0)
+        total[g] = jnp.dot(left, hidden_ref[...], preferred_element_type=jnp.float32) + jnp.dot(
+            right, hidden_other_ref[...], preferred_element_type=jnp.float32
+        )
+        for i in range(4):
+            row = pl.multiple_of(table_ref[4 * g + i] * HD, HD)
+            copy = pltpu.make_async_copy(
+                total.at[g, pl.ds(i * HD, HD)], out_ref.at[pl.ds(row, HD)], sems.at[4 * g + i]
+            )
+            copy.start()
+            copies.append(copy)
+    for copy in copies:
+        copy.wait()
+
+
+def grad_rows(table, own, other, hidden, hidden_other, rows, previous=None):
+    heads = own.shape[0]
+    tokens, features = hidden.shape
+    vmem = pl.BlockSpec(memory_space=pltpu.VMEM)
+    hbm = pl.BlockSpec(memory_space=pl.ANY)
+    args = [table, own, other, hidden, hidden_other] + ([] if previous is None else [previous])
+    return pl.pallas_call(
+        grad_kernel,
+        grid_spec=pltpu.PrefetchScalarGridSpec(
+            num_scalar_prefetch=1,
+            grid=(),
+            in_specs=[vmem] * 4 + ([] if previous is None else [hbm]),
+            out_specs=hbm,
+            scratch_shapes=[
+                pltpu.VMEM((heads // 4, 4 * HD, features), jnp.float32),
+                pltpu.SemaphoreType.DMA((heads,)),
+            ],
+        ),
+        out_shape=jax.ShapeDtypeStruct((rows, features), jnp.float32),
+        input_output_aliases={} if previous is None else {5: 0},
+        compiler_params=pltpu.CompilerParams(vmem_limit_bytes=32 << 20),
+        cost_estimate=pl.CostEstimate(
+            flops=4 * heads * HD * tokens * features,
+            bytes_accessed=4 * heads * HD * features,
+            transcendentals=0,
+        ),
+    )(*args)
+
+
+def head_train(joined, gain_query, gain_key, block_mask, cot_one, cot_two):
+    first, second = visible_sets(block_mask, joined.shape[0])
+    outputs, pullback = jax.vjp(
+        lambda j: head_steps(j, gain_query, gain_key, first, second), joined
+    )
+    return outputs[0], outputs[1], pullback((cot_one, cot_two))[0]
+
+
+def keep_weights_plan(hidden, fc_weight, gain_query, gain_key, block_mask, cotangent):
+    me_dp = lax.axis_index("dp")
+    me_z = lax.axis_index("mp")
+    me_y = lax.axis_index("section") // 2
+    me_c = lax.axis_index("section") % 2
+    upper = me_z // 2
+    over_x = swap("dp", 2, 1)
+    over_y = swap("section", 4, 2)
+    over_c = swap("section", 4, 1)
+    over_z = [swap("mp", 4, bit) for bit in range(4)]
+
+    def route(r):
+        return [
+            (4 * d + 2 * e + b, 4 * e + 2 * (d ^ r) + b)
+            for d in range(2)
+            for e in range(2)
+            for b in range(2)
+        ]
+
+    hidden_other = over_x(hidden)
+    tokens = hidden.shape[0]
+    cot_heads = cotangent.reshape(2, tokens, 2, HD)
+    cot_in = []
+    for r in range(2):
+        head = me_dp ^ r
+        sent = lax.dynamic_index_in_dim(cot_heads, head, 2, keepdims=False)
+        cot_in.append(lax.ppermute(sent, ("dp", "mp"), route(r)))
+    gains = jnp.stack([gain_query, gain_key]).reshape(2, 2, HD)
+    gains = lax.ppermute(
+        lax.dynamic_index_in_dim(gains, me_dp, 1, keepdims=False), ("dp", "mp"), route(0)
+    )
+    mask_other = over_x(block_mask)
+    own_first = upper == me_dp
+    cot_own = jnp.where(own_first, cot_in[0], cot_in[1])
+    cot_other = jnp.where(own_first, cot_in[1], cot_in[0])
+
+    def scatter_sum(tokens_in):
+        sent = half_product(tokens_in, fc_weight, 1 - me_c, jnp.bfloat16)
+        kept = half_product(tokens_in, fc_weight, me_c, jnp.float32)
+        got = over_c(sent)
+        sums = kept + got.astype(jnp.float32)
+        got = over_y(take(sums, 1 - me_y).astype(jnp.bfloat16))
+        sums = take(sums, me_y) + got.astype(jnp.float32)
+        pieces = [over_z[b](take(sums, me_z ^ b).astype(jnp.bfloat16)) for b in (1, 2, 3)]
+        total = take(sums, me_z)
+        for piece in pieces:
+            total = total + piece.astype(jnp.float32)
+        return total.astype(jnp.bfloat16)
+
+    def spread(piece):
+        part = jnp.stack([piece] + [over_z[b](piece) for b in (1, 2, 3)])
+        near = jnp.concatenate([part, over_y(part)])
+        return near, over_c(near)
+
+    joined_own = scatter_sum(hidden)
+    joined_other = scatter_sum(hidden_other)
+    one_own, two_own, d_own = head_train(
+        joined_own, gains[0], gains[1], block_mask, cot_own[0], cot_own[1]
+    )
+    near_own, far_own = spread(d_own.T)
+    one_other, two_other, d_other = head_train(
+        joined_other, gains[0], gains[1], mask_other, cot_other[0], cot_other[1]
+    )
+    near_other, far_other = spread(d_other.T)
+
+    def table(core):
+        ys = jnp.arange(2)[:, None]
+        zs = jnp.arange(4)[None, :]
+        z = me_z ^ zs
+        y = me_y ^ ys
+        return (2 * (4 * (z % 2) + 2 * y + core) + z // 2).reshape(8).astype(jnp.int32)
+
+    rows = fc_weight.shape[0]
+    fc_grad = grad_rows(table(me_c), near_own, near_other, hidden, hidden_other, rows)
+    fc_grad = grad_rows(
+        table(1 - me_c), far_own, far_other, hidden, hidden_other, rows, fc_grad
+    )
+    out_own = jnp.stack([one_own, two_own])
+    out_other = jnp.stack([one_other, two_other])
+    heads_back = []
+    for r in range(2):
+        back = [(b, a) for a, b in route(r)]
+        sent = jnp.where((upper ^ r) == me_dp, out_own, out_other)
+        heads_back.append(lax.ppermute(sent, ("dp", "mp"), back))
+    low = jnp.where(me_dp == 0, heads_back[0], heads_back[1])
+    high = jnp.where(me_dp == 0, heads_back[1], heads_back[0])
+    ttt_out = jnp.concatenate([low, high], axis=2)
+    return (ttt_out, fc_grad)
+
+
+def per_device(sizes, hidden, fc_weight, *rest):
+    heads = fc_weight.shape[0] // HD
+    if sizes == (2, 4, 4) and heads == 16 and rest[0].shape[0] == 2 * HD:
+        return keep_weights_plan(hidden, fc_weight, *rest)
+    return gather_weights_plan(hidden, fc_weight, *rest)
 
 
 def solution(mesh):
@@ -126,6 +340,7 @@
         P(None, "dp", ("mp", "section")),
     )
     out_specs = (P(None, "dp", ("mp", "section")), P("dp", ("mp", "section")))
+    sizes = tuple(mesh.shape[name] for name in ("dp", "mp", "section"))
     return jax.shard_map(
-        per_device, mesh=mesh, in_specs=in_specs, out_specs=out_specs, check_vma=False
-    )
+        partial(per_device, sizes), mesh=mesh, in_specs=in_specs, out_specs=out_specs, check_vma=False
+    )

time: 598 us -> 151 us (0.25)
  waiting for transfers between devices: 546 us -> 26.3 us
  starting transfers between devices: 0.16 us -> 38.7 us
  local copies, waits for them, and re-layouts: 0.89 us -> 25.5 us
  Pallas kernels: 0 us -> 24.5 us
  matrix products: 33.2 us -> 16.2 us
  other arithmetic: 2.81 us -> 17 us
  between operations: 14.1 us -> 1.5 us
    reduce_scatter x2 -> x0, waiting for transfers between devices: 348 us -> none  [the longest x1 277 us: per_device(): lax.psum_scatter(lax.dot_general(grad_full, hidden, (((0,), (0,)), ((), (...]
    all_gather x2 -> x0, waiting for transfers between devices: 197 us -> none  [the longest x1 157 us: per_device(): lax.all_gather(fc_weight, 'dp', axis=0, tiled=True)]
    ppermute x0 -> x27, starting transfers between devices: none -> 38.7 us  [the longest x22 32.9 us: swap(): lax.ppermute(array, axis, [(i, i ^ bit) for i in range(size)])]
    ppermute x0 -> x27, waiting for transfers between devices: none -> 26.3 us  [the longest x22 26.3 us: swap(): lax.ppermute(array, axis, [(i, i ^ bit) for i in range(size)])]
    dot_general x2 -> x0, matrix products: 25.8 us -> none  [the longest x1 14 us: per_device(): lax.dot_general(hidden, lax.all_gather(fc_weight, 'dp', axis=0, tiled=Tru...]
    pallas_call x0 -> x6, Pallas kernels: none -> 20.4 us  [the longest x4 10.6 us: half_product(): pl.pallas_call(half_product_kernel, grid_spec=pltpu.PrefetchScalarGridSpe...]
    unnamed x10 -> x55, local copies, waits for them, and re-layouts: 0.03 us -> 16.8 us
  transfers between devices with their start and end apart: 4 -> 27, of which waited for: 4 -> 7; matrix products, arithmetic and copies ran while one was open for 0% -> 16% of each run, Pallas kernels for 0% -> 11%
where the time goes in v1:
time: 151 us; the launch traced here: 150 us
  starting transfers between devices  38.7 us (26%)
  waiting for transfers between devices  26.3 us (17%)
  local copies, waits for them, and re-layouts  25.5 us (17%)
  Pallas kernels  24.5 us (16%)
  other arithmetic  17 us (11%)
  matrix products  16.2 us (11%)
    ppermute x22, starting transfers between devices, swap(): lax.ppermute(array, axis, [(i, i ^ bit) for i in range(size)])  32.9 us
    ppermute x22, waiting for transfers between devices, swap(): lax.ppermute(array, axis, [(i, i ^ bit) for i in range(size)])  26.3 us
    unnamed x55, local copies, waits for them, and re-layouts  16.8 us
    pallas_call x4, Pallas kernels, half_product(): pl.pallas_call(half_product_kernel, grid_spec=pltpu.PrefetchScalarGridSpe...  10.6 us
    pallas_call x2, Pallas kernels, grad_rows(): pl.pallas_call(grad_kernel, grid_spec=pltpu.PrefetchScalarGridSpec(num_sc...  9.86 us
    pallas_call x4, local copies, waits for them, and re-layouts, half_product(): pl.pallas_call(half_product_kernel, grid_spec=pltpu.PrefetchScalarGridSpe...  4.62 us
    dot_general x6, matrix products, head_steps(): jnp.dot(queries, keys_ctx.T, precision=lax.Precision.HIGHEST) * scale  4.35 us
    dot_general x6, matrix products, head_steps(): jnp.dot(queries_two, keys_ctx.T, precision=lax.Precision.HIGHEST) * scale  4.31 us
  transfers between devices with their start and end apart: 27, of which 7 were waited for; matrix products, arithmetic and copies ran while one was open for 16% of the time, Pallas kernels for 11%

profile of v1, /device:TPU:0, one launch (start us, length us, event | category | flops | bytes accessed | tf_op | source)
XLA Modules:
  0.0 149.6 jit_solution(13511064773208297544)
XLA Ops:
  2.1 6.8 %collective-permute-start.6 = (s32[4,4]{1,0:T(4,128)}, s32[4,4]{1,0:T(4,128)S(1)}, u32[]{:S(2)}, u32[]{:S(2)}) collective-permute-start(s32[4,4]{1,0:T(4,128)} %param.10), channel_id=1, source_target_pairs={{0,16},{16,0},{1,17},{17,1},{2,18},{18,2},{3,19},{19,3},{4,20},{20... | collective-permute-start | bytes 200 | tf_op jit(solution)/shard_map/ppermute | solution.py:126
  10.7 2.0 %collective-permute-start.7 = (bf16[256,1536]{1,0:T(8,128)(2,1)}, bf16[256,1536]{1,0:T(8,128)(2,1)S(1)}, u32[]{:S(2)}, u32[]{:S(2)}) collective-permute-start(bf16[256,1536]{1,0:T(8,128)(2,1)} %hidden_ref.7), channel_id=1, source_target_pairs={{0,16},{16,0},{1,17},{17,1},{2,18},{18,2},{3,19},{19,3},{4,20},{20... | collective-permute-start | bytes 2359304 | tf_op jit(solution)/shard_map/ppermute | solution.py:126
  12.7 2.8 %copy-done = bf16[2048,1536]{1,0:T(8,128)(2,1)S(1)} copy-done((bf16[2048,1536]{1,0:T(8,128)(2,1)S(1)}, bf16[2048,1536]{1,0:T(8,128)(2,1)}, u32[]{:S(2)}) %copy-start) | copy-done | bytes 6291480
  16.6 2.6 %shard_map.78 = bf16[2,4,256,128]{3,2,1,0:T(8,128)(2,1)S(1)} custom-call(s32[1]{0:T(128)} %bitcast.1.core_ref, bf16[256,1536]{1,0:T(8,128)(2,1)S(1)} %copy-done.4, bf16[2048,1536]{1,0:T(8,128)(2,1)S(1)} %copy-done), custom_call_target="tpu_custom_call" | custom-call | flops 805306368 | bytes 3932160 | tf_op jit(solution)/shard_map/pallas_call | solution.py:156
  22.9 2.8 %copy-done.1 = bf16[2048,1536]{1,0:T(8,128)(2,1)S(1)} copy-done((bf16[2048,1536]{1,0:T(8,128)(2,1)S(1)}, bf16[2048,1536]{1,0:T(8,128)(2,1)}, u32[]{:S(2)}) %copy-start.1) | copy-done | bytes 6291480
  25.7 2.6 %shard_map.77 = f32[2,4,256,128]{3,2,1,0:T(8,128)S(1)} custom-call(s32[1]{0:T(128)} %bitcast.core_ref, bf16[256,1536]{1,0:T(8,128)(2,1)S(1)} %copy-done.5, bf16[2048,1536]{1,0:T(8,128)(2,1)S(1)} %copy-done.1), custom_call_target="tpu_custom_call" | custom-call | flops 805306368 | bytes 3932160 | tf_op jit(solution)/shard_map/pallas_call | solution.py:156
  36.9 5.6 %collective-permute-done.1 = bf16[4,256,128]{1,2,0:T(8,128)(2,1)S(1)} collective-permute-done((bf16[4,256,128]{1,2,0:T(8,128)(2,1)S(1)}, bf16[4,256,128]{1,2,0:T(8,128)(2,1)S(1)}, u32[]{:S(2)}, u32[]{:S(2)}) %collective-permute-start.1) | collective-permute-done | bytes 262176 | tf_op jit(solution)/shard_map/ppermute | solution.py:126
  44.8 2.4 %collective-permute-start.4 = (bf16[256,128]{0,1:T(8,128)(2,1)}, bf16[256,128]{0,1:T(8,128)(2,1)}, u32[]{:S(2)}, u32[]{:S(2)}) collective-permute-start(bf16[256,128]{0,1:T(8,128)(2,1)} %get-tuple-element.42), channel_id=1, source_target_pairs={{0,12},{4,8},{8,4},{12,0},{1,13},{5,9},{9,5},{13,1},{2,14},{6,10},... | collective-permute-start | bytes 196616 | tf_op jit(solution)/shard_map/ppermute | solution.py:126
  47.3 2.8 %copy-done.2 = bf16[2048,1536]{1,0:T(8,128)(2,1)S(1)} copy-done((bf16[2048,1536]{1,0:T(8,128)(2,1)S(1)}, bf16[2048,1536]{1,0:T(8,128)(2,1)}, u32[]{:S(2)}) %copy-start.2) | copy-done | bytes 6291480
  50.1 2.6 %shard_map.80 = bf16[2,4,256,128]{3,2,1,0:T(8,128)(2,1)S(1)} custom-call(s32[1]{0:T(128)} %bitcast.1.core_ref, bf16[256,1536]{1,0:T(8,128)(2,1)S(1)} %collective-permute-done.7.hidden_ref.hidden_other_ref, bf16[2048,1536]{1,0:T(8,128)(2,1)S(1)} %copy-done.2), custom_call_target="tpu_custom_call" | custom-call | flops 805306368 | bytes 3932160 | tf_op jit(solution)/shard_map/pallas_call | solution.py:156
  53.8 2.8 %copy-done.3 = bf16[2048,1536]{1,0:T(8,128)(2,1)S(1)} copy-done((bf16[2048,1536]{1,0:T(8,128)(2,1)S(1)}, bf16[2048,1536]{1,0:T(8,128)(2,1)}, u32[]{:S(2)}) %copy-start.3) | copy-done | bytes 6291480
  56.5 2.8 %shard_map.79 = f32[2,4,256,128]{3,2,1,0:T(8,128)S(1)} custom-call(s32[1]{0:T(128)} %bitcast.core_ref, bf16[256,1536]{1,0:T(8,128)(2,1)S(1)} %collective-permute-done.7.hidden_ref.hidden_other_ref, bf16[2048,1536]{1,0:T(8,128)(2,1)S(1)} %copy-done.3), custom_call_target="tpu_custom_call" | custom-call | flops 805306368 | bytes 3932160 | tf_op jit(solution)/shard_map/pallas_call | solution.py:156
  63.6 2.0 %online-softmax = f32[256,128]{1,0:T(8,128)} custom-call(f32[256,256]{1,0:T(8,128)} %get-tuple-element.79, f32[256,128]{1,0:T(8,128)} %copy.13), custom_call_target="tpu_custom_call" | custom-call | tf_op online-softmax
  71.6 5.5 %collective-permute-done.9 = bf16[4,256,128]{1,2,0:T(8,128)(2,1)S(1)} collective-permute-done((bf16[4,256,128]{1,2,0:T(8,128)(2,1)S(1)}, bf16[4,256,128]{1,2,0:T(8,128)(2,1)S(1)}, u32[]{:S(2)}, u32[]{:S(2)}) %collective-permute-start.9) | collective-permute-done | bytes 262176 | tf_op jit(solution)/shard_map/ppermute | solution.py:126
  79.1 2.4 %collective-permute-start.12 = (bf16[256,128]{0,1:T(8,128)(2,1)S(1)}, bf16[256,128]{0,1:T(8,128)(2,1)S(1)}, u32[]{:S(2)}, u32[]{:S(2)}) collective-permute-start(bf16[256,128]{0,1:T(8,128)(2,1)S(1)} %get-tuple-element.45), channel_id=1, source_target_pairs={{0,12},{4,8},{8,4},{12,0},{1,13},{5,9},{9,5},{13,1},{2,14},{6,10},... | collective-permute-start | bytes 196616 | tf_op jit(solution)/shard_map/ppermute | solution.py:126
  82.1 3.7 %collective-permute-done.12 = bf16[256,128]{0,1:T(8,128)(2,1)S(1)} collective-permute-done((bf16[256,128]{0,1:T(8,128)(2,1)S(1)}, bf16[256,128]{0,1:T(8,128)(2,1)S(1)}, u32[]{:S(2)}, u32[]{:S(2)}) %collective-permute-start.12) | collective-permute-done | bytes 65568 | tf_op jit(solution)/shard_map/ppermute | solution.py:126
  89.7 2.0 %online-softmax.1 = f32[256,128]{1,0:T(8,128)} custom-call(f32[256,256]{1,0:T(8,128)} %get-tuple-element.86, f32[256,128]{1,0:T(8,128)} %copy.21), custom_call_target="tpu_custom_call" | custom-call | tf_op online-softmax
  110.1 2.4 %collective-permute-start.17 = (bf16[128,256]{1,0:T(8,128)(2,1)S(1)}, bf16[128,256]{1,0:T(8,128)(2,1)S(1)}, u32[]{:S(2)}, u32[]{:S(2)}) collective-permute-start(bf16[128,256]{1,0:T(8,128)(2,1)S(1)} %bitcast.123), channel_id=1, source_target_pairs={{0,4},{4,0},{8,12},{12,8},{1,5},{5,1},{9,13},{13,9},{2,6},{6,2},{1... | collective-permute-start | bytes 196616 | tf_op jit(solution)/shard_map/ppermute | solution.py:126
  116.3 2.4 %collective-permute-start.24 = (bf16[128,256]{1,0:T(8,128)(2,1)S(1)}, bf16[128,256]{1,0:T(8,128)(2,1)S(1)}, u32[]{:S(2)}, u32[]{:S(2)}) collective-permute-start(bf16[128,256]{1,0:T(8,128)(2,1)S(1)} %bitcast.128), channel_id=1, source_target_pairs={{0,12},{4,8},{8,4},{12,0},{1,13},{5,9},{9,5},{13,1},{2,14},{6,10},... | collective-permute-start | bytes 196616 | tf_op jit(solution)/shard_map/ppermute | solution.py:126
  119.4 2.0 %collective-permute-done.23 = bf16[128,256]{1,0:T(8,128)(2,1)S(1)} collective-permute-done((bf16[128,256]{1,0:T(8,128)(2,1)S(1)}, bf16[128,256]{1,0:T(8,128)(2,1)S(1)}, u32[]{:S(2)}, u32[]{:S(2)}) %collective-permute-start.23) | collective-permute-done | bytes 65568 | tf_op jit(solution)/shard_map/ppermute | solution.py:126
  124.2 2.0 %collective-permute-start.14 = (bf16[2,256,128]{1,2,0:T(8,128)(2,1)S(1)}, bf16[2,256,128]{1,2,0:T(8,128)(2,1)S(1)}, u32[]{:S(2)}, u32[]{:S(2)}) collective-permute-start(bf16[2,256,128]{1,2,0:T(8,128)(2,1)S(1)} %get-tuple-element.55), channel_id=1, source_target_pairs={{8,0},{12,4},{24,8},{28,12},{0,16},{4,20},{16,24},{20,28},{9,1},{1... | collective-permute-start | bytes 393224 | tf_op jit(solution)/shard_map/ppermute | solution.py:319
  129.7 7.4 %collective-permute-done.20 = bf16[4,128,256]{2,1,0:T(8,128)(2,1)S(1)} collective-permute-done((bf16[4,128,256]{2,1,0:T(8,128)(2,1)S(1)}, bf16[4,128,256]{2,1,0:T(8,128)(2,1)S(1)}, u32[]{:S(2)}, u32[]{:S(2)}) %collective-permute-start.20) | collective-permute-done | bytes 262176 | tf_op jit(solution)/shard_map/ppermute | solution.py:126
  139.6 4.6 %shard_map.81.rest_0_ = f32[2048,1536]{1,0:T(8,128)} custom-call(s32[8]{0:T(128)S(1)} %add.272.table_ref, bf16[8,128,256]{2,1,0:T(8,128)(2,1)S(1)} %constant_dynamic-update-slice_fusion.own_ref, bf16[8,128,256]{2,1,0:T(8,128)(2,1)S(1)} %constant_dynamic-update-slice_fusion.5.other_ref, bf16[256,1536]{1,0:T(8,128)(2,1)S(1)} %copy-done.5, ...), custom_call_target="tpu_custom_call" | custom-call | flops 1610612736 | bytes 6291456 | tf_op jit(solution)/shard_map/pallas_call | solution.py:205
  144.2 5.3 %shard_map.82 = f32[2048,1536]{1,0:T(8,128)} custom-call(s32[8]{0:T(128)S(1)} %add.267.table_ref, bf16[8,128,256]{2,1,0:T(8,128)(2,1)S(1)} %collective-permute-done.21.own_ref, bf16[8,128,256]{2,1,0:T(8,128)(2,1)} %collective-permute-done.26.other_ref, bf16[256,1536]{1,0:T(8,128)(2,1)S(1)} %copy-done.5, ...), custom_call_target="tpu_custom_call", output_to_operand_aliasing={{}: (5, {})} | custom-call | flops 1610612736 | bytes 6291456 | tf_op jit(solution)/shard_map/pallas_call | solution.py:205
  (188 shorter events, 68.0 us)
Async XLA Ops:
  1.4 33.9 %collective-permute-start.5 = (f32[2,128]{1,0:T(2,128)S(1)}, f32[2,128]{1,0:T(2,128)S(1)}, u32[]{:S(2)}, u32[]{:S(2)}) collective-permute-start(f32[2,128]{1,0:T(2,128)S(1)} %fusion.173), channel_id=1, source_target_pairs={{0,0},{4,4},{8,16},{12,20},{16,8},{20,12},{24,24},{28,28},{1,1},{5... | collective-permute-start | bytes 3080 | tf_op jit(solution)/shard_map/ppermute | solution.py:264
  2.1 28.1 %collective-permute-start.6 = (s32[4,4]{1,0:T(4,128)}, s32[4,4]{1,0:T(4,128)S(1)}, u32[]{:S(2)}, u32[]{:S(2)}) collective-permute-start(s32[4,4]{1,0:T(4,128)} %param.10), channel_id=1, source_target_pairs={{0,16},{16,0},{1,17},{17,1},{2,18},{18,2},{3,19},{19,3},{4,20},{20... | collective-permute-start | bytes 200 | tf_op jit(solution)/shard_map/ppermute | solution.py:126
  10.6 24.7 %collective-permute-start.16 = (bf16[2,256,128]{1,2,0:T(8,128)(2,1)S(1)}, bf16[2,256,128]{1,2,0:T(8,128)(2,1)S(1)}, u32[]{:S(2)}, u32[]{:S(2)}) collective-permute-start(bf16[2,256,128]{1,2,0:T(8,128)(2,1)S(1)} %bitcast.136), channel_id=1, source_target_pairs={{0,8},{4,12},{8,24},{12,28},{16,0},{20,4},{24,16},{28,20},{1,9},{5... | collective-permute-start | bytes 393224 | tf_op jit(solution)/shard_map/ppermute | solution.py:262
  10.7 36.7 %collective-permute-start.7 = (bf16[256,1536]{1,0:T(8,128)(2,1)}, bf16[256,1536]{1,0:T(8,128)(2,1)S(1)}, u32[]{:S(2)}, u32[]{:S(2)}) collective-permute-start(bf16[256,1536]{1,0:T(8,128)(2,1)} %hidden_ref.7), channel_id=1, source_target_pairs={{0,16},{16,0},{1,17},{17,1},{2,18},{18,2},{3,19},{19,3},{4,20},{20... | collective-permute-start | bytes 2359304 | tf_op jit(solution)/shard_map/ppermute | solution.py:126
  20.2 12.1 %collective-permute-start = (bf16[2,4,256,128]{2,3,1,0:T(8,128)(2,1)}, bf16[2,4,256,128]{2,3,1,0:T(8,128)(2,1)S(1)}, u32[]{:S(2)}, u32[]{:S(2)}) collective-permute-start(bf16[2,4,256,128]{2,3,1,0:T(8,128)(2,1)} %copy.10), channel_id=1, source_target_pairs={{0,1},{1,0},{2,3},{3,2},{4,5},{5,4},{6,7},{7,6},{8,9},{9,8},{10,11... | collective-permute-start | bytes 1572872 | tf_op jit(solution)/shard_map/ppermute | solution.py:126
  33.7 8.8 %collective-permute-start.1 = (bf16[4,256,128]{1,2,0:T(8,128)(2,1)S(1)}, bf16[4,256,128]{1,2,0:T(8,128)(2,1)S(1)}, u32[]{:S(2)}, u32[]{:S(2)}) collective-permute-start(bf16[4,256,128]{1,2,0:T(8,128)(2,1)S(1)} %fusion.26), channel_id=1, source_target_pairs={{0,2},{1,3},{2,0},{3,1},{4,6},{5,7},{6,4},{7,5},{8,10},{9,11},{10,... | collective-permute-start | bytes 786440 | tf_op jit(solution)/shard_map/ppermute | solution.py:126
  43.2 17.4 %collective-permute-start.2 = (bf16[256,128]{0,1:T(8,128)(2,1)}, bf16[256,128]{0,1:T(8,128)(2,1)}, u32[]{:S(2)}, u32[]{:S(2)}) collective-permute-start(bf16[256,128]{0,1:T(8,128)(2,1)} %get-tuple-element.41), channel_id=1, source_target_pairs={{0,4},{4,0},{8,12},{12,8},{1,5},{5,1},{9,13},{13,9},{2,6},{6,2},{1... | collective-permute-start | bytes 196616 | tf_op jit(solution)/shard_map/ppermute | solution.py:126
  44.8 15.8 %collective-permute-start.4 = (bf16[256,128]{0,1:T(8,128)(2,1)}, bf16[256,128]{0,1:T(8,128)(2,1)}, u32[]{:S(2)}, u32[]{:S(2)}) collective-permute-start(bf16[256,128]{0,1:T(8,128)(2,1)} %get-tuple-element.42), channel_id=1, source_target_pairs={{0,12},{4,8},{8,4},{12,0},{1,13},{5,9},{9,5},{13,1},{2,14},{6,10},... | collective-permute-start | bytes 196616 | tf_op jit(solution)/shard_map/ppermute | solution.py:126
  47.2 13.4 %collective-permute-start.3 = (bf16[256,128]{0,1:T(8,128)(2,1)}, bf16[256,128]{0,1:T(8,128)(2,1)}, u32[]{:S(2)}, u32[]{:S(2)}) collective-permute-start(bf16[256,128]{0,1:T(8,128)(2,1)} %get-tuple-element.43), channel_id=1, source_target_pairs={{0,8},{4,12},{8,0},{12,4},{1,9},{5,13},{9,1},{13,5},{2,10},{6,14},... | collective-permute-start | bytes 196616 | tf_op jit(solution)/shard_map/ppermute | solution.py:126
  53.7 13.0 %collective-permute-start.8 = (bf16[2,4,256,128]{2,3,1,0:T(8,128)(2,1)}, bf16[2,4,256,128]{2,3,1,0:T(8,128)(2,1)}, u32[]{:S(2)}, u32[]{:S(2)}) collective-permute-start(bf16[2,4,256,128]{2,3,1,0:T(8,128)(2,1)} %copy.18), channel_id=1, source_target_pairs={{0,1},{1,0},{2,3},{3,2},{4,5},{5,4},{6,7},{7,6},{8,9},{9,8},{10,11... | collective-permute-start | bytes 1572872 | tf_op jit(solution)/shard_map/ppermute | solution.py:126
  68.3 8.8 %collective-permute-start.9 = (bf16[4,256,128]{1,2,0:T(8,128)(2,1)S(1)}, bf16[4,256,128]{1,2,0:T(8,128)(2,1)S(1)}, u32[]{:S(2)}, u32[]{:S(2)}) collective-permute-start(bf16[4,256,128]{1,2,0:T(8,128)(2,1)S(1)} %fusion.27), channel_id=1, source_target_pairs={{0,2},{1,3},{2,0},{3,1},{4,6},{5,7},{6,4},{7,5},{8,10},{9,11},{10,... | collective-permute-start | bytes 786440 | tf_op jit(solution)/shard_map/ppermute | solution.py:126
  79.1 6.6 %collective-permute-start.12 = (bf16[256,128]{0,1:T(8,128)(2,1)S(1)}, bf16[256,128]{0,1:T(8,128)(2,1)S(1)}, u32[]{:S(2)}, u32[]{:S(2)}) collective-permute-start(bf16[256,128]{0,1:T(8,128)(2,1)S(1)} %get-tuple-element.45), channel_id=1, source_target_pairs={{0,12},{4,8},{8,4},{12,0},{1,13},{5,9},{9,5},{13,1},{2,14},{6,10},... | collective-permute-start | bytes 196616 | tf_op jit(solution)/shard_map/ppermute | solution.py:126
  109.4 16.7 %collective-permute-start.18 = (bf16[128,256]{1,0:T(8,128)(2,1)S(1)}, bf16[128,256]{1,0:T(8,128)(2,1)S(1)}, u32[]{:S(2)}, u32[]{:S(2)}) collective-permute-start(bf16[128,256]{1,0:T(8,128)(2,1)S(1)} %bitcast.122), channel_id=1, source_target_pairs={{0,8},{4,12},{8,0},{12,4},{1,9},{5,13},{9,1},{13,5},{2,10},{6,14},... | collective-permute-start | bytes 196616 | tf_op jit(solution)/shard_map/ppermute | solution.py:126
  110.1 17.7 %collective-permute-start.17 = (bf16[128,256]{1,0:T(8,128)(2,1)S(1)}, bf16[128,256]{1,0:T(8,128)(2,1)S(1)}, u32[]{:S(2)}, u32[]{:S(2)}) collective-permute-start(bf16[128,256]{1,0:T(8,128)(2,1)S(1)} %bitcast.123), channel_id=1, source_target_pairs={{0,4},{4,0},{8,12},{12,8},{1,5},{5,1},{9,13},{13,9},{2,6},{6,2},{1... | collective-permute-start | bytes 196616 | tf_op jit(solution)/shard_map/ppermute | solution.py:126
  114.2 7.1 %collective-permute-start.23 = (bf16[128,256]{1,0:T(8,128)(2,1)S(1)}, bf16[128,256]{1,0:T(8,128)(2,1)S(1)}, u32[]{:S(2)}, u32[]{:S(2)}) collective-permute-start(bf16[128,256]{1,0:T(8,128)(2,1)S(1)} %bitcast.126), channel_id=1, source_target_pairs={{0,8},{4,12},{8,0},{12,4},{1,9},{5,13},{9,1},{13,5},{2,10},{6,14},... | collective-permute-start | bytes 196616 | tf_op jit(solution)/shard_map/ppermute | solution.py:126
  114.4 8.2 %collective-permute-start.22 = (bf16[128,256]{1,0:T(8,128)(2,1)S(1)}, bf16[128,256]{1,0:T(8,128)(2,1)S(1)}, u32[]{:S(2)}, u32[]{:S(2)}) collective-permute-start(bf16[128,256]{1,0:T(8,128)(2,1)S(1)} %bitcast.127), channel_id=1, source_target_pairs={{0,4},{4,0},{8,12},{12,8},{1,5},{5,1},{9,13},{13,9},{2,6},{6,2},{1... | collective-permute-start | bytes 196616 | tf_op jit(solution)/shard_map/ppermute | solution.py:126
  116.3 7.9 %collective-permute-start.24 = (bf16[128,256]{1,0:T(8,128)(2,1)S(1)}, bf16[128,256]{1,0:T(8,128)(2,1)S(1)}, u32[]{:S(2)}, u32[]{:S(2)}) collective-permute-start(bf16[128,256]{1,0:T(8,128)(2,1)S(1)} %bitcast.128), channel_id=1, source_target_pairs={{0,12},{4,8},{8,4},{12,0},{1,13},{5,9},{9,5},{13,1},{2,14},{6,10},... | collective-permute-start | bytes 196616 | tf_op jit(solution)/shard_map/ppermute | solution.py:126
  121.4 6.6 %collective-permute-start.19 = (bf16[128,256]{1,0:T(8,128)(2,1)S(1)}, bf16[128,256]{1,0:T(8,128)(2,1)S(1)}, u32[]{:S(2)}, u32[]{:S(2)}) collective-permute-start(bf16[128,256]{1,0:T(8,128)(2,1)S(1)} %bitcast.124), channel_id=1, source_target_pairs={{0,12},{4,8},{8,4},{12,0},{1,13},{5,9},{9,5},{13,1},{2,14},{6,10},... | collective-permute-start | bytes 196616 | tf_op jit(solution)/shard_map/ppermute | solution.py:126
  122.6 16.1 %collective-permute-start.13 = (bf16[2,256,128]{1,2,0:T(8,128)(2,1)}, bf16[2,256,128]{1,2,0:T(8,128)(2,1)S(1)}, u32[]{:S(2)}, u32[]{:S(2)}) collective-permute-start(bf16[2,256,128]{1,2,0:T(8,128)(2,1)} %get-tuple-element.54), channel_id=1, source_target_pairs={{0,0},{4,4},{16,8},{20,12},{8,16},{12,20},{24,24},{28,28},{1,1},{5... | collective-permute-start | bytes 393224 | tf_op jit(solution)/shard_map/ppermute | solution.py:319
  124.2 14.5 %collective-permute-start.14 = (bf16[2,256,128]{1,2,0:T(8,128)(2,1)S(1)}, bf16[2,256,128]{1,2,0:T(8,128)(2,1)S(1)}, u32[]{:S(2)}, u32[]{:S(2)}) collective-permute-start(bf16[2,256,128]{1,2,0:T(8,128)(2,1)S(1)} %get-tuple-element.55), channel_id=1, source_target_pairs={{8,0},{12,4},{24,8},{28,12},{0,16},{4,20},{16,24},{20,28},{9,1},{1... | collective-permute-start | bytes 393224 | tf_op jit(solution)/shard_map/ppermute | solution.py:319
  126.2 11.0 %collective-permute-start.25 = (bf16[4,128,256]{2,1,0:T(8,128)(2,1)S(1)}, bf16[4,128,256]{2,1,0:T(8,128)(2,1)S(1)}, u32[]{:S(2)}, u32[]{:S(2)}) collective-permute-start(bf16[4,128,256]{2,1,0:T(8,128)(2,1)S(1)} %pad_maximum_fusion.2), channel_id=1, source_target_pairs={{0,2},{1,3},{2,0},{3,1},{4,6},{5,7},{6,4},{7,5},{8,10},{9,11},{10,... | collective-permute-start | bytes 786440 | tf_op jit(solution)/shard_map/ppermute | solution.py:126
  128.0 9.1 %collective-permute-start.20 = (bf16[4,128,256]{2,1,0:T(8,128)(2,1)S(1)}, bf16[4,128,256]{2,1,0:T(8,128)(2,1)S(1)}, u32[]{:S(2)}, u32[]{:S(2)}) collective-permute-start(bf16[4,128,256]{2,1,0:T(8,128)(2,1)S(1)} %pad_maximum_fusion.1), channel_id=1, source_target_pairs={{0,2},{1,3},{2,0},{3,1},{4,6},{5,7},{6,4},{7,5},{8,10},{9,11},{10,... | collective-permute-start | bytes 786440 | tf_op jit(solution)/shard_map/ppermute | solution.py:126
  137.1 7.0 %collective-permute-start.21 = (bf16[8,128,256]{2,1,0:T(8,128)(2,1)S(1)}, bf16[8,128,256]{2,1,0:T(8,128)(2,1)S(1)}, u32[]{:S(2)}, u32[]{:S(2)}) collective-permute-start(bf16[8,128,256]{2,1,0:T(8,128)(2,1)S(1)} %constant_dynamic-update-slice_fusion.own_ref), channel_id=1, source_target_pairs={{0,1},{1,0},{2,3},{3,2},{4,5},{5,4},{6,7},{7,6},{8,9},{9,8},{10,11... | collective-permute-start | bytes 1572872 | tf_op jit(solution)/shard_map/ppermute | solution.py:126
  137.2 6.9 %collective-permute-start.26 = (bf16[8,128,256]{2,1,0:T(8,128)(2,1)S(1)}, bf16[8,128,256]{2,1,0:T(8,128)(2,1)}, u32[]{:S(2)}, u32[]{:S(2)}) collective-permute-start(bf16[8,128,256]{2,1,0:T(8,128)(2,1)S(1)} %constant_dynamic-update-slice_fusion.5.other_ref), channel_id=1, source_target_pairs={{0,1},{1,0},{2,3},{3,2},{4,5},{5,4},{6,7},{7,6},{8,9},{9,8},{10,11... | collective-permute-start | bytes 1572872 | tf_op jit(solution)/shard_map/ppermute | solution.py:126
  (25 other events, 334.0 us)

commit v2 on v1

--- a/solution.py
+++ b/solution.py
@@ -158,7 +158,7 @@
         grid_spec=pltpu.PrefetchScalarGridSpec(
             num_scalar_prefetch=1,
             grid=(),
-            in_specs=[vmem, pl.BlockSpec(memory_space=pl.ANY)],
+            in_specs=[vmem, pl.BlockSpec(memory_space=pltpu.HBM)],
             out_specs=vmem,
             scratch_shapes=[
                 pltpu.VMEM((4, 2 * HD, features), weight.dtype),
@@ -175,13 +175,13 @@
     )(core.reshape(1), hidden, weight)
 
 
-def grad_kernel(table_ref, own_ref, other_ref, hidden_ref, hidden_other_ref, *rest):
+def grad_kernel(table_ref, *refs):
+    pieces, (hidden_ref, hidden_other_ref), rest = refs[:4], refs[4:6], refs[6:]
     out_ref, total, sems = rest[-3:]
-    groups = own_ref.shape[0] // 4
     copies = []
-    for g in range(groups):
-        left = jnp.concatenate([own_ref[4 * g + i] for i in range(4)], axis=0)
-        right = jnp.concatenate([other_ref[4 * g + i] for i in range(4)], axis=0)
+    for g in range(2):
+        left = jnp.concatenate([pieces[g][i] for i in range(4)], axis=0)
+        right = jnp.concatenate([pieces[2 + g][i] for i in range(4)], axis=0)
         total[g] = jnp.dot(left, hidden_ref[...], preferred_element_type=jnp.float32) + jnp.dot(
             right, hidden_other_ref[...], preferred_element_type=jnp.float32
         )
@@ -197,48 +197,241 @@
 
 
 def grad_rows(table, own, other, hidden, hidden_other, rows, previous=None):
-    heads = own.shape[0]
     tokens, features = hidden.shape
     vmem = pl.BlockSpec(memory_space=pltpu.VMEM)
-    hbm = pl.BlockSpec(memory_space=pl.ANY)
-    args = [table, own, other, hidden, hidden_other] + ([] if previous is None else [previous])
+    hbm = pl.BlockSpec(memory_space=pltpu.HBM)
+    before = [] if previous is None else [previous]
     return pl.pallas_call(
         grad_kernel,
         grid_spec=pltpu.PrefetchScalarGridSpec(
             num_scalar_prefetch=1,
             grid=(),
-            in_specs=[vmem] * 4 + ([] if previous is None else [hbm]),
+            in_specs=[vmem] * 6 + [hbm] * len(before),
             out_specs=hbm,
             scratch_shapes=[
-                pltpu.VMEM((heads // 4, 4 * HD, features), jnp.float32),
-                pltpu.SemaphoreType.DMA((heads,)),
+                pltpu.VMEM((2, 4 * HD, features), jnp.float32),
+                pltpu.SemaphoreType.DMA((8,)),
             ],
         ),
         out_shape=jax.ShapeDtypeStruct((rows, features), jnp.float32),
-        input_output_aliases={} if previous is None else {5: 0},
+        input_output_aliases={7: 0} if before else {},
         compiler_params=pltpu.CompilerParams(vmem_limit_bytes=32 << 20),
         cost_estimate=pl.CostEstimate(
-            flops=4 * heads * HD * tokens * features,
-            bytes_accessed=4 * heads * HD * features,
+            flops=32 * HD * tokens * features,
+            bytes_accessed=32 * HD * features,
             transcendentals=0,
         ),
-    )(*args)
-
-
-def head_train(joined, gain_query, gain_key, block_mask, cot_one, cot_two):
-    first, second = visible_sets(block_mask, joined.shape[0])
-    outputs, pullback = jax.vjp(
-        lambda j: head_steps(j, gain_query, gain_key, first, second), joined
-    )
-    return outputs[0], outputs[1], pullback((cot_one, cot_two))[0]
+    )(table, *own, *other, hidden, hidden_other, *before)
+
+
+def pack_kernel(dp_ref, cot_ref, query_ref, key_ref, mask_ref, first_ref, second_ref):
+    tokens = cot_ref.shape[1]
+    for r, out_ref in enumerate((first_ref, second_ref)):
+        lanes = pl.ds(pl.multiple_of((dp_ref[0] ^ r) * HD, HD), HD)
+        out_ref[:tokens] = cot_ref[0, :, lanes]
+        out_ref[tokens : 2 * tokens] = cot_ref[1, :, lanes]
+        terms = []
+        for gain_ref in (query_ref, key_ref):
+            rest = gain_ref[:, lanes]
+            for _ in range(3):
+                term = rest.astype(jnp.bfloat16).astype(jnp.float32)
+                terms.append(term)
+                rest = rest - term
+        terms.append(jnp.zeros((10, HD), jnp.float32))
+        out_ref[2 * tokens : 2 * tokens + 16] = jnp.concatenate(terms, axis=0).astype(jnp.bfloat16)
+        out_ref[2 * tokens + 16 :] = mask_ref[...].astype(jnp.bfloat16)
+
+
+def pack(dp, cotangent, gain_query, gain_key, block_mask):
+    tokens = cotangent.shape[1]
+    blocks = block_mask.shape[0]
+    mask = jnp.pad(block_mask.astype(jnp.float32), ((0, 16 - blocks), (0, HD - blocks)))
+    vmem = pl.BlockSpec(memory_space=pltpu.VMEM)
+    shape = jax.ShapeDtypeStruct((2 * tokens + 32, HD), jnp.bfloat16)
+    return pl.pallas_call(
+        pack_kernel,
+        grid_spec=pltpu.PrefetchScalarGridSpec(
+            num_scalar_prefetch=1, grid=(), in_specs=[vmem] * 4, out_specs=[vmem] * 2
+        ),
+        out_shape=[shape, shape],
+    )(dp.reshape(1), cotangent, gain_query.reshape(1, -1), gain_key.reshape(1, -1), mask)
+
+
+def core_sum_kernel(y_ref, kept_ref, got_ref, send_ref, keep_ref):
+    y = y_ref[0]
+    keep_ref[...] = kept_ref[y] + got_ref[y].astype(jnp.float32)
+    send_ref[...] = (kept_ref[1 - y] + got_ref[1 - y].astype(jnp.float32)).astype(send_ref.dtype)
+
+
+def core_sum(y, kept, got):
+    vmem = pl.BlockSpec(memory_space=pltpu.VMEM)
+    return pl.pallas_call(
+        core_sum_kernel,
+        grid_spec=pltpu.PrefetchScalarGridSpec(
+            num_scalar_prefetch=1, grid=(), in_specs=[vmem] * 2, out_specs=[vmem] * 2
+        ),
+        out_shape=[
+            jax.ShapeDtypeStruct(kept.shape[1:], jnp.bfloat16),
+            jax.ShapeDtypeStruct(kept.shape[1:], jnp.float32),
+        ],
+    )(y.reshape(1), kept, got)
+
+
+def row_sum_kernel(z_ref, kept_ref, got_ref, keep_ref, *send_refs):
+    z = z_ref[0]
+    keep_ref[...] = kept_ref[z] + got_ref[z].astype(jnp.float32)
+    for bit, send_ref in enumerate(send_refs, 1):
+        other = z ^ bit
+        send_ref[...] = (kept_ref[other] + got_ref[other].astype(jnp.float32)).astype(send_ref.dtype)
+
+
+def row_sum(z, kept, got):
+    vmem = pl.BlockSpec(memory_space=pltpu.VMEM)
+    return pl.pallas_call(
+        row_sum_kernel,
+        grid_spec=pltpu.PrefetchScalarGridSpec(
+            num_scalar_prefetch=1, grid=(), in_specs=[vmem] * 2, out_specs=[vmem] * 4
+        ),
+        out_shape=[jax.ShapeDtypeStruct(kept.shape[1:], jnp.float32)]
+        + [jax.ShapeDtypeStruct(kept.shape[1:], jnp.bfloat16)] * 3,
+    )(z.reshape(1), kept, got)
+
+
+NN = (((1,), (0,)), ((), ()))
+NT = (((1,), (1,)), ((), ()))
+TN = (((0,), (0,)), ((), ()))
+
+
+def dot(left, right, dims):
+    return lax.dot_general(left, right, dims, preferred_element_type=jnp.float32)
+
+
+def halves(values):
+    high = values.astype(jnp.bfloat16)
+    return high, (values - high.astype(jnp.float32)).astype(jnp.bfloat16)
+
+
+def dot_fine(left, right, dims):
+    return (
+        dot(left[0], right[0], dims) + dot(left[0], right[1], dims) + dot(left[1], right[0], dims)
+    )
+
+
+def row_mean(values):
+    return jnp.mean(values, axis=1, keepdims=True)
+
+
+def row_total(values):
+    return jnp.sum(values, axis=1, keepdims=True)
+
+
+def attention_kernel(
+    which_ref, kept_ref, near_ref, mid_ref, far_ref, first_ref, second_ref, out_ref, grad_ref
+):
+    f32, bf16 = jnp.float32, jnp.bfloat16
+    tokens = kept_ref.shape[0]
+    scale = HD ** (-0.5)
+    message = jnp.where(which_ref[0] == 0, first_ref[...], second_ref[...])
+    joined = kept_ref[...] + near_ref[...].astype(f32) + mid_ref[...].astype(f32)
+    joined = (joined + far_ref[...].astype(f32)).astype(bf16)
+    cot_one = message[:tokens]
+    cot_two = message[tokens : 2 * tokens]
+    gains = message[2 * tokens : 2 * tokens + 16].astype(f32)
+    gain_query = gains[0:1] + gains[1:2] + gains[2:3]
+    gain_key = gains[3:4] + gains[4:5] + gains[5:6]
+    mask = message[2 * tokens + 16 :]
+
+    rows = lax.broadcasted_iota(jnp.int32, (tokens, 16), 0) // 64
+    picks = (rows == lax.broadcasted_iota(jnp.int32, (tokens, 16), 1)).astype(f32).astype(bf16)
+    columns = lax.broadcasted_iota(jnp.int32, (HD, tokens), 1) // 64
+    spots = (columns == lax.broadcasted_iota(jnp.int32, (HD, tokens), 0)).astype(f32).astype(bf16)
+    opened = dot(dot(picks, mask, NN).astype(bf16), spots, NN) > 0.5
+    query_at = lax.broadcasted_iota(jnp.int32, (tokens, tokens), 0)
+    key_at = lax.broadcasted_iota(jnp.int32, (tokens, tokens), 1)
+    allowed = (query_at // 64 == key_at // 64) | opened
+    first = allowed & (key_at <= query_at)
+    second = allowed & (key_at < query_at)
+
+    values = joined.astype(f32)
+    inverse = lax.rsqrt(row_mean(values * values) + EPS)
+    normed = values * inverse
+    queries = halves(normed * gain_query)
+    keys = halves(normed * gain_key)
+    scores = jnp.where(first, dot_fine(queries, keys, NT) * scale, -jnp.inf)
+    expo = jnp.exp(scores - jnp.max(scores, axis=1, keepdims=True))
+    soft_one = expo * (1.0 / row_total(expo))
+    weights_one = soft_one.astype(bf16)
+    step_one = dot(weights_one, joined, NN).astype(bf16)
+    out_ref[0] = step_one
+
+    step = step_one.astype(f32)
+    inverse_two = lax.rsqrt(row_mean(step * step) + EPS)
+    renormed = step * inverse_two
+    query_two = renormed * gain_query
+    own_key = renormed * gain_key
+    queries_two = halves(query_two)
+    scores = jnp.where(second, dot_fine(queries_two, keys, NT) * scale, -jnp.inf)
+    own_score = row_total(query_two * own_key) * scale
+    top = jnp.maximum(jnp.max(scores, axis=1, keepdims=True), own_score)
+    expo = jnp.exp(scores - top)
+    own_expo = jnp.exp(own_score - top)
+    share = 1.0 / (row_total(expo) + own_expo)
+    soft_two = expo * share
+    own_soft = own_expo * share
+    weights_two = soft_two.astype(bf16)
+    step_two = dot(weights_two, joined, NN) + own_soft * step
+    out_ref[1] = step_two.astype(bf16)
+
+    d_two = cot_two.astype(f32)
+    d_soft = dot(cot_two, joined, NT).astype(bf16).astype(f32)
+    d_joined = dot(weights_two, cot_two, TN)
+    d_own = row_total(d_two * step)
+    d_step = own_soft * d_two
+    shared = row_total(soft_two * d_soft) + own_soft * d_own
+    d_scores = halves(soft_two * (d_soft - shared) * scale)
+    d_own_score = own_soft * (d_own - shared) * scale
+    d_query = dot_fine(d_scores, keys, NN) + d_own_score * own_key
+    d_keys = dot_fine(d_scores, queries_two, TN)
+    d_renormed = d_query * gain_query + d_own_score * query_two * gain_key
+    d_step = d_step + inverse_two * (d_renormed - renormed * row_mean(d_renormed * renormed))
+    d_one = (d_step.astype(bf16).astype(f32) + cot_one.astype(f32)).astype(bf16)
+    d_soft = dot(d_one, joined, NT).astype(bf16).astype(f32)
+    d_joined = d_joined + dot(weights_one, d_one, TN)
+    d_scores = halves(soft_one * (d_soft - row_total(soft_one * d_soft)) * scale)
+    d_query = dot_fine(d_scores, keys, NN)
+    d_keys = d_keys + dot_fine(d_scores, queries, TN)
+    d_normed = d_query * gain_query + d_keys * gain_key
+    d_joined = d_joined + inverse * (d_normed - normed * row_mean(d_normed * normed))
+    grad_ref[...] = d_joined.T.astype(bf16)
+
+
+def attention(which, kept, pieces, messages):
+    tokens = kept.shape[0]
+    vmem = pl.BlockSpec(memory_space=pltpu.VMEM)
+    return pl.pallas_call(
+        attention_kernel,
+        grid_spec=pltpu.PrefetchScalarGridSpec(
+            num_scalar_prefetch=1, grid=(), in_specs=[vmem] * 6, out_specs=[vmem] * 2
+        ),
+        out_shape=[
+            jax.ShapeDtypeStruct((2, tokens, HD), jnp.bfloat16),
+            jax.ShapeDtypeStruct((HD, tokens), jnp.bfloat16),
+        ],
+        compiler_params=pltpu.CompilerParams(vmem_limit_bytes=24 << 20),
+        cost_estimate=pl.CostEstimate(
+            flops=24 * 2 * tokens * tokens * HD,
+            bytes_accessed=16 * tokens * HD,
+            transcendentals=2 * tokens * tokens,
+        ),
+    )(which.astype(jnp.int32).reshape(1), kept, *pieces, *messages)
 
 
 def keep_weights_plan(hidden, fc_weight, gain_query, gain_key, block_mask, cotangent):
     me_dp = lax.axis_index("dp")
     me_z = lax.axis_index("mp")
-    me_y = lax.axis_index("section") // 2
-    me_c = lax.axis_index("section") % 2
-    upper = me_z // 2
+    me_y = lax.axis_index("section") >> 1
+    me_c = lax.axis_index("section") & 1
+    upper = me_z >> 1
     over_x = swap("dp", 2, 1)
     over_y = swap("section", 4, 2)
     over_c = swap("section", 4, 1)
@@ -253,72 +446,44 @@
         ]
 
     hidden_other = over_x(hidden)
-    tokens = hidden.shape[0]
-    cot_heads = cotangent.reshape(2, tokens, 2, HD)
-    cot_in = []
-    for r in range(2):
-        head = me_dp ^ r
-        sent = lax.dynamic_index_in_dim(cot_heads, head, 2, keepdims=False)
-        cot_in.append(lax.ppermute(sent, ("dp", "mp"), route(r)))
-    gains = jnp.stack([gain_query, gain_key]).reshape(2, 2, HD)
-    gains = lax.ppermute(
-        lax.dynamic_index_in_dim(gains, me_dp, 1, keepdims=False), ("dp", "mp"), route(0)
-    )
-    mask_other = over_x(block_mask)
-    own_first = upper == me_dp
-    cot_own = jnp.where(own_first, cot_in[0], cot_in[1])
-    cot_other = jnp.where(own_first, cot_in[1], cot_in[0])
+    messages = pack(me_dp, cotangent, gain_query, gain_key, block_mask)
+    messages = [lax.ppermute(messages[r], ("dp", "mp"), route(r)) for r in range(2)]
+    own_at = upper ^ me_dp
 
     def scatter_sum(tokens_in):
         sent = half_product(tokens_in, fc_weight, 1 - me_c, jnp.bfloat16)
         kept = half_product(tokens_in, fc_weight, me_c, jnp.float32)
-        got = over_c(sent)
-        sums = kept + got.astype(jnp.float32)
-        got = over_y(take(sums, 1 - me_y).astype(jnp.bfloat16))
-        sums = take(sums, me_y) + got.astype(jnp.float32)
-        pieces = [over_z[b](take(sums, me_z ^ b).astype(jnp.bfloat16)) for b in (1, 2, 3)]
-        total = take(sums, me_z)
-        for piece in pieces:
-            total = total + piece.astype(jnp.float32)
-        return total.astype(jnp.bfloat16)
+        send, kept = core_sum(me_y, kept, over_c(sent))
+        kept, *send = row_sum(me_z, kept, over_y(send))
+        return kept, [over_z[b](send[b - 1]) for b in (1, 2, 3)]
 
     def spread(piece):
         part = jnp.stack([piece] + [over_z[b](piece) for b in (1, 2, 3)])
-        near = jnp.concatenate([part, over_y(part)])
-        return near, over_c(near)
-
-    joined_own = scatter_sum(hidden)
-    joined_other = scatter_sum(hidden_other)
-    one_own, two_own, d_own = head_train(
-        joined_own, gains[0], gains[1], block_mask, cot_own[0], cot_own[1]
-    )
-    near_own, far_own = spread(d_own.T)
-    one_other, two_other, d_other = head_train(
-        joined_other, gains[0], gains[1], mask_other, cot_other[0], cot_other[1]
-    )
-    near_other, far_other = spread(d_other.T)
-
-    def table(core):
-        ys = jnp.arange(2)[:, None]
-        zs = jnp.arange(4)[None, :]
-        z = me_z ^ zs
-        y = me_y ^ ys
-        return (2 * (4 * (z % 2) + 2 * y + core) + z // 2).reshape(8).astype(jnp.int32)
+        rest = over_y(part)
+        return (part, over_c(part)), (rest, over_c(rest))
+
+    out_own, d_own = attention(own_at, *scatter_sum(hidden), messages)
+    out_other, d_other = attention(1 - own_at, *scatter_sum(hidden_other), messages)
+    own_parts = spread(d_own)
+    other_parts = spread(d_other)
 
     rows = fc_weight.shape[0]
-    fc_grad = grad_rows(table(me_c), near_own, near_other, hidden, hidden_other, rows)
-    fc_grad = grad_rows(
-        table(1 - me_c), far_own, far_other, hidden, hidden_other, rows, fc_grad
-    )
-    out_own = jnp.stack([one_own, two_own])
-    out_other = jnp.stack([one_other, two_other])
-    heads_back = []
+    fc_grad = None
+    for flip in range(2):
+        heads = []
+        for core in (me_c, 1 - me_c):
+            z = me_z ^ jnp.arange(4)
+            heads.append(2 * (4 * (z & 1) + 2 * (me_y ^ flip) + core) + (z >> 1))
+        table = jnp.concatenate(heads).astype(jnp.int32)
+        fc_grad = grad_rows(
+            table, own_parts[flip], other_parts[flip], hidden, hidden_other, rows, fc_grad
+        )
+    back = []
     for r in range(2):
-        back = [(b, a) for a, b in route(r)]
-        sent = jnp.where((upper ^ r) == me_dp, out_own, out_other)
-        heads_back.append(lax.ppermute(sent, ("dp", "mp"), back))
-    low = jnp.where(me_dp == 0, heads_back[0], heads_back[1])
-    high = jnp.where(me_dp == 0, heads_back[1], heads_back[0])
+        sent = jnp.where(own_at == r, out_own, out_other)
+        back.append(lax.ppermute(sent, ("dp", "mp"), [(b, a) for a, b in route(r)]))
+    low = jnp.where(me_dp == 0, back[0], back[1])
+    high = jnp.where(me_dp == 0, back[1], back[0])
     ttt_out = jnp.concatenate([low, high], axis=2)
     return (ttt_out, fc_grad)
 

time: 151 us -> 122 us (0.81)
  matrix products: 16.2 us -> 0 us
  other arithmetic: 17 us -> 1.05 us
  Pallas kernels: 24.5 us -> 34.9 us
  local copies, waits for them, and re-layouts: 25.5 us -> 18 us
  waiting for transfers between devices: 26.3 us -> 31.2 us
  starting transfers between devices: 38.7 us -> 35.7 us
    dot_general x26 -> x0, matrix products: 16.2 us -> none  [the longest x6 4.35 us: head_steps(): jnp.dot(queries, keys_ctx.T, precision=lax.Precision.HIGHEST) * scale]
    pallas_call x0 -> x7, Pallas kernels: none -> 15.4 us  [the longest x2 5.3 us: attention(): pl.pallas_call(attention_kernel, grid_spec=pltpu.PrefetchScalarGridSpec(n...]
    ppermute x5 -> x4, waiting for transfers between devices: 0.01 us -> 5.9 us  [the longest x2 5.89 us: keep_weights_plan(): back.append(lax.ppermute(sent, ('dp', 'mp'), [(b, a) for a, b in route(r)]))]
    ppermute x22 -> x23, starting transfers between devices: 32.9 us -> 27.1 us  [swap(): lax.ppermute(array, axis, [(i, i ^ bit) for i in range(size)])]
    reduce_sum x12 -> x0, other arithmetic: 5.42 us -> none  [the longest x2 2.27 us: head_steps(): jnp.sum(expo_one, axis=-1, keepdims=True)]
    pallas_call x4 -> x0, local copies, waits for them, and re-layouts: 4.62 us -> none  [half_product(): pl.pallas_call(half_product_kernel, grid_spec=pltpu.PrefetchScalarGridSpe...]
    unnamed x2 -> x0, Pallas kernels: 4.07 us -> none
    add x5 -> x4, other arithmetic: 3.68 us -> 0.04 us  [keep_weights_plan(): heads.append(2 * (4 * (z & 1) + 2 * (me_y ^ flip) + core) + (z >> 1))]
  transfers between devices with their start and end apart: 27 -> 27, of which waited for: 7 -> 6; matrix products, arithmetic and copies ran while one was open for 16% -> 1% of each run, Pallas kernels for 11% -> 25%
where the time goes in v2:
time: 122 us
  starting transfers between devices  35.7 us (29%)
  Pallas kernels  34.9 us (29%)
  waiting for transfers between devices  31.2 us (26%)
  local copies, waits for them, and re-layouts  18 us (15%)
    ppermute x23, starting transfers between devices, swap(): lax.ppermute(array, axis, [(i, i ^ bit) for i in range(size)])  27.1 us
    ppermute x23, waiting for transfers between devices, swap(): lax.ppermute(array, axis, [(i, i ^ bit) for i in range(size)])  25.3 us
    unnamed x28, local copies, waits for them, and re-layouts  17.4 us
    pallas_call x4, Pallas kernels, half_product(): pl.pallas_call(half_product_kernel, grid_spec=pltpu.PrefetchScalarGridSpe...  10.4 us
    pallas_call x2, Pallas kernels, grad_rows(): pl.pallas_call(grad_kernel, grid_spec=pltpu.PrefetchScalarGridSpec(num_sc...  9.11 us
    ppermute x2, starting transfers between devices, keep_weights_plan(): lax.ppermute(messages[r], ('dp', 'mp'), route(r))  6.06 us
    ppermute x2, waiting for transfers between devices, keep_weights_plan(): back.append(lax.ppermute(sent, ('dp', 'mp'), [(b, a) for a, b in route(r)]))  5.89 us
    pallas_call x2, Pallas kernels, attention(): pl.pallas_call(attention_kernel, grid_spec=pltpu.PrefetchScalarGridSpec(n...  5.3 us
  transfers between devices with their start and end apart: 27, of which 6 were waited for; matrix products, arithmetic and copies ran while one was open for 1% of the time, Pallas kernels for 25%

profile of v2, /device:TPU:0, one launch (start us, length us, event | category | flops | bytes accessed | tf_op | source)
XLA Modules:
  0.0 121.9 jit_solution(8878849785693734522)
XLA Ops:
  0.6 3.0 %collective-permute-start.7 = (bf16[256,1536]{1,0:T(8,128)(2,1)}, bf16[256,1536]{1,0:T(8,128)(2,1)S(1)}, u32[]{:S(2)}, u32[]{:S(2)}) collective-permute-start(bf16[256,1536]{1,0:T(8,128)(2,1)} %refs_4_.3), channel_id=1, source_target_pairs={{0,16},{16,0},{1,17},{17,1},{2,18},{18,2},{3,19},{19,3},{4,20},{20... | collective-permute-start | bytes 2359304 | tf_op jit(solution)/shard_map/ppermute | solution.py:126
  3.6 2.8 %copy-done = bf16[2048,1536]{1,0:T(8,128)(2,1)S(1)} copy-done((bf16[2048,1536]{1,0:T(8,128)(2,1)S(1)}, bf16[2048,1536]{1,0:T(8,128)(2,1)}, u32[]{:S(2)}) %copy-start) | copy-done | bytes 6291480
  7.6 2.6 %shard_map.78 = bf16[2,4,256,128]{3,2,1,0:T(8,128)(2,1)S(1)} custom-call(s32[1]{0:T(128)} %bitcast.4.core_ref, bf16[256,1536]{1,0:T(8,128)(2,1)S(1)} %copy-done.4, bf16[2048,1536]{1,0:T(8,128)(2,1)S(1)} %copy-done), custom_call_target="tpu_custom_call" | custom-call | flops 805306368 | bytes 3932160 | tf_op jit(solution)/shard_map/pallas_call | solution.py:156
  10.3 11.1 %collective-permute-done.7.hidden_ref.refs_5_ = bf16[256,1536]{1,0:T(8,128)(2,1)S(1)} collective-permute-done((bf16[256,1536]{1,0:T(8,128)(2,1)}, bf16[256,1536]{1,0:T(8,128)(2,1)S(1)}, u32[]{:S(2)}, u32[]{:S(2)}) %collective-permute-start.7) | collective-permute-done | bytes 786464 | tf_op jit(solution)/shard_map/ppermute | solution.py:126
  21.4 2.8 %copy-done.1 = bf16[2048,1536]{1,0:T(8,128)(2,1)S(1)} copy-done((bf16[2048,1536]{1,0:T(8,128)(2,1)S(1)}, bf16[2048,1536]{1,0:T(8,128)(2,1)}, u32[]{:S(2)}) %copy-start.1) | copy-done | bytes 6291480
  24.2 2.6 %shard_map.84 = bf16[2,4,256,128]{3,2,1,0:T(8,128)(2,1)S(1)} custom-call(s32[1]{0:T(128)} %bitcast.4.core_ref, bf16[256,1536]{1,0:T(8,128)(2,1)S(1)} %collective-permute-done.7.hidden_ref.refs_5_, bf16[2048,1536]{1,0:T(8,128)(2,1)S(1)} %copy-done.1), custom_call_target="tpu_custom_call" | custom-call | flops 805306368 | bytes 3932160 | tf_op jit(solution)/shard_map/pallas_call | solution.py:156
  30.8 4.5 %collective-permute-start.6 = (bf16[544,128]{1,0:T(8,128)(2,1)}, bf16[544,128]{1,0:T(8,128)(2,1)S(1)}, u32[]{:S(2)}, u32[]{:S(2)}) collective-permute-start(bf16[544,128]{1,0:T(8,128)(2,1)} %get-tuple-element.27), channel_id=1, source_target_pairs={{0,8},{4,12},{8,24},{12,28},{16,0},{20,4},{24,16},{28,20},{1,9},{5... | collective-permute-start | bytes 417800 | tf_op jit(solution)/shard_map/ppermute | solution.py:450
  35.3 2.8 %copy-done.2 = bf16[2048,1536]{1,0:T(8,128)(2,1)S(1)} copy-done((bf16[2048,1536]{1,0:T(8,128)(2,1)S(1)}, bf16[2048,1536]{1,0:T(8,128)(2,1)}, u32[]{:S(2)}) %copy-start.2) | copy-done | bytes 6291480
  38.1 2.6 %shard_map.77.kept_ref = f32[2,4,256,128]{3,2,1,0:T(8,128)S(1)} custom-call(s32[1]{0:T(128)} %bitcast.3.core_ref, bf16[256,1536]{1,0:T(8,128)(2,1)S(1)} %copy-done.5, bf16[2048,1536]{1,0:T(8,128)(2,1)S(1)} %copy-done.2), custom_call_target="tpu_custom_call" | custom-call | flops 805306368 | bytes 3932160 | tf_op jit(solution)/shard_map/pallas_call | solution.py:156
  41.7 2.3 %shard_map.79 = (bf16[4,256,128]{2,1,0:T(8,128)(2,1)}, f32[4,256,128]{2,1,0:T(8,128)}) custom-call(s32[1]{0:T(128)} %bitcast.2.y_ref, f32[2,4,256,128]{3,2,1,0:T(8,128)} %copy-done.7, bf16[2,4,256,128]{3,2,1,0:T(8,128)(2,1)} %collective-permute-done.got_ref), custom_call_target="tpu_custom_call" | custom-call | tf_op jit(solution)/shard_map/pallas_call | solution.py:268
  45.5 6.8 %collective-permute-done.1.got_ref = bf16[4,256,128]{2,1,0:T(8,128)(2,1)S(1)} collective-permute-done((bf16[4,256,128]{2,1,0:T(8,128)(2,1)}, bf16[4,256,128]{2,1,0:T(8,128)(2,1)S(1)}, u32[]{:S(2)}, u32[]{:S(2)}) %collective-permute-start.1) | collective-permute-done | bytes 262176 | tf_op jit(solution)/shard_map/ppermute | solution.py:126
  56.8 2.8 %copy-done.3 = bf16[2048,1536]{1,0:T(8,128)(2,1)S(1)} copy-done((bf16[2048,1536]{1,0:T(8,128)(2,1)S(1)}, bf16[2048,1536]{1,0:T(8,128)(2,1)}, u32[]{:S(2)}) %copy-start.3) | copy-done | bytes 6291480
  59.5 2.6 %shard_map.83.kept_ref = f32[2,4,256,128]{3,2,1,0:T(8,128)S(1)} custom-call(s32[1]{0:T(128)} %bitcast.3.core_ref, bf16[256,1536]{1,0:T(8,128)(2,1)S(1)} %collective-permute-done.7.hidden_ref.refs_5_, bf16[2048,1536]{1,0:T(8,128)(2,1)S(1)} %copy-done.3), custom_call_target="tpu_custom_call" | custom-call | flops 805306368 | bytes 3932160 | tf_op jit(solution)/shard_map/pallas_call | solution.py:156
  63.1 2.5 %collective-permute-start.4 = (bf16[256,128]{1,0:T(8,128)(2,1)}, bf16[256,128]{1,0:T(8,128)(2,1)S(1)}, u32[]{:S(2)}, u32[]{:S(2)}) collective-permute-start(bf16[256,128]{1,0:T(8,128)(2,1)} %get-tuple-element.25), channel_id=1, source_target_pairs={{0,12},{4,8},{8,4},{12,0},{1,13},{5,9},{9,5},{13,1},{2,14},{6,10},... | collective-permute-start | bytes 196616 | tf_op jit(solution)/shard_map/ppermute | solution.py:126
  70.4 2.6 %shard_map.82 = (bf16[2,256,128]{2,1,0:T(8,128)(2,1)S(1)}, bf16[128,256]{1,0:T(8,128)(2,1)S(1)}) custom-call(s32[1]{0:T(128)} %bitcast.which_ref, f32[256,128]{1,0:T(8,128)S(1)} %copy-done.8, bf16[256,128]{1,0:T(8,128)(2,1)S(1)} %collective-permute-done.2.near_ref, bf16[256,128]{1,0:T(8,128)(2,1)S(1)} %collective-permute-done.3.mid_ref, ...), custom_call_target="tpu_custom_call" | custom-call | flops 402653184 | bytes 524288 | tf_op jit(solution)/shard_map/pallas_call | solution.py:411
  73.1 2.5 %collective-permute-start.17 = (bf16[128,256]{1,0:T(8,128)(2,1)S(1)}, bf16[128,256]{1,0:T(8,128)(2,1)S(1)}, u32[]{:S(2)}, u32[]{:S(2)}) collective-permute-start(bf16[128,256]{1,0:T(8,128)(2,1)S(1)} %get-tuple-element.36), channel_id=1, source_target_pairs={{0,12},{4,8},{8,4},{12,0},{1,13},{5,9},{9,5},{13,1},{2,14},{6,10},... | collective-permute-start | bytes 196616 | tf_op jit(solution)/shard_map/ppermute | solution.py:126
  80.2 2.9 %collective-permute-start.11 = (bf16[256,128]{1,0:T(8,128)(2,1)}, bf16[256,128]{1,0:T(8,128)(2,1)S(1)}, u32[]{:S(2)}, u32[]{:S(2)}) collective-permute-start(bf16[256,128]{1,0:T(8,128)(2,1)} %get-tuple-element.33), channel_id=1, source_target_pairs={{0,8},{4,12},{8,0},{12,4},{1,9},{5,13},{9,1},{13,5},{2,10},{6,14},... | collective-permute-start | bytes 196616 | tf_op jit(solution)/shard_map/ppermute | solution.py:126
  86.1 3.3 %collective-permute-done.12.far_ref = bf16[256,128]{1,0:T(8,128)(2,1)S(1)} collective-permute-done((bf16[256,128]{1,0:T(8,128)(2,1)}, bf16[256,128]{1,0:T(8,128)(2,1)S(1)}, u32[]{:S(2)}, u32[]{:S(2)}) %collective-permute-start.12) | collective-permute-done | bytes 65568 | tf_op jit(solution)/shard_map/ppermute | solution.py:126
  90.3 2.6 %shard_map.87 = (bf16[2,256,128]{2,1,0:T(8,128)(2,1)S(1)}, bf16[128,256]{1,0:T(8,128)(2,1)S(1)}) custom-call(s32[1]{0:T(128)} %bitcast.8.which_ref, f32[256,128]{1,0:T(8,128)S(1)} %copy-done.9, bf16[256,128]{1,0:T(8,128)(2,1)S(1)} %collective-permute-done.10.near_ref, bf16[256,128]{1,0:T(8,128)(2,1)S(1)} %collective-permute-done.11.mid_ref, ...), custom_call_target="tpu_custom_call" | custom-call | flops 402653184 | bytes 524288 | tf_op jit(solution)/shard_map/pallas_call | solution.py:411
  94.4 3.0 %collective-permute-start.20 = (bf16[128,256]{1,0:T(8,128)(2,1)S(1)}, bf16[128,256]{1,0:T(8,128)(2,1)S(1)}, u32[]{:S(2)}, u32[]{:S(2)}) collective-permute-start(bf16[128,256]{1,0:T(8,128)(2,1)S(1)} %get-tuple-element.37), channel_id=1, source_target_pairs={{0,4},{4,0},{8,12},{12,8},{1,5},{5,1},{9,13},{13,9},{2,6},{6,2},{1... | collective-permute-start | bytes 196616 | tf_op jit(solution)/shard_map/ppermute | solution.py:126
  101.3 2.7 %collective-permute-done.21 = bf16[128,256]{1,0:T(8,128)(2,1)S(1)} collective-permute-done((bf16[128,256]{1,0:T(8,128)(2,1)S(1)}, bf16[128,256]{1,0:T(8,128)(2,1)S(1)}, u32[]{:S(2)}, u32[]{:S(2)}) %collective-permute-start.21) | collective-permute-done | bytes 65568 | tf_op jit(solution)/shard_map/ppermute | solution.py:126
  105.9 5.9 %collective-permute-done.14 = bf16[2,256,128]{2,1,0:T(8,128)(2,1)S(1)} collective-permute-done((bf16[2,256,128]{2,1,0:T(8,128)(2,1)S(1)}, bf16[2,256,128]{2,1,0:T(8,128)(2,1)S(1)}, u32[]{:S(2)}, u32[]{:S(2)}) %collective-permute-start.14) | collective-permute-done | bytes 131104 | tf_op jit(solution)/shard_map/ppermute | solution.py:484
  112.6 4.6 %shard_map.88.refs_6_ = f32[2048,1536]{1,0:T(8,128)} custom-call(s32[8]{0:T(128)S(1)} %pad_add_fusion.1.table_ref, bf16[4,128,256]{2,1,0:T(8,128)(2,1)S(1)} %pad_maximum_fusion.1.refs_0_, bf16[4,128,256]{2,1,0:T(8,128)(2,1)S(1)} %collective-permute-done.25.refs_1_, bf16[4,128,256]{2,1,0:T(8,128)(2,1)S(1)} %pad_maximum_fusion.2.refs_2_, ...), custom_call_target="tpu_custom_call" | custom-call | flops 1610612736 | bytes 6291456 | tf_op jit(solution)/shard_map/pallas_call | solution.py:204
  117.2 4.6 %shard_map.89 = f32[2048,1536]{1,0:T(8,128)} custom-call(s32[8]{0:T(128)S(1)} %pad_add_fusion.table_ref, bf16[4,128,256]{2,1,0:T(8,128)(2,1)S(1)} %collective-permute-done.18.refs_0_, bf16[4,128,256]{2,1,0:T(8,128)(2,1)S(1)} %collective-permute-done.19.refs_1_, ...), custom_call_target="tpu_custom_call", output_to_operand_aliasing={{}: (7, {})} | custom-call | flops 1610612736 | bytes 6291456 | tf_op jit(solution)/shard_map/pallas_call | solution.py:204
  (84 shorter events, 34.4 us)
Async XLA Ops:
  0.6 20.8 %collective-permute-start.7 = (bf16[256,1536]{1,0:T(8,128)(2,1)}, bf16[256,1536]{1,0:T(8,128)(2,1)S(1)}, u32[]{:S(2)}, u32[]{:S(2)}) collective-permute-start(bf16[256,1536]{1,0:T(8,128)(2,1)} %refs_4_.3), channel_id=1, source_target_pairs={{0,16},{16,0},{1,17},{17,1},{2,18},{18,2},{3,19},{19,3},{4,20},{20... | collective-permute-start | bytes 2359304 | tf_op jit(solution)/shard_map/ppermute | solution.py:126
  10.2 31.5 %collective-permute-start = (bf16[2,4,256,128]{3,2,1,0:T(8,128)(2,1)S(1)}, bf16[2,4,256,128]{3,2,1,0:T(8,128)(2,1)}, u32[]{:S(2)}, u32[]{:S(2)}) collective-permute-start(bf16[2,4,256,128]{3,2,1,0:T(8,128)(2,1)S(1)} %shard_map.78), channel_id=1, source_target_pairs={{0,1},{1,0},{2,3},{3,2},{4,5},{5,4},{6,7},{7,6},{8,9},{9,8},{10,11... | collective-permute-start | bytes 1572872 | tf_op jit(solution)/shard_map/ppermute | solution.py:126
  26.8 36.3 %collective-permute-start.8 = (bf16[2,4,256,128]{3,2,1,0:T(8,128)(2,1)S(1)}, bf16[2,4,256,128]{3,2,1,0:T(8,128)(2,1)S(1)}, u32[]{:S(2)}, u32[]{:S(2)}) collective-permute-start(bf16[2,4,256,128]{3,2,1,0:T(8,128)(2,1)S(1)} %shard_map.84), channel_id=1, source_target_pairs={{0,1},{1,0},{2,3},{3,2},{4,5},{5,4},{6,7},{7,6},{8,9},{9,8},{10,11... | collective-permute-start | bytes 1572872 | tf_op jit(solution)/shard_map/ppermute | solution.py:126
  29.2 38.7 %collective-permute-start.5 = (bf16[544,128]{1,0:T(8,128)(2,1)}, bf16[544,128]{1,0:T(8,128)(2,1)S(1)}, u32[]{:S(2)}, u32[]{:S(2)}) collective-permute-start(bf16[544,128]{1,0:T(8,128)(2,1)} %get-tuple-element.26), channel_id=1, source_target_pairs={{0,0},{4,4},{8,16},{12,20},{16,8},{20,12},{24,24},{28,28},{1,1},{5... | collective-permute-start | bytes 417800 | tf_op jit(solution)/shard_map/ppermute | solution.py:450
  30.8 38.7 %collective-permute-start.6 = (bf16[544,128]{1,0:T(8,128)(2,1)}, bf16[544,128]{1,0:T(8,128)(2,1)S(1)}, u32[]{:S(2)}, u32[]{:S(2)}) collective-permute-start(bf16[544,128]{1,0:T(8,128)(2,1)} %get-tuple-element.27), channel_id=1, source_target_pairs={{0,8},{4,12},{8,24},{12,28},{16,0},{20,4},{24,16},{28,20},{1,9},{5... | collective-permute-start | bytes 417800 | tf_op jit(solution)/shard_map/ppermute | solution.py:450
  44.0 8.3 %collective-permute-start.1 = (bf16[4,256,128]{2,1,0:T(8,128)(2,1)}, bf16[4,256,128]{2,1,0:T(8,128)(2,1)S(1)}, u32[]{:S(2)}, u32[]{:S(2)}) collective-permute-start(bf16[4,256,128]{2,1,0:T(8,128)(2,1)} %get-tuple-element.21), channel_id=1, source_target_pairs={{0,2},{1,3},{2,0},{3,1},{4,6},{5,7},{6,4},{7,5},{8,10},{9,11},{10,... | collective-permute-start | bytes 786440 | tf_op jit(solution)/shard_map/ppermute | solution.py:126
  54.9 14.6 %collective-permute-start.2 = (bf16[256,128]{1,0:T(8,128)(2,1)}, bf16[256,128]{1,0:T(8,128)(2,1)S(1)}, u32[]{:S(2)}, u32[]{:S(2)}) collective-permute-start(bf16[256,128]{1,0:T(8,128)(2,1)} %get-tuple-element.23), channel_id=1, source_target_pairs={{0,4},{4,0},{8,12},{12,8},{1,5},{5,1},{9,13},{13,9},{2,6},{6,2},{1... | collective-permute-start | bytes 196616 | tf_op jit(solution)/shard_map/ppermute | solution.py:126
  56.5 13.0 %collective-permute-start.3 = (bf16[256,128]{1,0:T(8,128)(2,1)}, bf16[256,128]{1,0:T(8,128)(2,1)S(1)}, u32[]{:S(2)}, u32[]{:S(2)}) collective-permute-start(bf16[256,128]{1,0:T(8,128)(2,1)} %get-tuple-element.24), channel_id=1, source_target_pairs={{0,8},{4,12},{8,0},{12,4},{1,9},{5,13},{9,1},{13,5},{2,10},{6,14},... | collective-permute-start | bytes 196616 | tf_op jit(solution)/shard_map/ppermute | solution.py:126
  63.1 6.4 %collective-permute-start.4 = (bf16[256,128]{1,0:T(8,128)(2,1)}, bf16[256,128]{1,0:T(8,128)(2,1)S(1)}, u32[]{:S(2)}, u32[]{:S(2)}) collective-permute-start(bf16[256,128]{1,0:T(8,128)(2,1)} %get-tuple-element.25), channel_id=1, source_target_pairs={{0,12},{4,8},{8,4},{12,0},{1,13},{5,9},{9,5},{13,1},{2,14},{6,10},... | collective-permute-start | bytes 196616 | tf_op jit(solution)/shard_map/ppermute | solution.py:126
  68.0 9.7 %collective-permute-start.9 = (bf16[4,256,128]{2,1,0:T(8,128)(2,1)}, bf16[4,256,128]{2,1,0:T(8,128)(2,1)S(1)}, u32[]{:S(2)}, u32[]{:S(2)}) collective-permute-start(bf16[4,256,128]{2,1,0:T(8,128)(2,1)} %get-tuple-element.30), channel_id=1, source_target_pairs={{0,2},{1,3},{2,0},{3,1},{4,6},{5,7},{6,4},{7,5},{8,10},{9,11},{10,... | collective-permute-start | bytes 786440 | tf_op jit(solution)/shard_map/ppermute | solution.py:126
  73.1 10.1 %collective-permute-start.17 = (bf16[128,256]{1,0:T(8,128)(2,1)S(1)}, bf16[128,256]{1,0:T(8,128)(2,1)S(1)}, u32[]{:S(2)}, u32[]{:S(2)}) collective-permute-start(bf16[128,256]{1,0:T(8,128)(2,1)S(1)} %get-tuple-element.36), channel_id=1, source_target_pairs={{0,12},{4,8},{8,4},{12,0},{1,13},{5,9},{9,5},{13,1},{2,14},{6,10},... | collective-permute-start | bytes 196616 | tf_op jit(solution)/shard_map/ppermute | solution.py:126
  75.5 9.0 %collective-permute-start.16 = (bf16[128,256]{1,0:T(8,128)(2,1)S(1)}, bf16[128,256]{1,0:T(8,128)(2,1)S(1)}, u32[]{:S(2)}, u32[]{:S(2)}) collective-permute-start(bf16[128,256]{1,0:T(8,128)(2,1)S(1)} %get-tuple-element.36), channel_id=1, source_target_pairs={{0,8},{4,12},{8,0},{12,4},{1,9},{5,13},{9,1},{13,5},{2,10},{6,14},... | collective-permute-start | bytes 196616 | tf_op jit(solution)/shard_map/ppermute | solution.py:126
  75.5 9.0 %collective-permute-start.15 = (bf16[128,256]{1,0:T(8,128)(2,1)S(1)}, bf16[128,256]{1,0:T(8,128)(2,1)S(1)}, u32[]{:S(2)}, u32[]{:S(2)}) collective-permute-start(bf16[128,256]{1,0:T(8,128)(2,1)S(1)} %get-tuple-element.36), channel_id=1, source_target_pairs={{0,4},{4,0},{8,12},{12,8},{1,5},{5,1},{9,13},{13,9},{2,6},{6,2},{1... | collective-permute-start | bytes 196616 | tf_op jit(solution)/shard_map/ppermute | solution.py:126
  83.1 6.3 %collective-permute-start.12 = (bf16[256,128]{1,0:T(8,128)(2,1)}, bf16[256,128]{1,0:T(8,128)(2,1)S(1)}, u32[]{:S(2)}, u32[]{:S(2)}) collective-permute-start(bf16[256,128]{1,0:T(8,128)(2,1)} %get-tuple-element.34), channel_id=1, source_target_pairs={{0,12},{4,8},{8,4},{12,0},{1,13},{5,9},{9,5},{13,1},{2,14},{6,10},... | collective-permute-start | bytes 196616 | tf_op jit(solution)/shard_map/ppermute | solution.py:126
  84.6 20.7 %collective-permute-start.18 = (bf16[4,128,256]{2,1,0:T(8,128)(2,1)S(1)}, bf16[4,128,256]{2,1,0:T(8,128)(2,1)S(1)}, u32[]{:S(2)}, u32[]{:S(2)}) collective-permute-start(bf16[4,128,256]{2,1,0:T(8,128)(2,1)S(1)} %pad_maximum_fusion.1.refs_0_), channel_id=1, source_target_pairs={{0,2},{1,3},{2,0},{3,1},{4,6},{5,7},{6,4},{7,5},{8,10},{9,11},{10,... | collective-permute-start | bytes 786440 | tf_op jit(solution)/shard_map/ppermute | solution.py:126
  93.0 6.5 %collective-permute-start.22 = (bf16[128,256]{1,0:T(8,128)(2,1)S(1)}, bf16[128,256]{1,0:T(8,128)(2,1)S(1)}, u32[]{:S(2)}, u32[]{:S(2)}) collective-permute-start(bf16[128,256]{1,0:T(8,128)(2,1)S(1)} %get-tuple-element.37), channel_id=1, source_target_pairs={{0,12},{4,8},{8,4},{12,0},{1,13},{5,9},{9,5},{13,1},{2,14},{6,10},... | collective-permute-start | bytes 196616 | tf_op jit(solution)/shard_map/ppermute | solution.py:126
  94.4 9.6 %collective-permute-start.21 = (bf16[128,256]{1,0:T(8,128)(2,1)S(1)}, bf16[128,256]{1,0:T(8,128)(2,1)S(1)}, u32[]{:S(2)}, u32[]{:S(2)}) collective-permute-start(bf16[128,256]{1,0:T(8,128)(2,1)S(1)} %get-tuple-element.37), channel_id=1, source_target_pairs={{0,8},{4,12},{8,0},{12,4},{1,9},{5,13},{9,1},{13,5},{2,10},{6,14},... | collective-permute-start | bytes 196616 | tf_op jit(solution)/shard_map/ppermute | solution.py:126
  94.4 9.6 %collective-permute-start.20 = (bf16[128,256]{1,0:T(8,128)(2,1)S(1)}, bf16[128,256]{1,0:T(8,128)(2,1)S(1)}, u32[]{:S(2)}, u32[]{:S(2)}) collective-permute-start(bf16[128,256]{1,0:T(8,128)(2,1)S(1)} %get-tuple-element.37), channel_id=1, source_target_pairs={{0,4},{4,0},{8,12},{12,8},{1,5},{5,1},{9,13},{13,9},{2,6},{6,2},{1... | collective-permute-start | bytes 196616 | tf_op jit(solution)/shard_map/ppermute | solution.py:126
  97.5 8.3 %collective-permute-start.13 = (bf16[2,256,128]{2,1,0:T(8,128)(2,1)S(1)}, bf16[2,256,128]{2,1,0:T(8,128)(2,1)S(1)}, u32[]{:S(2)}, u32[]{:S(2)}) collective-permute-start(bf16[2,256,128]{2,1,0:T(8,128)(2,1)S(1)} %get-tuple-element.40), channel_id=1, source_target_pairs={{0,0},{4,4},{16,8},{20,12},{8,16},{12,20},{24,24},{28,28},{1,1},{5... | collective-permute-start | bytes 393224 | tf_op jit(solution)/shard_map/ppermute | solution.py:484
  99.5 12.3 %collective-permute-start.14 = (bf16[2,256,128]{2,1,0:T(8,128)(2,1)S(1)}, bf16[2,256,128]{2,1,0:T(8,128)(2,1)S(1)}, u32[]{:S(2)}, u32[]{:S(2)}) collective-permute-start(bf16[2,256,128]{2,1,0:T(8,128)(2,1)S(1)} %get-tuple-element.41), channel_id=1, source_target_pairs={{8,0},{12,4},{24,8},{28,12},{0,16},{4,20},{16,24},{20,28},{9,1},{1... | collective-permute-start | bytes 393224 | tf_op jit(solution)/shard_map/ppermute | solution.py:484
  104.1 7.7 %collective-permute-start.23 = (bf16[4,128,256]{2,1,0:T(8,128)(2,1)S(1)}, bf16[4,128,256]{2,1,0:T(8,128)(2,1)S(1)}, u32[]{:S(2)}, u32[]{:S(2)}) collective-permute-start(bf16[4,128,256]{2,1,0:T(8,128)(2,1)S(1)} %pad_maximum_fusion.2.refs_2_), channel_id=1, source_target_pairs={{0,2},{1,3},{2,0},{3,1},{4,6},{5,7},{6,4},{7,5},{8,10},{9,11},{10,... | collective-permute-start | bytes 786440 | tf_op jit(solution)/shard_map/ppermute | solution.py:126
  105.3 7.3 %collective-permute-start.25 = (bf16[4,128,256]{2,1,0:T(8,128)(2,1)S(1)}, bf16[4,128,256]{2,1,0:T(8,128)(2,1)S(1)}, u32[]{:S(2)}, u32[]{:S(2)}) collective-permute-start(bf16[4,128,256]{2,1,0:T(8,128)(2,1)S(1)} %pad_maximum_fusion.1.refs_0_), channel_id=1, source_target_pairs={{0,1},{1,0},{2,3},{3,2},{4,5},{5,4},{6,7},{7,6},{8,9},{9,8},{10,11... | collective-permute-start | bytes 786440 | tf_op jit(solution)/shard_map/ppermute | solution.py:126
  105.3 11.9 %collective-permute-start.19 = (bf16[4,128,256]{2,1,0:T(8,128)(2,1)S(1)}, bf16[4,128,256]{2,1,0:T(8,128)(2,1)S(1)}, u32[]{:S(2)}, u32[]{:S(2)}) collective-permute-start(bf16[4,128,256]{2,1,0:T(8,128)(2,1)S(1)} %collective-permute-done.18.refs_0_), channel_id=1, source_target_pairs={{0,1},{1,0},{2,3},{3,2},{4,5},{5,4},{6,7},{7,6},{8,9},{9,8},{10,11... | collective-permute-start | bytes 786440 | tf_op jit(solution)/shard_map/ppermute | solution.py:126
  105.8 6.8 %collective-permute-start.26 = (bf16[4,128,256]{2,1,0:T(8,128)(2,1)S(1)}, bf16[4,128,256]{2,1,0:T(8,128)(2,1)S(1)}, u32[]{:S(2)}, u32[]{:S(2)}) collective-permute-start(bf16[4,128,256]{2,1,0:T(8,128)(2,1)S(1)} %pad_maximum_fusion.2.refs_2_), channel_id=1, source_target_pairs={{0,1},{1,0},{2,3},{3,2},{4,5},{5,4},{6,7},{7,6},{8,9},{9,8},{10,11... | collective-permute-start | bytes 786440 | tf_op jit(solution)/shard_map/ppermute | solution.py:126
  (17 other events, 91.1 us)

commit v3 on v2

--- a/solution.py
+++ b/solution.py
@@ -118,116 +118,218 @@
     return (ttt_out, fc_grad)
 
 
-def take(array, index):
-    return lax.dynamic_index_in_dim(array, index, 0, keepdims=False)
+def after(array, *others):
+    return lax.optimization_barrier((array, *others))[0]
 
 
 def swap(axis, size, bit):
     return lambda array: lax.ppermute(array, axis, [(i, i ^ bit) for i in range(size)])
 
 
-def half_product_kernel(core_ref, hidden_ref, weight_ref, out_ref, rows, sems):
-    core = core_ref[0]
-    copies = []
+def tile_product(hidden, weight_rows, out_ref, y, z0):
+    product = lax.dot_general(
+        hidden, weight_rows, (((1,), (1,)), ((), ())), preferred_element_type=jnp.float32
+    )
+    out_ref[y, z0] = product[:, :HD].astype(out_ref.dtype)
+    out_ref[y, 2 + z0] = product[:, HD:].astype(out_ref.dtype)
+
+
+def streamed_product_kernel(core_ref, hidden_ref, weight_ref, out_ref, held, rows, sems):
+    loads = [pltpu.make_async_copy(hidden_ref, held, sems.at[4])]
     for y in range(2):
         for z0 in range(2):
-            block = 4 * z0 + 2 * y + core
-            copy = pltpu.make_async_copy(
-                weight_ref.at[pl.ds(block * 2 * HD, 2 * HD)], rows.at[2 * y + z0], sems.at[2 * y + z0]
+            row = pl.multiple_of((4 * z0 + 2 * y + core_ref[0]) * 2 * HD, 2 * HD)
+            slot = 2 * y + z0
+            loads.append(
+                pltpu.make_async_copy(
+                    weight_ref.at[pl.ds(row, 2 * HD)], rows.at[slot], sems.at[slot]
+                )
             )
-            copy.start()
-            copies.append(copy)
+    for load in loads:
+        load.start()
+    for load in loads:
+        load.wait()
     for y in range(2):
         for z0 in range(2):
-            copies[2 * y + z0].wait()
-            product = lax.dot_general(
-                hidden_ref[...],
-                rows[2 * y + z0],
-                (((1,), (1,)), ((), ())),
-                preferred_element_type=jnp.float32,
-            )
-            out_ref[y, z0] = product[:, :HD].astype(out_ref.dtype)
-            out_ref[y, 2 + z0] = product[:, HD:].astype(out_ref.dtype)
-
-
-def half_product(hidden, weight, core, dtype):
+            tile_product(held[...], rows[2 * y + z0], out_ref, y, z0)
+
+
+def streamed_product(hidden, weight, core, dtype):
     tokens, features = hidden.shape
     vmem = pl.BlockSpec(memory_space=pltpu.VMEM)
-    return pl.pallas_call(
-        half_product_kernel,
+    hbm = pl.BlockSpec(memory_space=pltpu.HBM)
+    return pl.pallas_call(
+        streamed_product_kernel,
+        name="streamed_product",
         grid_spec=pltpu.PrefetchScalarGridSpec(
             num_scalar_prefetch=1,
             grid=(),
-            in_specs=[vmem, pl.BlockSpec(memory_space=pltpu.HBM)],
+            in_specs=[hbm, hbm],
             out_specs=vmem,
             scratch_shapes=[
+                pltpu.VMEM((tokens, features), hidden.dtype),
                 pltpu.VMEM((4, 2 * HD, features), weight.dtype),
-                pltpu.SemaphoreType.DMA((4,)),
+                pltpu.SemaphoreType.DMA((5,)),
             ],
         ),
         out_shape=jax.ShapeDtypeStruct((2, 4, tokens, HD), dtype),
-        compiler_params=pltpu.CompilerParams(vmem_limit_bytes=24 << 20),
+        compiler_params=pltpu.CompilerParams(vmem_limit_bytes=12 << 20),
         cost_estimate=pl.CostEstimate(
             flops=2 * tokens * features * 8 * HD,
             bytes_accessed=2 * features * 8 * HD + 2 * tokens * features,
             transcendentals=0,
         ),
-    )(core.reshape(1), hidden, weight)
-
-
-def grad_kernel(table_ref, *refs):
-    pieces, (hidden_ref, hidden_other_ref), rest = refs[:4], refs[4:6], refs[6:]
-    out_ref, total, sems = rest[-3:]
+    )(
+        core.reshape(1),
+        pltpu.with_memory_space_constraint(hidden, pltpu.HBM),
+        pltpu.with_memory_space_constraint(weight, pltpu.HBM),
+    )
+
+
+def load_kernel(core_ref, weight_ref, send_ref, keep_ref, sems):
     copies = []
-    for g in range(2):
-        left = jnp.concatenate([pieces[g][i] for i in range(4)], axis=0)
-        right = jnp.concatenate([pieces[2 + g][i] for i in range(4)], axis=0)
+    for half, store_ref in enumerate((send_ref, keep_ref)):
+        core = (1 - core_ref[0]) if half == 0 else core_ref[0]
+        for y in range(2):
+            for z0 in range(2):
+                row = pl.multiple_of((4 * z0 + 2 * y + core) * 2 * HD, 2 * HD)
+                slot = 2 * y + z0
+                copy = pltpu.make_async_copy(
+                    weight_ref.at[pl.ds(row, 2 * HD)], store_ref.at[slot], sems.at[4 * half + slot]
+                )
+                copy.start()
+                copies.append(copy)
+    for copy in copies:
+        copy.wait()
+
+
+def load_weights(weight, core):
+    vmem = pl.BlockSpec(memory_space=pltpu.VMEM)
+    half = jax.ShapeDtypeStruct((4, 2 * HD, weight.shape[1]), weight.dtype)
+    return pl.pallas_call(
+        load_kernel,
+        name="load_weights",
+        grid_spec=pltpu.PrefetchScalarGridSpec(
+            num_scalar_prefetch=1,
+            grid=(),
+            in_specs=[pl.BlockSpec(memory_space=pltpu.HBM)],
+            out_specs=[vmem] * 2,
+            scratch_shapes=[pltpu.SemaphoreType.DMA((8,))],
+        ),
+        out_shape=[half, half],
+        compiler_params=pltpu.CompilerParams(vmem_limit_bytes=14 << 20),
+    )(core.reshape(1), pltpu.with_memory_space_constraint(weight, pltpu.HBM))
+
+
+def half_product_kernel(hidden_ref, store_ref, out_ref):
+    for y in range(2):
+        for z0 in range(2):
+            tile_product(hidden_ref[...], store_ref[2 * y + z0], out_ref, y, z0)
+
+
+def half_product(hidden, store, dtype):
+    tokens, features = hidden.shape
+    vmem = pl.BlockSpec(memory_space=pltpu.VMEM)
+    return pl.pallas_call(
+        half_product_kernel,
+        in_specs=[vmem] * 2,
+        out_specs=vmem,
+        out_shape=jax.ShapeDtypeStruct((2, 4, tokens, HD), dtype),
+        compiler_params=pltpu.CompilerParams(vmem_limit_bytes=8 << 20),
+        cost_estimate=pl.CostEstimate(
+            flops=2 * tokens * features * 8 * HD,
+            bytes_accessed=2 * features * 8 * HD + 2 * tokens * features,
+            transcendentals=0,
+        ),
+        name="half_product",
+    )(hidden, store)
+
+
+def fill_rows(table_ref, pieces, hidden_ref, hidden_other_ref, out_ref, total, sems):
+    copies = []
+    for g in range(4):
+        left = jnp.concatenate([pieces[g // 2][2 * (g % 2) + i] for i in range(2)], axis=0)
+        right = jnp.concatenate([pieces[2 + g // 2][2 * (g % 2) + i] for i in range(2)], axis=0)
         total[g] = jnp.dot(left, hidden_ref[...], preferred_element_type=jnp.float32) + jnp.dot(
             right, hidden_other_ref[...], preferred_element_type=jnp.float32
         )
-        for i in range(4):
-            row = pl.multiple_of(table_ref[4 * g + i] * HD, HD)
+        for i in range(2):
+            row = pl.multiple_of(table_ref[2 * g + i] * HD, HD)
             copy = pltpu.make_async_copy(
-                total.at[g, pl.ds(i * HD, HD)], out_ref.at[pl.ds(row, HD)], sems.at[4 * g + i]
+                total.at[g, pl.ds(i * HD, HD)], out_ref.at[pl.ds(row, HD)], sems.at[2 * g + i]
             )
             copy.start()
             copies.append(copy)
+    return copies
+
+
+def grad_kernel(table_ref, *refs):
+    pieces, hiddens, (out_ref, token_ref), scratch = refs[:4], refs[4:6], refs[6:8], refs[8:]
+    copies = fill_rows(table_ref, pieces, *hiddens, out_ref, *scratch)
+    token_ref[...] = jnp.zeros_like(token_ref)
     for copy in copies:
         copy.wait()
 
 
-def grad_rows(table, own, other, hidden, hidden_other, rows, previous=None):
+def last_grad_kernel(table_ref, home_ref, dp_ref, *refs):
+    pieces, hiddens, outs = refs[:4], refs[4:6], refs[6:9]
+    out_ref, steps_ref, *scratch = refs[11:]
+    copies = fill_rows(table_ref, pieces, *hiddens, out_ref, *scratch)
+    own, across, beside = (ref[...] for ref in outs)
+    home = home_ref[0] == 1
+    near = jnp.where(home, own, beside)
+    other = jnp.where(home, beside, across)
+    low = dp_ref[0] == 0
+    steps_ref[:, :, :HD] = jnp.where(low, near, other)
+    steps_ref[:, :, HD:] = jnp.where(low, other, near)
+    for copy in copies:
+        copy.wait()
+
+
+def grad_rows(table, own, other, hidden, hidden_other, rows, last=None):
     tokens, features = hidden.shape
     vmem = pl.BlockSpec(memory_space=pltpu.VMEM)
     hbm = pl.BlockSpec(memory_space=pltpu.HBM)
-    before = [] if previous is None else [previous]
-    return pl.pallas_call(
-        grad_kernel,
+    grads = jax.ShapeDtypeStruct((rows, features), jnp.float32)
+    args = [*own, *other, hidden, hidden_other]
+    if last is None:
+        kernel, scalars, in_specs = grad_kernel, [table], [vmem] * 6
+        out_shape, aliases = [grads, jax.ShapeDtypeStruct((8, HD), jnp.float32)], {}
+    else:
+        home, dp, outs, token, previous = last
+        kernel, scalars = last_grad_kernel, [table, home.reshape(1), dp.reshape(1)]
+        in_specs = [vmem] * 10 + [hbm]
+        out_shape = [grads, jax.ShapeDtypeStruct((2, tokens, 2 * HD), jnp.bfloat16)]
+        aliases = {13: 0}
+        args = args + [*outs, token, previous]
+    return pl.pallas_call(
+        kernel,
+        name="grad_rows",
         grid_spec=pltpu.PrefetchScalarGridSpec(
-            num_scalar_prefetch=1,
+            num_scalar_prefetch=len(scalars),
             grid=(),
-            in_specs=[vmem] * 6 + [hbm] * len(before),
-            out_specs=hbm,
+            in_specs=in_specs,
+            out_specs=[hbm, vmem],
             scratch_shapes=[
-                pltpu.VMEM((2, 4 * HD, features), jnp.float32),
+                pltpu.VMEM((4, 2 * HD, features), jnp.float32),
                 pltpu.SemaphoreType.DMA((8,)),
             ],
         ),
-        out_shape=jax.ShapeDtypeStruct((rows, features), jnp.float32),
-        input_output_aliases={7: 0} if before else {},
-        compiler_params=pltpu.CompilerParams(vmem_limit_bytes=32 << 20),
+        out_shape=out_shape,
+        input_output_aliases=aliases,
+        compiler_params=pltpu.CompilerParams(vmem_limit_bytes=14 << 20),
         cost_estimate=pl.CostEstimate(
             flops=32 * HD * tokens * features,
             bytes_accessed=32 * HD * features,
             transcendentals=0,
         ),
-    )(table, *own, *other, hidden, hidden_other, *before)
-
-
-def pack_kernel(dp_ref, cot_ref, query_ref, key_ref, mask_ref, first_ref, second_ref):
+    )(*scalars, *args)
+
+
+def pack_kernel(head_ref, cot_ref, query_ref, key_ref, mask_ref, first_ref, second_ref):
     tokens = cot_ref.shape[1]
     for r, out_ref in enumerate((first_ref, second_ref)):
-        lanes = pl.ds(pl.multiple_of((dp_ref[0] ^ r) * HD, HD), HD)
+        lanes = pl.ds(pl.multiple_of((head_ref[0] ^ r) * HD, HD), HD)
         out_ref[:tokens] = cot_ref[0, :, lanes]
         out_ref[tokens : 2 * tokens] = cot_ref[1, :, lanes]
         terms = []
@@ -242,7 +344,7 @@
         out_ref[2 * tokens + 16 :] = mask_ref[...].astype(jnp.bfloat16)
 
 
-def pack(dp, cotangent, gain_query, gain_key, block_mask):
+def pack(head, cotangent, gain_query, gain_key, block_mask):
     tokens = cotangent.shape[1]
     blocks = block_mask.shape[0]
     mask = jnp.pad(block_mask.astype(jnp.float32), ((0, 16 - blocks), (0, HD - blocks)))
@@ -250,11 +352,13 @@
     shape = jax.ShapeDtypeStruct((2 * tokens + 32, HD), jnp.bfloat16)
     return pl.pallas_call(
         pack_kernel,
+        name="pack",
         grid_spec=pltpu.PrefetchScalarGridSpec(
             num_scalar_prefetch=1, grid=(), in_specs=[vmem] * 4, out_specs=[vmem] * 2
         ),
         out_shape=[shape, shape],
-    )(dp.reshape(1), cotangent, gain_query.reshape(1, -1), gain_key.reshape(1, -1), mask)
+        compiler_params=pltpu.CompilerParams(vmem_limit_bytes=4 << 20),
+    )(head.reshape(1), cotangent, gain_query.reshape(1, -1), gain_key.reshape(1, -1), mask)
 
 
 def core_sum_kernel(y_ref, kept_ref, got_ref, send_ref, keep_ref):
@@ -267,6 +371,7 @@
     vmem = pl.BlockSpec(memory_space=pltpu.VMEM)
     return pl.pallas_call(
         core_sum_kernel,
+        name="core_sum",
         grid_spec=pltpu.PrefetchScalarGridSpec(
             num_scalar_prefetch=1, grid=(), in_specs=[vmem] * 2, out_specs=[vmem] * 2
         ),
@@ -274,6 +379,7 @@
             jax.ShapeDtypeStruct(kept.shape[1:], jnp.bfloat16),
             jax.ShapeDtypeStruct(kept.shape[1:], jnp.float32),
         ],
+        compiler_params=pltpu.CompilerParams(vmem_limit_bytes=4 << 20),
     )(y.reshape(1), kept, got)
 
 
@@ -289,11 +395,13 @@
     vmem = pl.BlockSpec(memory_space=pltpu.VMEM)
     return pl.pallas_call(
         row_sum_kernel,
+        name="row_sum",
         grid_spec=pltpu.PrefetchScalarGridSpec(
             num_scalar_prefetch=1, grid=(), in_specs=[vmem] * 2, out_specs=[vmem] * 4
         ),
         out_shape=[jax.ShapeDtypeStruct(kept.shape[1:], jnp.float32)]
         + [jax.ShapeDtypeStruct(kept.shape[1:], jnp.bfloat16)] * 3,
+        compiler_params=pltpu.CompilerParams(vmem_limit_bytes=4 << 20),
     )(z.reshape(1), kept, got)
 
 
@@ -331,7 +439,7 @@
     f32, bf16 = jnp.float32, jnp.bfloat16
     tokens = kept_ref.shape[0]
     scale = HD ** (-0.5)
-    message = jnp.where(which_ref[0] == 0, first_ref[...], second_ref[...])
+    message = jnp.where(which_ref[0] == 1, first_ref[...], second_ref[...])
     joined = kept_ref[...] + near_ref[...].astype(f32) + mid_ref[...].astype(f32)
     joined = (joined + far_ref[...].astype(f32)).astype(bf16)
     cot_one = message[:tokens]
@@ -362,11 +470,10 @@
     soft_one = expo * (1.0 / row_total(expo))
     weights_one = soft_one.astype(bf16)
     step_one = dot(weights_one, joined, NN).astype(bf16)
-    out_ref[0] = step_one
-
-    step = step_one.astype(f32)
-    inverse_two = lax.rsqrt(row_mean(step * step) + EPS)
-    renormed = step * inverse_two
+
+    step_values = step_one.astype(f32)
+    inverse_two = lax.rsqrt(row_mean(step_values * step_values) + EPS)
+    renormed = step_values * inverse_two
     query_two = renormed * gain_query
     own_key = renormed * gain_key
     queries_two = halves(query_two)
@@ -379,13 +486,14 @@
     soft_two = expo * share
     own_soft = own_expo * share
     weights_two = soft_two.astype(bf16)
-    step_two = dot(weights_two, joined, NN) + own_soft * step
+    step_two = dot(weights_two, joined, NN) + own_soft * step_values
+    out_ref[0] = step_one
     out_ref[1] = step_two.astype(bf16)
 
     d_two = cot_two.astype(f32)
     d_soft = dot(cot_two, joined, NT).astype(bf16).astype(f32)
     d_joined = dot(weights_two, cot_two, TN)
-    d_own = row_total(d_two * step)
+    d_own = row_total(d_two * step_values)
     d_step = own_soft * d_two
     shared = row_total(soft_two * d_soft) + own_soft * d_own
     d_scores = halves(soft_two * (d_soft - shared) * scale)
@@ -405,11 +513,12 @@
     grad_ref[...] = d_joined.T.astype(bf16)
 
 
-def attention(which, kept, pieces, messages):
+def attention(home, kept, pieces, messages):
     tokens = kept.shape[0]
     vmem = pl.BlockSpec(memory_space=pltpu.VMEM)
     return pl.pallas_call(
         attention_kernel,
+        name="attention",
         grid_spec=pltpu.PrefetchScalarGridSpec(
             num_scalar_prefetch=1, grid=(), in_specs=[vmem] * 6, out_specs=[vmem] * 2
         ),
@@ -417,13 +526,13 @@
             jax.ShapeDtypeStruct((2, tokens, HD), jnp.bfloat16),
             jax.ShapeDtypeStruct((HD, tokens), jnp.bfloat16),
         ],
-        compiler_params=pltpu.CompilerParams(vmem_limit_bytes=24 << 20),
+        compiler_params=pltpu.CompilerParams(vmem_limit_bytes=12 << 20),
         cost_estimate=pl.CostEstimate(
             flops=24 * 2 * tokens * tokens * HD,
             bytes_accessed=16 * tokens * HD,
             transcendentals=2 * tokens * tokens,
         ),
-    )(which.astype(jnp.int32).reshape(1), kept, *pieces, *messages)
+    )(home.reshape(1), kept, *pieces, *messages)
 
 
 def keep_weights_plan(hidden, fc_weight, gain_query, gain_key, block_mask, cotangent):
@@ -431,60 +540,75 @@
     me_z = lax.axis_index("mp")
     me_y = lax.axis_index("section") >> 1
     me_c = lax.axis_index("section") & 1
-    upper = me_z >> 1
     over_x = swap("dp", 2, 1)
     over_y = swap("section", 4, 2)
     over_c = swap("section", 4, 1)
     over_z = [swap("mp", 4, bit) for bit in range(4)]
-
-    def route(r):
-        return [
-            (4 * d + 2 * e + b, 4 * e + 2 * (d ^ r) + b)
-            for d in range(2)
-            for e in range(2)
-            for b in range(2)
+    at_home = (me_z >> 1) == me_dp
+    home = at_home.astype(jnp.int32)
+
+    def far_half(kept, got):
+        kept, *sent = row_sum(me_z, kept, got)
+        return kept, [over_z[b](sent[b - 1]) for b in (3, 2, 1)], sent
+
+    def spread_z(piece, *first):
+        return jnp.stack([piece] + [after(over_z[b](piece), *first) for b in (1, 2, 3)])
+
+    hidden_other = over_x(hidden)
+    sent = streamed_product(hidden, fc_weight, 1 - me_c, jnp.bfloat16)
+    kept = streamed_product(hidden, fc_weight, me_c, jnp.float32)
+    sent, kept = core_sum(me_y, kept, over_c(sent))
+    got = over_y(sent)
+    stay, go = pack(
+        me_dp ^ (1 - home), after(cotangent, sent), gain_query, gain_key, block_mask
+    )
+    come = over_z[2](go)
+    own_kept, own_pieces, sent = far_half(kept, got)
+    stores = load_weights(after(fc_weight, go), me_c)
+    crossing = jnp.where(at_home, come, stay)
+    late = after(hidden_other, come, *own_pieces, *stores)
+    sent = half_product(late, stores[0], jnp.bfloat16)
+    kept = half_product(late, stores[1], jnp.float32)
+    sent, kept = core_sum(me_y, kept, over_c(sent))
+    got = over_y(sent)
+    crossed = over_x(after(crossing, sent))
+    out_own, d_own = attention(home, after(own_kept, sent), own_pieces, (stay, come))
+    kept, pieces, sent = far_half(kept, after(got, d_own))
+    own_part = spread_z(d_own, *sent)
+    kept = after(kept, own_part)
+    own_rest = over_y(own_part)
+    out_other, d_other = attention(home, kept, pieces, (crossed, crossed))
+    across = over_x(out_other)
+    other_part = spread_z(d_other, across, own_rest)
+    other_rest = over_y(other_part)
+    beside = over_z[2](jnp.where(at_home, across, out_own))
+
+    def table(flip):
+        z = me_z ^ jnp.arange(4)
+        heads = [
+            2 * (4 * (z & 1) + 2 * (me_y ^ flip) + core) + (z >> 1) for core in (me_c, 1 - me_c)
         ]
-
-    hidden_other = over_x(hidden)
-    messages = pack(me_dp, cotangent, gain_query, gain_key, block_mask)
-    messages = [lax.ppermute(messages[r], ("dp", "mp"), route(r)) for r in range(2)]
-    own_at = upper ^ me_dp
-
-    def scatter_sum(tokens_in):
-        sent = half_product(tokens_in, fc_weight, 1 - me_c, jnp.bfloat16)
-        kept = half_product(tokens_in, fc_weight, me_c, jnp.float32)
-        send, kept = core_sum(me_y, kept, over_c(sent))
-        kept, *send = row_sum(me_z, kept, over_y(send))
-        return kept, [over_z[b](send[b - 1]) for b in (1, 2, 3)]
-
-    def spread(piece):
-        part = jnp.stack([piece] + [over_z[b](piece) for b in (1, 2, 3)])
-        rest = over_y(part)
-        return (part, over_c(part)), (rest, over_c(rest))
-
-    out_own, d_own = attention(own_at, *scatter_sum(hidden), messages)
-    out_other, d_other = attention(1 - own_at, *scatter_sum(hidden_other), messages)
-    own_parts = spread(d_own)
-    other_parts = spread(d_other)
+        return jnp.concatenate(heads).astype(jnp.int32)
 
     rows = fc_weight.shape[0]
-    fc_grad = None
-    for flip in range(2):
-        heads = []
-        for core in (me_c, 1 - me_c):
-            z = me_z ^ jnp.arange(4)
-            heads.append(2 * (4 * (z & 1) + 2 * (me_y ^ flip) + core) + (z >> 1))
-        table = jnp.concatenate(heads).astype(jnp.int32)
-        fc_grad = grad_rows(
-            table, own_parts[flip], other_parts[flip], hidden, hidden_other, rows, fc_grad
-        )
-    back = []
-    for r in range(2):
-        sent = jnp.where(own_at == r, out_own, out_other)
-        back.append(lax.ppermute(sent, ("dp", "mp"), [(b, a) for a, b in route(r)]))
-    low = jnp.where(me_dp == 0, back[0], back[1])
-    high = jnp.where(me_dp == 0, back[1], back[0])
-    ttt_out = jnp.concatenate([low, high], axis=2)
+    fc_grad, token = grad_rows(
+        table(0),
+        (own_part, over_c(own_part)),
+        (other_part, over_c(other_part)),
+        hidden,
+        hidden_other,
+        rows,
+    )
+    other_rest, token, beside = lax.optimization_barrier((other_rest, token, beside))
+    fc_grad, ttt_out = grad_rows(
+        table(1),
+        (own_rest, over_c(own_rest)),
+        (other_rest, over_c(other_rest)),
+        hidden,
+        hidden_other,
+        rows,
+        (home, me_dp, (out_own, across, beside), token, fc_grad),
+    )
     return (ttt_out, fc_grad)
 
 

time: 122 us -> 77.8 us (0.64)
  local copies, waits for them, and re-layouts: 18 us -> 0.05 us
  waiting for transfers between devices: 31.2 us -> 20.8 us
  Pallas kernels: 34.9 us -> 25.3 us
  starting transfers between devices: 35.7 us -> 30.3 us
    unnamed x28 -> x12, local copies, waits for them, and re-layouts: 17.4 us -> 0.04 us
    pallas_call x13 -> x14, Pallas kernels: 34.9 us -> 25.3 us  [the longest x2 8.4 us: grad_rows(): pl.pallas_call(kernel, name='grad_rows', grid_spec=pltpu.PrefetchScalarGr...]
    ppermute x4 -> x0, starting transfers between devices: 8.59 us -> none  [the longest x2 6.06 us: keep_weights_plan(): lax.ppermute(messages[r], ('dp', 'mp'), route(r))]
    ppermute x4 -> x0, waiting for transfers between devices: 5.9 us -> none  [the longest x2 5.89 us: keep_weights_plan(): back.append(lax.ppermute(sent, ('dp', 'mp'), [(b, a) for a, b in route(r)]))]
    ppermute x23 -> x27, waiting for transfers between devices: 25.3 us -> 20.8 us  [swap(): lax.ppermute(array, axis, [(i, i ^ bit) for i in range(size)])]
    ppermute x23 -> x27, starting transfers between devices: 27.1 us -> 30.3 us  [swap(): lax.ppermute(array, axis, [(i, i ^ bit) for i in range(size)])]
  transfers between devices with their start and end apart: 27 -> 27, of which waited for: 6 -> 10; matrix products, arithmetic and copies ran while one was open for 1% -> 0% of each run, Pallas kernels for 25% -> 21%
where the time goes in v3:
time: 77.8 us; the launch traced here: 77.7 us
  starting transfers between devices  30.3 us (39%)
  Pallas kernels  25.3 us (33%)
  waiting for transfers between devices  20.8 us (27%)
  between operations  0.89 us (1%)
    ppermute x27, starting transfers between devices, swap(): lax.ppermute(array, axis, [(i, i ^ bit) for i in range(size)])  30.3 us
    ppermute x27, waiting for transfers between devices, swap(): lax.ppermute(array, axis, [(i, i ^ bit) for i in range(size)])  20.8 us
    pallas_call x2, Pallas kernels, grad_rows(): pl.pallas_call(kernel, name='grad_rows', grid_spec=pltpu.PrefetchScalarGr...  8.4 us
    pallas_call x2, Pallas kernels, streamed_product(): pl.pallas_call(streamed_product_kernel, name='streamed_product', grid_spe...  6.33 us
    pallas_call x2, Pallas kernels, attention(): pl.pallas_call(attention_kernel, name='attention', grid_spec=pltpu.Prefet...  5.3 us
    pallas_call x1, Pallas kernels, load_weights(): pl.pallas_call(load_kernel, name='load_weights', grid_spec=pltpu.Prefetch...  2.86 us
    pallas_call x2, Pallas kernels, half_product(): pl.pallas_call(half_product_kernel, in_specs=[vmem] * 2, out_specs=vmem,...  2.02 us
  transfers between devices with their start and end apart: 27, of which 10 were waited for; matrix products, arithmetic and copies ran while one was open for 0% of the time, Pallas kernels for 21%

profile of v3, /device:TPU:0, one launch (start us, length us, event | category | flops | bytes accessed | tf_op | source)
XLA Modules:
  0.0 77.7 jit_solution(16433561499652345026)
XLA Ops:
  0.6 3.2 %streamed_product.3 = bf16[2,4,256,128]{3,2,1,0:T(8,128)(2,1)S(1)} custom-call(s32[1]{0:T(128)} %bitcast.5.core_ref, bf16[256,1536]{1,0:T(8,128)(2,1)} %refs_4_.3, bf16[2048,1536]{1,0:T(8,128)(2,1)} %weight_ref.4), custom_call_target="tpu_custom_call" | custom-call | flops 805306368 | bytes 3932160 | tf_op jit(solution)/shard_map/streamed_product/pallas_call | solution.py:161
  4.4 2.6 %collective-permute-start.2 = (bf16[256,1536]{1,0:T(8,128)(2,1)S(1)}, bf16[256,1536]{1,0:T(8,128)(2,1)S(1)}, u32[]{:S(2)}, u32[]{:S(2)}) collective-permute-start(bf16[256,1536]{1,0:T(8,128)(2,1)S(1)} %copy-done), channel_id=1, source_target_pairs={{0,16},{16,0},{1,17},{17,1},{2,18},{18,2},{3,19},{19,3},{4,20},{20... | collective-permute-start | bytes 2359304 | tf_op jit(solution)/shard_map/ppermute | solution.py:126
  7.0 3.1 %streamed_product.2.kept_ref = f32[2,4,256,128]{3,2,1,0:T(8,128)S(1)} custom-call(s32[1]{0:T(128)} %bitcast.4.core_ref, bf16[256,1536]{1,0:T(8,128)(2,1)} %refs_4_.3, bf16[2048,1536]{1,0:T(8,128)(2,1)} %weight_ref.4), custom_call_target="tpu_custom_call" | custom-call | flops 805306368 | bytes 3932160 | tf_op jit(solution)/shard_map/streamed_product/pallas_call | solution.py:161
  10.3 1.6 %collective-permute-start.1 = (bf16[4,256,128]{2,1,0:T(8,128)(2,1)S(1)}, bf16[4,256,128]{2,1,0:T(8,128)(2,1)S(1)}, u32[]{:S(2)}, u32[]{:S(2)}) collective-permute-start(bf16[4,256,128]{2,1,0:T(8,128)(2,1)S(1)} %get-tuple-element.43), channel_id=1, source_target_pairs={{0,2},{1,3},{2,0},{3,1},{4,6},{5,7},{6,4},{7,5},{8,10},{9,11},{10,... | collective-permute-start | bytes 786440 | tf_op jit(solution)/shard_map/ppermute | solution.py:126
  12.0 2.7 %collective-permute-start.3 = (bf16[544,128]{1,0:T(8,128)(2,1)S(1)}, bf16[544,128]{1,0:T(8,128)(2,1)S(1)}, u32[]{:S(2)}, u32[]{:S(2)}) collective-permute-start(bf16[544,128]{1,0:T(8,128)(2,1)S(1)} %get-tuple-element.46), channel_id=1, source_target_pairs={{0,8},{4,12},{8,0},{12,4},{1,9},{5,13},{9,1},{13,5},{2,10},{6,14},... | collective-permute-start | bytes 417800 | tf_op jit(solution)/shard_map/ppermute | solution.py:126
  14.6 4.1 %collective-permute-done.1.got_ref = bf16[4,256,128]{2,1,0:T(8,128)(2,1)S(1)} collective-permute-done((bf16[4,256,128]{2,1,0:T(8,128)(2,1)S(1)}, bf16[4,256,128]{2,1,0:T(8,128)(2,1)S(1)}, u32[]{:S(2)}, u32[]{:S(2)}) %collective-permute-start.1) | collective-permute-done | bytes 262176 | tf_op jit(solution)/shard_map/ppermute | solution.py:126
  18.8 3.7 %collective-permute-start.4 = (bf16[256,128]{1,0:T(8,128)(2,1)S(1)}, bf16[256,128]{1,0:T(8,128)(2,1)S(1)}, u32[]{:S(2)}, u32[]{:S(2)}) collective-permute-start(bf16[256,128]{1,0:T(8,128)(2,1)S(1)} %get-tuple-element.47), channel_id=1, source_target_pairs={{0,12},{4,8},{8,4},{12,0},{1,13},{5,9},{9,5},{13,1},{2,14},{6,10},... | collective-permute-start | bytes 196616 | tf_op jit(solution)/shard_map/ppermute | solution.py:126
  23.2 2.9 %load_weights.1 = (bf16[4,256,1536]{2,1,0:T(8,128)(2,1)S(1)}, bf16[4,256,1536]{2,1,0:T(8,128)(2,1)S(1)}) custom-call(s32[1]{0:T(128)} %bitcast.4.core_ref, bf16[2048,1536]{1,0:T(8,128)(2,1)} %weight_ref.4), custom_call_target="tpu_custom_call" | custom-call | tf_op jit(solution)/shard_map/load_weights/pallas_call | solution.py:209
  26.1 1.6 %collective-permute-done.5.mid_ref = bf16[256,128]{1,0:T(8,128)(2,1)S(1)} collective-permute-done((bf16[256,128]{1,0:T(8,128)(2,1)S(1)}, bf16[256,128]{1,0:T(8,128)(2,1)S(1)}, u32[]{:S(2)}, u32[]{:S(2)}) %collective-permute-start.5) | collective-permute-done | bytes 65568 | tf_op jit(solution)/shard_map/ppermute | solution.py:126
  30.8 1.6 %collective-permute-start.9 = (bf16[4,256,128]{2,1,0:T(8,128)(2,1)S(1)}, bf16[4,256,128]{2,1,0:T(8,128)(2,1)S(1)}, u32[]{:S(2)}, u32[]{:S(2)}) collective-permute-start(bf16[4,256,128]{2,1,0:T(8,128)(2,1)S(1)} %get-tuple-element.54), channel_id=1, source_target_pairs={{0,2},{1,3},{2,0},{3,1},{4,6},{5,7},{6,4},{7,5},{8,10},{9,11},{10,... | collective-permute-start | bytes 786440 | tf_op jit(solution)/shard_map/ppermute | solution.py:126
  32.4 2.7 %attention.2 = (bf16[2,256,128]{2,1,0:T(8,128)(2,1)S(1)}, bf16[128,256]{1,0:T(8,128)(2,1)S(1)}) custom-call(s32[1]{0:T(128)} %bitcast.which_ref.home_ref, f32[256,128]{1,0:T(8,128)S(1)} %get-tuple-element.55.kept_ref, bf16[256,128]{1,0:T(8,128)(2,1)S(1)} %collective-permute-done.4.near_ref, bf16[256,128]{1,0:T(8,128)(2,1)S(1)} %collective-permute-done.5.mid_ref, ...), custom_call_target="tpu_custom_call" | custom-call | flops 402653184 | bytes 524288 | tf_op jit(solution)/shard_map/attention/pallas_call | solution.py:519
  35.1 2.6 %collective-permute-start.11 = (bf16[128,256]{1,0:T(8,128)(2,1)S(1)}, bf16[128,256]{1,0:T(8,128)(2,1)S(1)}, u32[]{:S(2)}, u32[]{:S(2)}) collective-permute-start(bf16[128,256]{1,0:T(8,128)(2,1)S(1)} %get-tuple-element.57), channel_id=1, source_target_pairs={{0,12},{4,8},{8,4},{12,0},{1,13},{5,9},{9,5},{13,1},{2,14},{6,10},... | collective-permute-start | bytes 196616 | tf_op jit(solution)/shard_map/ppermute | solution.py:126
  37.7 1.9 %collective-permute-start.8 = (bf16[128,256]{1,0:T(8,128)(2,1)S(1)}, bf16[128,256]{1,0:T(8,128)(2,1)S(1)}, u32[]{:S(2)}, u32[]{:S(2)}) collective-permute-start(bf16[128,256]{1,0:T(8,128)(2,1)S(1)} %get-tuple-element.57), channel_id=1, source_target_pairs={{0,4},{4,0},{8,12},{12,8},{1,5},{5,1},{9,13},{13,9},{2,6},{6,2},{1... | collective-permute-start | bytes 196616 | tf_op jit(solution)/shard_map/ppermute | solution.py:126
  41.6 2.1 %collective-permute-start.15 = (bf16[256,128]{1,0:T(8,128)(2,1)S(1)}, bf16[256,128]{1,0:T(8,128)(2,1)S(1)}, u32[]{:S(2)}, u32[]{:S(2)}) collective-permute-start(bf16[256,128]{1,0:T(8,128)(2,1)S(1)} %get-tuple-element.61), channel_id=1, source_target_pairs={{0,8},{4,12},{8,0},{12,4},{1,9},{5,13},{9,1},{13,5},{2,10},{6,14},... | collective-permute-start | bytes 196616 | tf_op jit(solution)/shard_map/ppermute | solution.py:126
  44.6 2.3 %collective-permute-start.14 = (bf16[256,128]{1,0:T(8,128)(2,1)S(1)}, bf16[256,128]{1,0:T(8,128)(2,1)S(1)}, u32[]{:S(2)}, u32[]{:S(2)}) collective-permute-start(bf16[256,128]{1,0:T(8,128)(2,1)S(1)} %get-tuple-element.62), channel_id=1, source_target_pairs={{0,12},{4,8},{8,4},{12,0},{1,13},{5,9},{9,5},{13,1},{2,14},{6,10},... | collective-permute-start | bytes 196616 | tf_op jit(solution)/shard_map/ppermute | solution.py:126
  47.1 3.5 %collective-permute-done.14.near_ref = bf16[256,128]{1,0:T(8,128)(2,1)S(1)} collective-permute-done((bf16[256,128]{1,0:T(8,128)(2,1)S(1)}, bf16[256,128]{1,0:T(8,128)(2,1)S(1)}, u32[]{:S(2)}, u32[]{:S(2)}) %collective-permute-start.14) | collective-permute-done | bytes 65568 | tf_op jit(solution)/shard_map/ppermute | solution.py:126
  50.6 2.6 %attention.3 = (bf16[2,256,128]{2,1,0:T(8,128)(2,1)S(1)}, bf16[128,256]{1,0:T(8,128)(2,1)S(1)}) custom-call(s32[1]{0:T(128)} %bitcast.which_ref.home_ref, f32[256,128]{1,0:T(8,128)S(1)} %get-tuple-element.67.kept_ref, bf16[256,128]{1,0:T(8,128)(2,1)S(1)} %collective-permute-done.14.near_ref, bf16[256,128]{1,0:T(8,128)(2,1)S(1)} %collective-permute-done.15.mid_ref, ...), custom_call_target="tpu_custom_call" | custom-call | flops 402653184 | bytes 524288 | tf_op jit(solution)/shard_map/attention/pallas_call | solution.py:519
  53.6 2.4 %collective-permute-start.21 = (bf16[128,256]{1,0:T(8,128)(2,1)S(1)}, bf16[128,256]{1,0:T(8,128)(2,1)S(1)}, u32[]{:S(2)}, u32[]{:S(2)}) collective-permute-start(bf16[128,256]{1,0:T(8,128)(2,1)S(1)} %get-tuple-element.69), channel_id=1, source_target_pairs={{0,12},{4,8},{8,4},{12,0},{1,13},{5,9},{9,5},{13,1},{2,14},{6,10},... | collective-permute-start | bytes 196616 | tf_op jit(solution)/shard_map/ppermute | solution.py:126
  56.1 2.0 %collective-permute-start.18 = (bf16[128,256]{1,0:T(8,128)(2,1)S(1)}, bf16[128,256]{1,0:T(8,128)(2,1)S(1)}, u32[]{:S(2)}, u32[]{:S(2)}) collective-permute-start(bf16[128,256]{1,0:T(8,128)(2,1)S(1)} %get-tuple-element.69), channel_id=1, source_target_pairs={{0,4},{4,0},{8,12},{12,8},{1,5},{5,1},{9,13},{13,9},{2,6},{6,2},{1... | collective-permute-start | bytes 196616 | tf_op jit(solution)/shard_map/ppermute | solution.py:126
  58.0 2.1 %collective-permute-done.21 = bf16[128,256]{1,0:T(8,128)(2,1)S(1)} collective-permute-done((bf16[128,256]{1,0:T(8,128)(2,1)S(1)}, bf16[128,256]{1,0:T(8,128)(2,1)S(1)}, u32[]{:S(2)}, u32[]{:S(2)}) %collective-permute-start.21) | collective-permute-done | bytes 65568 | tf_op jit(solution)/shard_map/ppermute | solution.py:126
  62.2 1.7 %collective-permute-start.25 = (bf16[2,256,128]{2,1,0:T(8,128)(2,1)S(1)}, bf16[2,256,128]{2,1,0:T(8,128)(2,1)S(1)}, u32[]{:S(2)}, u32[]{:S(2)}) collective-permute-start(bf16[2,256,128]{2,1,0:T(8,128)(2,1)S(1)} %broadcast_select_fusion.1), channel_id=1, source_target_pairs={{0,8},{4,12},{8,0},{12,4},{1,9},{5,13},{9,1},{13,5},{2,10},{6,14},... | collective-permute-start | bytes 393224 | tf_op jit(solution)/shard_map/ppermute | solution.py:126
  63.9 3.9 %grad_rows.2 = (f32[2048,1536]{1,0:T(8,128)}, f32[8,128]{1,0:T(8,128)S(1)}) custom-call(s32[8]{0:T(128)S(1)} %pad_add_fusion.1.table_ref, bf16[4,128,256]{2,1,0:T(8,128)(2,1)S(1)} %pad_maximum_fusion.refs_0_, bf16[4,128,256]{2,1,0:T(8,128)(2,1)S(1)} %collective-permute-done.23.refs_1_, bf16[4,128,256]{2,1,0:T(8,128)(2,1)S(1)} %pad_maximum_fusion.1.refs_2_, ...), custom_call_target="tpu_custom_call" | custom-call | flops 1610612736 | bytes 6291456 | tf_op jit(solution)/shard_map/grad_rows/pallas_call | solution.py:305
  67.7 3.8 %collective-permute-done.25.refs_8_ = bf16[2,256,128]{2,1,0:T(8,128)(2,1)S(1)} collective-permute-done((bf16[2,256,128]{2,1,0:T(8,128)(2,1)S(1)}, bf16[2,256,128]{2,1,0:T(8,128)(2,1)S(1)}, u32[]{:S(2)}, u32[]{:S(2)}) %collective-permute-start.25) | collective-permute-done | bytes 131104 | tf_op jit(solution)/shard_map/ppermute | solution.py:126
  73.1 4.5 %grad_rows.3 = (f32[2048,1536]{1,0:T(8,128)}, bf16[2,256,256]{2,1,0:T(8,128)(2,1)}) custom-call(s32[8]{0:T(128)S(1)} %pad_add_fusion.table_ref, s32[1]{0:T(128)} %bitcast.which_ref.home_ref, s32[1]{0:T(128)} %bitcast.1.dp_ref, bf16[4,128,256]{2,1,0:T(8,128)(2,1)S(1)} %collective-permute-done.12.refs_0_, ...), custom_call_target="tpu_custom_call", output_to_operand_aliasing={{0}: (13, {})} | custom-call | flops 1610612736 | bytes 6291456 | tf_op jit(solution)/shard_map/grad_rows/pallas_call | solution.py:305
  (68 shorter events, 11.8 us)
Async XLA Ops:
  3.9 6.2 %collective-permute-start = (bf16[2,4,256,128]{3,2,1,0:T(8,128)(2,1)S(1)}, bf16[2,4,256,128]{3,2,1,0:T(8,128)(2,1)S(1)}, u32[]{:S(2)}, u32[]{:S(2)}) collective-permute-start(bf16[2,4,256,128]{3,2,1,0:T(8,128)(2,1)S(1)} %streamed_product.3), channel_id=1, source_target_pairs={{0,1},{1,0},{2,3},{3,2},{4,5},{5,4},{6,7},{7,6},{8,9},{9,8},{10,11... | collective-permute-start | bytes 1572872 | tf_op jit(solution)/shard_map/ppermute | solution.py:126
  4.4 21.7 %collective-permute-start.2 = (bf16[256,1536]{1,0:T(8,128)(2,1)S(1)}, bf16[256,1536]{1,0:T(8,128)(2,1)S(1)}, u32[]{:S(2)}, u32[]{:S(2)}) collective-permute-start(bf16[256,1536]{1,0:T(8,128)(2,1)S(1)} %copy-done), channel_id=1, source_target_pairs={{0,16},{16,0},{1,17},{17,1},{2,18},{18,2},{3,19},{19,3},{4,20},{20... | collective-permute-start | bytes 2359304 | tf_op jit(solution)/shard_map/ppermute | solution.py:126
  10.3 8.4 %collective-permute-start.1 = (bf16[4,256,128]{2,1,0:T(8,128)(2,1)S(1)}, bf16[4,256,128]{2,1,0:T(8,128)(2,1)S(1)}, u32[]{:S(2)}, u32[]{:S(2)}) collective-permute-start(bf16[4,256,128]{2,1,0:T(8,128)(2,1)S(1)} %get-tuple-element.43), channel_id=1, source_target_pairs={{0,2},{1,3},{2,0},{3,1},{4,6},{5,7},{6,4},{7,5},{8,10},{9,11},{10,... | collective-permute-start | bytes 786440 | tf_op jit(solution)/shard_map/ppermute | solution.py:126
  12.0 14.1 %collective-permute-start.3 = (bf16[544,128]{1,0:T(8,128)(2,1)S(1)}, bf16[544,128]{1,0:T(8,128)(2,1)S(1)}, u32[]{:S(2)}, u32[]{:S(2)}) collective-permute-start(bf16[544,128]{1,0:T(8,128)(2,1)S(1)} %get-tuple-element.46), channel_id=1, source_target_pairs={{0,8},{4,12},{8,0},{12,4},{1,9},{5,13},{9,1},{13,5},{2,10},{6,14},... | collective-permute-start | bytes 417800 | tf_op jit(solution)/shard_map/ppermute | solution.py:126
  18.8 7.3 %collective-permute-start.4 = (bf16[256,128]{1,0:T(8,128)(2,1)S(1)}, bf16[256,128]{1,0:T(8,128)(2,1)S(1)}, u32[]{:S(2)}, u32[]{:S(2)}) collective-permute-start(bf16[256,128]{1,0:T(8,128)(2,1)S(1)} %get-tuple-element.47), channel_id=1, source_target_pairs={{0,12},{4,8},{8,4},{12,0},{1,13},{5,9},{9,5},{13,1},{2,14},{6,10},... | collective-permute-start | bytes 196616 | tf_op jit(solution)/shard_map/ppermute | solution.py:126
  22.4 5.3 %collective-permute-start.5 = (bf16[256,128]{1,0:T(8,128)(2,1)S(1)}, bf16[256,128]{1,0:T(8,128)(2,1)S(1)}, u32[]{:S(2)}, u32[]{:S(2)}) collective-permute-start(bf16[256,128]{1,0:T(8,128)(2,1)S(1)} %get-tuple-element.48), channel_id=1, source_target_pairs={{0,8},{4,12},{8,0},{12,4},{1,9},{5,13},{9,1},{13,5},{2,10},{6,14},... | collective-permute-start | bytes 196616 | tf_op jit(solution)/shard_map/ppermute | solution.py:126
  22.4 5.3 %collective-permute-start.6 = (bf16[256,128]{1,0:T(8,128)(2,1)S(1)}, bf16[256,128]{1,0:T(8,128)(2,1)S(1)}, u32[]{:S(2)}, u32[]{:S(2)}) collective-permute-start(bf16[256,128]{1,0:T(8,128)(2,1)S(1)} %get-tuple-element.49), channel_id=1, source_target_pairs={{0,4},{4,0},{8,12},{12,8},{1,5},{5,1},{9,13},{13,9},{2,6},{6,2},{1... | collective-permute-start | bytes 196616 | tf_op jit(solution)/shard_map/ppermute | solution.py:126
  30.8 9.3 %collective-permute-start.9 = (bf16[4,256,128]{2,1,0:T(8,128)(2,1)S(1)}, bf16[4,256,128]{2,1,0:T(8,128)(2,1)S(1)}, u32[]{:S(2)}, u32[]{:S(2)}) collective-permute-start(bf16[4,256,128]{2,1,0:T(8,128)(2,1)S(1)} %get-tuple-element.54), channel_id=1, source_target_pairs={{0,2},{1,3},{2,0},{3,1},{4,6},{5,7},{6,4},{7,5},{8,10},{9,11},{10,... | collective-permute-start | bytes 786440 | tf_op jit(solution)/shard_map/ppermute | solution.py:126
  35.1 6.6 %collective-permute-start.11 = (bf16[128,256]{1,0:T(8,128)(2,1)S(1)}, bf16[128,256]{1,0:T(8,128)(2,1)S(1)}, u32[]{:S(2)}, u32[]{:S(2)}) collective-permute-start(bf16[128,256]{1,0:T(8,128)(2,1)S(1)} %get-tuple-element.57), channel_id=1, source_target_pairs={{0,12},{4,8},{8,4},{12,0},{1,13},{5,9},{9,5},{13,1},{2,14},{6,10},... | collective-permute-start | bytes 196616 | tf_op jit(solution)/shard_map/ppermute | solution.py:126
  37.7 6.9 %collective-permute-start.10 = (bf16[128,256]{1,0:T(8,128)(2,1)S(1)}, bf16[128,256]{1,0:T(8,128)(2,1)S(1)}, u32[]{:S(2)}, u32[]{:S(2)}) collective-permute-start(bf16[128,256]{1,0:T(8,128)(2,1)S(1)} %get-tuple-element.57), channel_id=1, source_target_pairs={{0,8},{4,12},{8,0},{12,4},{1,9},{5,13},{9,1},{13,5},{2,10},{6,14},... | collective-permute-start | bytes 196616 | tf_op jit(solution)/shard_map/ppermute | solution.py:126
  37.7 9.2 %collective-permute-start.8 = (bf16[128,256]{1,0:T(8,128)(2,1)S(1)}, bf16[128,256]{1,0:T(8,128)(2,1)S(1)}, u32[]{:S(2)}, u32[]{:S(2)}) collective-permute-start(bf16[128,256]{1,0:T(8,128)(2,1)S(1)} %get-tuple-element.57), channel_id=1, source_target_pairs={{0,4},{4,0},{8,12},{12,8},{1,5},{5,1},{9,13},{13,9},{2,6},{6,2},{1... | collective-permute-start | bytes 196616 | tf_op jit(solution)/shard_map/ppermute | solution.py:126
  39.6 7.5 %collective-permute-start.17 = (bf16[544,128]{1,0:T(8,128)(2,1)S(1)}, bf16[544,128]{1,0:T(8,128)(2,1)S(1)}, u32[]{:S(2)}, u32[]{:S(2)}) collective-permute-start(bf16[544,128]{1,0:T(8,128)(2,1)S(1)} %broadcast_select_fusion), channel_id=1, source_target_pairs={{0,16},{16,0},{1,17},{17,1},{2,18},{18,2},{3,19},{19,3},{4,20},{20... | collective-permute-start | bytes 417800 | tf_op jit(solution)/shard_map/ppermute | solution.py:126
  40.2 6.9 %collective-permute-start.16 = (bf16[256,128]{1,0:T(8,128)(2,1)S(1)}, bf16[256,128]{1,0:T(8,128)(2,1)S(1)}, u32[]{:S(2)}, u32[]{:S(2)}) collective-permute-start(bf16[256,128]{1,0:T(8,128)(2,1)S(1)} %get-tuple-element.60), channel_id=1, source_target_pairs={{0,4},{4,0},{8,12},{12,8},{1,5},{5,1},{9,13},{13,9},{2,6},{6,2},{1... | collective-permute-start | bytes 196616 | tf_op jit(solution)/shard_map/ppermute | solution.py:126
  41.6 5.5 %collective-permute-start.15 = (bf16[256,128]{1,0:T(8,128)(2,1)S(1)}, bf16[256,128]{1,0:T(8,128)(2,1)S(1)}, u32[]{:S(2)}, u32[]{:S(2)}) collective-permute-start(bf16[256,128]{1,0:T(8,128)(2,1)S(1)} %get-tuple-element.61), channel_id=1, source_target_pairs={{0,8},{4,12},{8,0},{12,4},{1,9},{5,13},{9,1},{13,5},{2,10},{6,14},... | collective-permute-start | bytes 196616 | tf_op jit(solution)/shard_map/ppermute | solution.py:126
  44.6 6.1 %collective-permute-start.14 = (bf16[256,128]{1,0:T(8,128)(2,1)S(1)}, bf16[256,128]{1,0:T(8,128)(2,1)S(1)}, u32[]{:S(2)}, u32[]{:S(2)}) collective-permute-start(bf16[256,128]{1,0:T(8,128)(2,1)S(1)} %get-tuple-element.62), channel_id=1, source_target_pairs={{0,12},{4,8},{8,4},{12,0},{1,13},{5,9},{9,5},{13,1},{2,14},{6,10},... | collective-permute-start | bytes 196616 | tf_op jit(solution)/shard_map/ppermute | solution.py:126
  46.9 13.3 %collective-permute-start.12 = (bf16[4,128,256]{2,1,0:T(8,128)(2,1)S(1)}, bf16[4,128,256]{2,1,0:T(8,128)(2,1)S(1)}, u32[]{:S(2)}, u32[]{:S(2)}) collective-permute-start(bf16[4,128,256]{2,1,0:T(8,128)(2,1)S(1)} %pad_maximum_fusion.refs_0_), channel_id=1, source_target_pairs={{0,2},{1,3},{2,0},{3,1},{4,6},{5,7},{6,4},{7,5},{8,10},{9,11},{10,... | collective-permute-start | bytes 786440 | tf_op jit(solution)/shard_map/ppermute | solution.py:126
  53.3 6.9 %collective-permute-start.19 = (bf16[2,256,128]{2,1,0:T(8,128)(2,1)S(1)}, bf16[2,256,128]{2,1,0:T(8,128)(2,1)S(1)}, u32[]{:S(2)}, u32[]{:S(2)}) collective-permute-start(bf16[2,256,128]{2,1,0:T(8,128)(2,1)S(1)} %get-tuple-element.70), channel_id=1, source_target_pairs={{0,16},{16,0},{1,17},{17,1},{2,18},{18,2},{3,19},{19,3},{4,20},{20... | collective-permute-start | bytes 393224 | tf_op jit(solution)/shard_map/ppermute | solution.py:126
  53.6 6.5 %collective-permute-start.21 = (bf16[128,256]{1,0:T(8,128)(2,1)S(1)}, bf16[128,256]{1,0:T(8,128)(2,1)S(1)}, u32[]{:S(2)}, u32[]{:S(2)}) collective-permute-start(bf16[128,256]{1,0:T(8,128)(2,1)S(1)} %get-tuple-element.69), channel_id=1, source_target_pairs={{0,12},{4,8},{8,4},{12,0},{1,13},{5,9},{9,5},{13,1},{2,14},{6,10},... | collective-permute-start | bytes 196616 | tf_op jit(solution)/shard_map/ppermute | solution.py:126
  56.0 5.4 %collective-permute-start.20 = (bf16[128,256]{1,0:T(8,128)(2,1)S(1)}, bf16[128,256]{1,0:T(8,128)(2,1)S(1)}, u32[]{:S(2)}, u32[]{:S(2)}) collective-permute-start(bf16[128,256]{1,0:T(8,128)(2,1)S(1)} %get-tuple-element.69), channel_id=1, source_target_pairs={{0,8},{4,12},{8,0},{12,4},{1,9},{5,13},{9,1},{13,5},{2,10},{6,14},... | collective-permute-start | bytes 196616 | tf_op jit(solution)/shard_map/ppermute | solution.py:126
  56.1 5.4 %collective-permute-start.18 = (bf16[128,256]{1,0:T(8,128)(2,1)S(1)}, bf16[128,256]{1,0:T(8,128)(2,1)S(1)}, u32[]{:S(2)}, u32[]{:S(2)}) collective-permute-start(bf16[128,256]{1,0:T(8,128)(2,1)S(1)} %get-tuple-element.69), channel_id=1, source_target_pairs={{0,4},{4,0},{8,12},{12,8},{1,5},{5,1},{9,13},{13,9},{2,6},{6,2},{1... | collective-permute-start | bytes 196616 | tf_op jit(solution)/shard_map/ppermute | solution.py:126
  60.1 3.7 %collective-permute-start.23 = (bf16[4,128,256]{2,1,0:T(8,128)(2,1)S(1)}, bf16[4,128,256]{2,1,0:T(8,128)(2,1)S(1)}, u32[]{:S(2)}, u32[]{:S(2)}) collective-permute-start(bf16[4,128,256]{2,1,0:T(8,128)(2,1)S(1)} %pad_maximum_fusion.refs_0_), channel_id=1, source_target_pairs={{0,1},{1,0},{2,3},{3,2},{4,5},{5,4},{6,7},{7,6},{8,9},{9,8},{10,11... | collective-permute-start | bytes 786440 | tf_op jit(solution)/shard_map/ppermute | solution.py:126
  61.6 10.0 %collective-permute-start.22 = (bf16[4,128,256]{2,1,0:T(8,128)(2,1)S(1)}, bf16[4,128,256]{2,1,0:T(8,128)(2,1)S(1)}, u32[]{:S(2)}, u32[]{:S(2)}) collective-permute-start(bf16[4,128,256]{2,1,0:T(8,128)(2,1)S(1)} %pad_maximum_fusion.1.refs_2_), channel_id=1, source_target_pairs={{0,2},{1,3},{2,0},{3,1},{4,6},{5,7},{6,4},{7,5},{8,10},{9,11},{10,... | collective-permute-start | bytes 786440 | tf_op jit(solution)/shard_map/ppermute | solution.py:126
  62.2 9.4 %collective-permute-start.25 = (bf16[2,256,128]{2,1,0:T(8,128)(2,1)S(1)}, bf16[2,256,128]{2,1,0:T(8,128)(2,1)S(1)}, u32[]{:S(2)}, u32[]{:S(2)}) collective-permute-start(bf16[2,256,128]{2,1,0:T(8,128)(2,1)S(1)} %broadcast_select_fusion.1), channel_id=1, source_target_pairs={{0,8},{4,12},{8,0},{12,4},{1,9},{5,13},{9,1},{13,5},{2,10},{6,14},... | collective-permute-start | bytes 393224 | tf_op jit(solution)/shard_map/ppermute | solution.py:126
  63.9 7.8 %collective-permute-start.13 = (bf16[4,128,256]{2,1,0:T(8,128)(2,1)S(1)}, bf16[4,128,256]{2,1,0:T(8,128)(2,1)S(1)}, u32[]{:S(2)}, u32[]{:S(2)}) collective-permute-start(bf16[4,128,256]{2,1,0:T(8,128)(2,1)S(1)} %collective-permute-done.12.refs_0_), channel_id=1, source_target_pairs={{0,1},{1,0},{2,3},{3,2},{4,5},{5,4},{6,7},{7,6},{8,9},{9,8},{10,11... | collective-permute-start | bytes 786440 | tf_op jit(solution)/shard_map/ppermute | solution.py:126
  (9 other events, 76.8 us)

commit v4 on v3

--- a/solution.py
+++ b/solution.py
@@ -247,25 +247,21 @@
 
 def fill_rows(table_ref, pieces, hidden_ref, hidden_other_ref, out_ref, total, sems):
     copies = []
-    for g in range(4):
-        left = jnp.concatenate([pieces[g // 2][2 * (g % 2) + i] for i in range(2)], axis=0)
-        right = jnp.concatenate([pieces[2 + g // 2][2 * (g % 2) + i] for i in range(2)], axis=0)
-        total[g] = jnp.dot(left, hidden_ref[...], preferred_element_type=jnp.float32) + jnp.dot(
-            right, hidden_other_ref[...], preferred_element_type=jnp.float32
-        )
-        for i in range(2):
-            row = pl.multiple_of(table_ref[2 * g + i] * HD, HD)
-            copy = pltpu.make_async_copy(
-                total.at[g, pl.ds(i * HD, HD)], out_ref.at[pl.ds(row, HD)], sems.at[2 * g + i]
-            )
-            copy.start()
-            copies.append(copy)
+    for head in range(8):
+        side, at = divmod(head, 4)
+        total[head] = jnp.dot(
+            pieces[side][at], hidden_ref[...], preferred_element_type=jnp.float32
+        ) + jnp.dot(pieces[2 + side][at], hidden_other_ref[...], preferred_element_type=jnp.float32)
+        row = pl.multiple_of(table_ref[head] * HD, HD)
+        copy = pltpu.make_async_copy(total.at[head], out_ref.at[pl.ds(row, HD)], sems.at[head])
+        copy.start()
+        copies.append(copy)
     return copies
 
 
 def grad_kernel(table_ref, *refs):
-    pieces, hiddens, (out_ref, token_ref), scratch = refs[:4], refs[4:6], refs[6:8], refs[8:]
-    copies = fill_rows(table_ref, pieces, *hiddens, out_ref, *scratch)
+    pieces, hiddens, (out_ref, token_ref), (total, _, sems) = refs[:4], refs[4:6], refs[6:8], refs[8:]
+    copies = fill_rows(table_ref, pieces, *hiddens, out_ref, total, sems)
     token_ref[...] = jnp.zeros_like(token_ref)
     for copy in copies:
         copy.wait()
@@ -273,15 +269,17 @@
 
 def last_grad_kernel(table_ref, home_ref, dp_ref, *refs):
     pieces, hiddens, outs = refs[:4], refs[4:6], refs[6:9]
-    out_ref, steps_ref, *scratch = refs[11:]
-    copies = fill_rows(table_ref, pieces, *hiddens, out_ref, *scratch)
+    out_ref, steps_ref, total, steps, sems = refs[11:]
     own, across, beside = (ref[...] for ref in outs)
     home = home_ref[0] == 1
     near = jnp.where(home, own, beside)
     other = jnp.where(home, beside, across)
     low = dp_ref[0] == 0
-    steps_ref[:, :, :HD] = jnp.where(low, near, other)
-    steps_ref[:, :, HD:] = jnp.where(low, other, near)
+    steps[:, :, :HD] = jnp.where(low, near, other)
+    steps[:, :, HD:] = jnp.where(low, other, near)
+    copies = [pltpu.make_async_copy(steps, steps_ref, sems.at[8])]
+    copies[0].start()
+    copies += fill_rows(table_ref, pieces, *hiddens, out_ref, total, sems)
     for copy in copies:
         copy.wait()
 
@@ -309,10 +307,11 @@
             num_scalar_prefetch=len(scalars),
             grid=(),
             in_specs=in_specs,
-            out_specs=[hbm, vmem],
+            out_specs=[hbm, vmem if last is None else hbm],
             scratch_shapes=[
-                pltpu.VMEM((4, 2 * HD, features), jnp.float32),
-                pltpu.SemaphoreType.DMA((8,)),
+                pltpu.VMEM((8, HD, features), jnp.float32),
+                pltpu.VMEM((2, tokens, 2 * HD), jnp.bfloat16),
+                pltpu.SemaphoreType.DMA((9,)),
             ],
         ),
         out_shape=out_shape,
@@ -496,18 +495,18 @@
     d_own = row_total(d_two * step_values)
     d_step = own_soft * d_two
     shared = row_total(soft_two * d_soft) + own_soft * d_own
-    d_scores = halves(soft_two * (d_soft - shared) * scale)
+    d_scores = (soft_two * (d_soft - shared) * scale).astype(bf16)
     d_own_score = own_soft * (d_own - shared) * scale
-    d_query = dot_fine(d_scores, keys, NN) + d_own_score * own_key
-    d_keys = dot_fine(d_scores, queries_two, TN)
+    d_query = dot(d_scores, keys[0], NN) + d_own_score * own_key
+    d_keys = dot(d_scores, queries_two[0], TN)
     d_renormed = d_query * gain_query + d_own_score * query_two * gain_key
     d_step = d_step + inverse_two * (d_renormed - renormed * row_mean(d_renormed * renormed))
     d_one = (d_step.astype(bf16).astype(f32) + cot_one.astype(f32)).astype(bf16)
     d_soft = dot(d_one, joined, NT).astype(bf16).astype(f32)
     d_joined = d_joined + dot(weights_one, d_one, TN)
-    d_scores = halves(soft_one * (d_soft - row_total(soft_one * d_soft)) * scale)
-    d_query = dot_fine(d_scores, keys, NN)
-    d_keys = d_keys + dot_fine(d_scores, queries, TN)
+    d_scores = (soft_one * (d_soft - row_total(soft_one * d_soft)) * scale).astype(bf16)
+    d_query = dot(d_scores, keys[0], NN)
+    d_keys = d_keys + dot(d_scores, queries[0], TN)
     d_normed = d_query * gain_query + d_keys * gain_key
     d_joined = d_joined + inverse * (d_normed - normed * row_mean(d_normed * normed))
     grad_ref[...] = d_joined.T.astype(bf16)
@@ -547,9 +546,9 @@
     at_home = (me_z >> 1) == me_dp
     home = at_home.astype(jnp.int32)
 
-    def far_half(kept, got):
+    def far_half(kept, got, bits):
         kept, *sent = row_sum(me_z, kept, got)
-        return kept, [over_z[b](sent[b - 1]) for b in (3, 2, 1)], sent
+        return kept, [over_z[b](sent[b - 1]) for b in bits], sent
 
     def spread_z(piece, *first):
         return jnp.stack([piece] + [after(over_z[b](piece), *first) for b in (1, 2, 3)])
@@ -563,17 +562,18 @@
         me_dp ^ (1 - home), after(cotangent, sent), gain_query, gain_key, block_mask
     )
     come = over_z[2](go)
-    own_kept, own_pieces, sent = far_half(kept, got)
     stores = load_weights(after(fc_weight, go), me_c)
+    own_kept, own_pieces, sent = far_half(kept, after(got, stores[0]), (3, 2, 1))
     crossing = jnp.where(at_home, come, stay)
-    late = after(hidden_other, come, *own_pieces, *stores)
+    late = after(hidden_other, come, *stores)
     sent = half_product(late, stores[0], jnp.bfloat16)
     kept = half_product(late, stores[1], jnp.float32)
+    sent = after(sent, *own_pieces)
     sent, kept = core_sum(me_y, kept, over_c(sent))
     got = over_y(sent)
     crossed = over_x(after(crossing, sent))
     out_own, d_own = attention(home, after(own_kept, sent), own_pieces, (stay, come))
-    kept, pieces, sent = far_half(kept, after(got, d_own))
+    kept, pieces, sent = far_half(kept, after(got, d_own), (2, 3, 1))
     own_part = spread_z(d_own, *sent)
     kept = after(kept, own_part)
     own_rest = over_y(own_part)

time: 77.8 us -> 75.7 us (0.973)
  waiting for transfers between devices: 20.8 us -> 17.4 us
  starting transfers between devices: 30.3 us -> 32.9 us
  Pallas kernels: 25.3 us -> 24 us
    ppermute x27, waiting for transfers between devices: 20.8 us -> 17.4 us  [swap(): lax.ppermute(array, axis, [(i, i ^ bit) for i in range(size)])]
    ppermute x27, starting transfers between devices: 30.3 us -> 32.9 us  [swap(): lax.ppermute(array, axis, [(i, i ^ bit) for i in range(size)])]
    pallas_call x2, Pallas kernels: 8.4 us -> 7.56 us  [grad_rows(): pl.pallas_call(kernel, name='grad_rows', grid_spec=pltpu.PrefetchScalarGr...]
  transfers between devices with their start and end apart: 27 -> 27, of which waited for: 10 -> 10; matrix products, arithmetic and copies ran while one was open for 0% -> 0% of each run, Pallas kernels for 21% -> 22%
where the time goes in v4:
time: 75.7 us; the launch traced here: 75.6 us
  starting transfers between devices  32.9 us (43%)
  Pallas kernels  24 us (32%)
  waiting for transfers between devices  17.4 us (23%)
  between operations  0.87 us (1%)
    ppermute x27, starting transfers between devices, swap(): lax.ppermute(array, axis, [(i, i ^ bit) for i in range(size)])  32.9 us
    ppermute x27, waiting for transfers between devices, swap(): lax.ppermute(array, axis, [(i, i ^ bit) for i in range(size)])  17.4 us
    pallas_call x2, Pallas kernels, grad_rows(): pl.pallas_call(kernel, name='grad_rows', grid_spec=pltpu.PrefetchScalarGr...  7.56 us
    pallas_call x2, Pallas kernels, streamed_product(): pl.pallas_call(streamed_product_kernel, name='streamed_product', grid_spe...  6.33 us
    pallas_call x2, Pallas kernels, attention(): pl.pallas_call(attention_kernel, name='attention', grid_spec=pltpu.Prefet...  4.88 us
    pallas_call x1, Pallas kernels, load_weights(): pl.pallas_call(load_kernel, name='load_weights', grid_spec=pltpu.Prefetch...  2.86 us
    pallas_call x2, Pallas kernels, half_product(): pl.pallas_call(half_product_kernel, in_specs=[vmem] * 2, out_specs=vmem,...  2.01 us
  transfers between devices with their start and end apart: 27, of which 10 were waited for; matrix products, arithmetic and copies ran while one was open for 0% of the time, Pallas kernels for 22%

profile of v4, /device:TPU:0, one launch (start us, length us, event | category | flops | bytes accessed | tf_op | source)
XLA Modules:
  0.0 75.6 jit_solution(9298821158125683470)
XLA Ops:
  0.6 3.2 %streamed_product.3 = bf16[2,4,256,128]{3,2,1,0:T(8,128)(2,1)S(1)} custom-call(s32[1]{0:T(128)} %bitcast.5.core_ref, bf16[256,1536]{1,0:T(8,128)(2,1)} %refs_4_.3, bf16[2048,1536]{1,0:T(8,128)(2,1)} %weight_ref.4), custom_call_target="tpu_custom_call" | custom-call | flops 805306368 | bytes 3932160 | tf_op jit(solution)/shard_map/streamed_product/pallas_call | solution.py:161
  4.4 2.6 %collective-permute-start.2 = (bf16[256,1536]{1,0:T(8,128)(2,1)S(1)}, bf16[256,1536]{1,0:T(8,128)(2,1)S(1)}, u32[]{:S(2)}, u32[]{:S(2)}) collective-permute-start(bf16[256,1536]{1,0:T(8,128)(2,1)S(1)} %copy-done), channel_id=1, source_target_pairs={{0,16},{16,0},{1,17},{17,1},{2,18},{18,2},{3,19},{19,3},{4,20},{20... | collective-permute-start | bytes 2359304 | tf_op jit(solution)/shard_map/ppermute | solution.py:126
  7.0 3.1 %streamed_product.2.kept_ref = f32[2,4,256,128]{3,2,1,0:T(8,128)S(1)} custom-call(s32[1]{0:T(128)} %bitcast.4.core_ref, bf16[256,1536]{1,0:T(8,128)(2,1)} %refs_4_.3, bf16[2048,1536]{1,0:T(8,128)(2,1)} %weight_ref.4), custom_call_target="tpu_custom_call" | custom-call | flops 805306368 | bytes 3932160 | tf_op jit(solution)/shard_map/streamed_product/pallas_call | solution.py:161
  10.3 1.6 %collective-permute-start.1 = (bf16[4,256,128]{2,1,0:T(8,128)(2,1)S(1)}, bf16[4,256,128]{2,1,0:T(8,128)(2,1)S(1)}, u32[]{:S(2)}, u32[]{:S(2)}) collective-permute-start(bf16[4,256,128]{2,1,0:T(8,128)(2,1)S(1)} %get-tuple-element.45), channel_id=1, source_target_pairs={{0,2},{1,3},{2,0},{3,1},{4,6},{5,7},{6,4},{7,5},{8,10},{9,11},{10,... | collective-permute-start | bytes 786440 | tf_op jit(solution)/shard_map/ppermute | solution.py:126
  12.0 2.7 %collective-permute-start.3 = (bf16[544,128]{1,0:T(8,128)(2,1)S(1)}, bf16[544,128]{1,0:T(8,128)(2,1)S(1)}, u32[]{:S(2)}, u32[]{:S(2)}) collective-permute-start(bf16[544,128]{1,0:T(8,128)(2,1)S(1)} %get-tuple-element.47), channel_id=1, source_target_pairs={{0,8},{4,12},{8,0},{12,4},{1,9},{5,13},{9,1},{13,5},{2,10},{6,14},... | collective-permute-start | bytes 417800 | tf_op jit(solution)/shard_map/ppermute | solution.py:126
  14.6 2.9 %load_weights.1 = (bf16[4,256,1536]{2,1,0:T(8,128)(2,1)S(1)}, bf16[4,256,1536]{2,1,0:T(8,128)(2,1)S(1)}) custom-call(s32[1]{0:T(128)} %bitcast.4.core_ref, bf16[2048,1536]{1,0:T(8,128)(2,1)} %weight_ref.4), custom_call_target="tpu_custom_call" | custom-call | tf_op jit(solution)/shard_map/load_weights/pallas_call | solution.py:209
  18.8 3.7 %collective-permute-start.4 = (bf16[256,128]{1,0:T(8,128)(2,1)S(1)}, bf16[256,128]{1,0:T(8,128)(2,1)S(1)}, u32[]{:S(2)}, u32[]{:S(2)}) collective-permute-start(bf16[256,128]{1,0:T(8,128)(2,1)S(1)} %get-tuple-element.54), channel_id=1, source_target_pairs={{0,12},{4,8},{8,4},{12,0},{1,13},{5,9},{9,5},{13,1},{2,14},{6,10},... | collective-permute-start | bytes 196616 | tf_op jit(solution)/shard_map/ppermute | solution.py:126
  23.2 1.9 %collective-permute-done.2.hidden_ref.refs_5_ = bf16[256,1536]{1,0:T(8,128)(2,1)S(1)} collective-permute-done((bf16[256,1536]{1,0:T(8,128)(2,1)S(1)}, bf16[256,1536]{1,0:T(8,128)(2,1)S(1)}, u32[]{:S(2)}, u32[]{:S(2)}) %collective-permute-start.2) | collective-permute-done | bytes 786464 | tf_op jit(solution)/shard_map/ppermute | solution.py:126
  26.2 1.5 %collective-permute-done.5.mid_ref = bf16[256,128]{1,0:T(8,128)(2,1)S(1)} collective-permute-done((bf16[256,128]{1,0:T(8,128)(2,1)S(1)}, bf16[256,128]{1,0:T(8,128)(2,1)S(1)}, u32[]{:S(2)}, u32[]{:S(2)}) %collective-permute-start.5) | collective-permute-done | bytes 65568 | tf_op jit(solution)/shard_map/ppermute | solution.py:126
  29.7 1.6 %collective-permute-start.9 = (bf16[4,256,128]{2,1,0:T(8,128)(2,1)S(1)}, bf16[4,256,128]{2,1,0:T(8,128)(2,1)S(1)}, u32[]{:S(2)}, u32[]{:S(2)}) collective-permute-start(bf16[4,256,128]{2,1,0:T(8,128)(2,1)S(1)} %get-tuple-element.58), channel_id=1, source_target_pairs={{0,2},{1,3},{2,0},{3,1},{4,6},{5,7},{6,4},{7,5},{8,10},{9,11},{10,... | collective-permute-start | bytes 786440 | tf_op jit(solution)/shard_map/ppermute | solution.py:126
  31.3 2.4 %attention.2 = (bf16[2,256,128]{2,1,0:T(8,128)(2,1)S(1)}, bf16[128,256]{1,0:T(8,128)(2,1)S(1)}) custom-call(s32[1]{0:T(128)} %bitcast.which_ref.home_ref, f32[256,128]{1,0:T(8,128)S(1)} %get-tuple-element.59.kept_ref, bf16[256,128]{1,0:T(8,128)(2,1)S(1)} %collective-permute-done.4.near_ref, bf16[256,128]{1,0:T(8,128)(2,1)S(1)} %collective-permute-done.5.mid_ref, ...), custom_call_target="tpu_custom_call" | custom-call | flops 402653184 | bytes 524288 | tf_op jit(solution)/shard_map/attention/pallas_call | solution.py:518
  33.8 2.6 %collective-permute-start.11 = (bf16[128,256]{1,0:T(8,128)(2,1)S(1)}, bf16[128,256]{1,0:T(8,128)(2,1)S(1)}, u32[]{:S(2)}, u32[]{:S(2)}) collective-permute-start(bf16[128,256]{1,0:T(8,128)(2,1)S(1)} %get-tuple-element.61), channel_id=1, source_target_pairs={{0,12},{4,8},{8,4},{12,0},{1,13},{5,9},{9,5},{13,1},{2,14},{6,10},... | collective-permute-start | bytes 196616 | tf_op jit(solution)/shard_map/ppermute | solution.py:126
  36.3 1.9 %collective-permute-start.8 = (bf16[128,256]{1,0:T(8,128)(2,1)S(1)}, bf16[128,256]{1,0:T(8,128)(2,1)S(1)}, u32[]{:S(2)}, u32[]{:S(2)}) collective-permute-start(bf16[128,256]{1,0:T(8,128)(2,1)S(1)} %get-tuple-element.61), channel_id=1, source_target_pairs={{0,4},{4,0},{8,12},{12,8},{1,5},{5,1},{9,13},{13,9},{2,6},{6,2},{1... | collective-permute-start | bytes 196616 | tf_op jit(solution)/shard_map/ppermute | solution.py:126
  40.3 2.6 %collective-permute-start.14 = (bf16[256,128]{1,0:T(8,128)(2,1)S(1)}, bf16[256,128]{1,0:T(8,128)(2,1)S(1)}, u32[]{:S(2)}, u32[]{:S(2)}) collective-permute-start(bf16[256,128]{1,0:T(8,128)(2,1)S(1)} %get-tuple-element.65), channel_id=1, source_target_pairs={{0,8},{4,12},{8,0},{12,4},{1,9},{5,13},{9,1},{13,5},{2,10},{6,14},... | collective-permute-start | bytes 196616 | tf_op jit(solution)/shard_map/ppermute | solution.py:126
  42.9 2.5 %collective-permute-start.15 = (bf16[256,128]{1,0:T(8,128)(2,1)S(1)}, bf16[256,128]{1,0:T(8,128)(2,1)S(1)}, u32[]{:S(2)}, u32[]{:S(2)}) collective-permute-start(bf16[256,128]{1,0:T(8,128)(2,1)S(1)} %get-tuple-element.66), channel_id=1, source_target_pairs={{0,12},{4,8},{8,4},{12,0},{1,13},{5,9},{9,5},{13,1},{2,14},{6,10},... | collective-permute-start | bytes 196616 | tf_op jit(solution)/shard_map/ppermute | solution.py:126
  45.8 3.2 %collective-permute-done.15.mid_ref = bf16[256,128]{1,0:T(8,128)(2,1)S(1)} collective-permute-done((bf16[256,128]{1,0:T(8,128)(2,1)S(1)}, bf16[256,128]{1,0:T(8,128)(2,1)S(1)}, u32[]{:S(2)}, u32[]{:S(2)}) %collective-permute-start.15) | collective-permute-done | bytes 65568 | tf_op jit(solution)/shard_map/ppermute | solution.py:126
  48.9 2.4 %attention.3 = (bf16[2,256,128]{2,1,0:T(8,128)(2,1)S(1)}, bf16[128,256]{1,0:T(8,128)(2,1)S(1)}) custom-call(s32[1]{0:T(128)} %bitcast.which_ref.home_ref, f32[256,128]{1,0:T(8,128)S(1)} %get-tuple-element.71.kept_ref, bf16[256,128]{1,0:T(8,128)(2,1)S(1)} %collective-permute-done.14.near_ref, bf16[256,128]{1,0:T(8,128)(2,1)S(1)} %collective-permute-done.15.mid_ref, ...), custom_call_target="tpu_custom_call" | custom-call | flops 402653184 | bytes 524288 | tf_op jit(solution)/shard_map/attention/pallas_call | solution.py:518
  52.5 2.3 %collective-permute-start.21 = (bf16[128,256]{1,0:T(8,128)(2,1)S(1)}, bf16[128,256]{1,0:T(8,128)(2,1)S(1)}, u32[]{:S(2)}, u32[]{:S(2)}) collective-permute-start(bf16[128,256]{1,0:T(8,128)(2,1)S(1)} %get-tuple-element.73), channel_id=1, source_target_pairs={{0,12},{4,8},{8,4},{12,0},{1,13},{5,9},{9,5},{13,1},{2,14},{6,10},... | collective-permute-start | bytes 196616 | tf_op jit(solution)/shard_map/ppermute | solution.py:126
  54.8 2.1 %collective-permute-start.18 = (bf16[128,256]{1,0:T(8,128)(2,1)S(1)}, bf16[128,256]{1,0:T(8,128)(2,1)S(1)}, u32[]{:S(2)}, u32[]{:S(2)}) collective-permute-start(bf16[128,256]{1,0:T(8,128)(2,1)S(1)} %get-tuple-element.73), channel_id=1, source_target_pairs={{0,4},{4,0},{8,12},{12,8},{1,5},{5,1},{9,13},{13,9},{2,6},{6,2},{1... | collective-permute-start | bytes 196616 | tf_op jit(solution)/shard_map/ppermute | solution.py:126
  56.9 1.8 %collective-permute-done.21 = bf16[128,256]{1,0:T(8,128)(2,1)S(1)} collective-permute-done((bf16[128,256]{1,0:T(8,128)(2,1)S(1)}, bf16[128,256]{1,0:T(8,128)(2,1)S(1)}, u32[]{:S(2)}, u32[]{:S(2)}) %collective-permute-start.21) | collective-permute-done | bytes 65568 | tf_op jit(solution)/shard_map/ppermute | solution.py:126
  60.8 2.0 %collective-permute-start.25 = (bf16[2,256,128]{2,1,0:T(8,128)(2,1)S(1)}, bf16[2,256,128]{2,1,0:T(8,128)(2,1)S(1)}, u32[]{:S(2)}, u32[]{:S(2)}) collective-permute-start(bf16[2,256,128]{2,1,0:T(8,128)(2,1)S(1)} %broadcast_select_fusion.1), channel_id=1, source_target_pairs={{0,8},{4,12},{8,0},{12,4},{1,9},{5,13},{9,1},{13,5},{2,10},{6,14},... | collective-permute-start | bytes 393224 | tf_op jit(solution)/shard_map/ppermute | solution.py:126
  62.8 3.7 %grad_rows.2 = (f32[2048,1536]{1,0:T(8,128)}, f32[8,128]{1,0:T(8,128)S(1)}) custom-call(s32[8]{0:T(128)S(1)} %pad_add_fusion.1.table_ref, bf16[4,128,256]{2,1,0:T(8,128)(2,1)S(1)} %pad_maximum_fusion.refs_0_, bf16[4,128,256]{2,1,0:T(8,128)(2,1)S(1)} %collective-permute-done.23.refs_1_, bf16[4,128,256]{2,1,0:T(8,128)(2,1)S(1)} %pad_maximum_fusion.1.refs_2_, ...), custom_call_target="tpu_custom_call" | custom-call | flops 1610612736 | bytes 6291456 | tf_op jit(solution)/shard_map/grad_rows/pallas_call | solution.py:303
  66.5 3.7 %collective-permute-done.25.refs_8_ = bf16[2,256,128]{2,1,0:T(8,128)(2,1)S(1)} collective-permute-done((bf16[2,256,128]{2,1,0:T(8,128)(2,1)S(1)}, bf16[2,256,128]{2,1,0:T(8,128)(2,1)S(1)}, u32[]{:S(2)}, u32[]{:S(2)}) %collective-permute-start.25) | collective-permute-done | bytes 131104 | tf_op jit(solution)/shard_map/ppermute | solution.py:126
  71.7 3.9 %grad_rows.3 = (f32[2048,1536]{1,0:T(8,128)}, bf16[2,256,256]{2,1,0:T(8,128)(2,1)}) custom-call(s32[8]{0:T(128)S(1)} %pad_add_fusion.table_ref, s32[1]{0:T(128)} %bitcast.which_ref.home_ref, s32[1]{0:T(128)} %bitcast.1.dp_ref, bf16[4,128,256]{2,1,0:T(8,128)(2,1)S(1)} %collective-permute-done.12.refs_0_, ...), custom_call_target="tpu_custom_call", output_to_operand_aliasing={{0}: (13, {})} | custom-call | flops 1610612736 | bytes 6291456 | tf_op jit(solution)/shard_map/grad_rows/pallas_call | solution.py:303
  (68 shorter events, 13.0 us)
Async XLA Ops:
  3.9 6.2 %collective-permute-start = (bf16[2,4,256,128]{3,2,1,0:T(8,128)(2,1)S(1)}, bf16[2,4,256,128]{3,2,1,0:T(8,128)(2,1)S(1)}, u32[]{:S(2)}, u32[]{:S(2)}) collective-permute-start(bf16[2,4,256,128]{3,2,1,0:T(8,128)(2,1)S(1)} %streamed_product.3), channel_id=1, source_target_pairs={{0,1},{1,0},{2,3},{3,2},{4,5},{5,4},{6,7},{7,6},{8,9},{9,8},{10,11... | collective-permute-start | bytes 1572872 | tf_op jit(solution)/shard_map/ppermute | solution.py:126
  4.4 20.7 %collective-permute-start.2 = (bf16[256,1536]{1,0:T(8,128)(2,1)S(1)}, bf16[256,1536]{1,0:T(8,128)(2,1)S(1)}, u32[]{:S(2)}, u32[]{:S(2)}) collective-permute-start(bf16[256,1536]{1,0:T(8,128)(2,1)S(1)} %copy-done), channel_id=1, source_target_pairs={{0,16},{16,0},{1,17},{17,1},{2,18},{18,2},{3,19},{19,3},{4,20},{20... | collective-permute-start | bytes 2359304 | tf_op jit(solution)/shard_map/ppermute | solution.py:126
  10.3 8.4 %collective-permute-start.1 = (bf16[4,256,128]{2,1,0:T(8,128)(2,1)S(1)}, bf16[4,256,128]{2,1,0:T(8,128)(2,1)S(1)}, u32[]{:S(2)}, u32[]{:S(2)}) collective-permute-start(bf16[4,256,128]{2,1,0:T(8,128)(2,1)S(1)} %get-tuple-element.45), channel_id=1, source_target_pairs={{0,2},{1,3},{2,0},{3,1},{4,6},{5,7},{6,4},{7,5},{8,10},{9,11},{10,... | collective-permute-start | bytes 786440 | tf_op jit(solution)/shard_map/ppermute | solution.py:126
  12.0 11.2 %collective-permute-start.3 = (bf16[544,128]{1,0:T(8,128)(2,1)S(1)}, bf16[544,128]{1,0:T(8,128)(2,1)S(1)}, u32[]{:S(2)}, u32[]{:S(2)}) collective-permute-start(bf16[544,128]{1,0:T(8,128)(2,1)S(1)} %get-tuple-element.47), channel_id=1, source_target_pairs={{0,8},{4,12},{8,0},{12,4},{1,9},{5,13},{9,1},{13,5},{2,10},{6,14},... | collective-permute-start | bytes 417800 | tf_op jit(solution)/shard_map/ppermute | solution.py:126
  18.8 7.4 %collective-permute-start.4 = (bf16[256,128]{1,0:T(8,128)(2,1)S(1)}, bf16[256,128]{1,0:T(8,128)(2,1)S(1)}, u32[]{:S(2)}, u32[]{:S(2)}) collective-permute-start(bf16[256,128]{1,0:T(8,128)(2,1)S(1)} %get-tuple-element.54), channel_id=1, source_target_pairs={{0,12},{4,8},{8,4},{12,0},{1,13},{5,9},{9,5},{13,1},{2,14},{6,10},... | collective-permute-start | bytes 196616 | tf_op jit(solution)/shard_map/ppermute | solution.py:126
  22.4 5.3 %collective-permute-start.5 = (bf16[256,128]{1,0:T(8,128)(2,1)S(1)}, bf16[256,128]{1,0:T(8,128)(2,1)S(1)}, u32[]{:S(2)}, u32[]{:S(2)}) collective-permute-start(bf16[256,128]{1,0:T(8,128)(2,1)S(1)} %get-tuple-element.55), channel_id=1, source_target_pairs={{0,8},{4,12},{8,0},{12,4},{1,9},{5,13},{9,1},{13,5},{2,10},{6,14},... | collective-permute-start | bytes 196616 | tf_op jit(solution)/shard_map/ppermute | solution.py:126
  22.4 5.3 %collective-permute-start.6 = (bf16[256,128]{1,0:T(8,128)(2,1)S(1)}, bf16[256,128]{1,0:T(8,128)(2,1)S(1)}, u32[]{:S(2)}, u32[]{:S(2)}) collective-permute-start(bf16[256,128]{1,0:T(8,128)(2,1)S(1)} %get-tuple-element.56), channel_id=1, source_target_pairs={{0,4},{4,0},{8,12},{12,8},{1,5},{5,1},{9,13},{13,9},{2,6},{6,2},{1... | collective-permute-start | bytes 196616 | tf_op jit(solution)/shard_map/ppermute | solution.py:126
  29.7 9.1 %collective-permute-start.9 = (bf16[4,256,128]{2,1,0:T(8,128)(2,1)S(1)}, bf16[4,256,128]{2,1,0:T(8,128)(2,1)S(1)}, u32[]{:S(2)}, u32[]{:S(2)}) collective-permute-start(bf16[4,256,128]{2,1,0:T(8,128)(2,1)S(1)} %get-tuple-element.58), channel_id=1, source_target_pairs={{0,2},{1,3},{2,0},{3,1},{4,6},{5,7},{6,4},{7,5},{8,10},{9,11},{10,... | collective-permute-start | bytes 786440 | tf_op jit(solution)/shard_map/ppermute | solution.py:126
  33.8 6.5 %collective-permute-start.11 = (bf16[128,256]{1,0:T(8,128)(2,1)S(1)}, bf16[128,256]{1,0:T(8,128)(2,1)S(1)}, u32[]{:S(2)}, u32[]{:S(2)}) collective-permute-start(bf16[128,256]{1,0:T(8,128)(2,1)S(1)} %get-tuple-element.61), channel_id=1, source_target_pairs={{0,12},{4,8},{8,4},{12,0},{1,13},{5,9},{9,5},{13,1},{2,14},{6,10},... | collective-permute-start | bytes 196616 | tf_op jit(solution)/shard_map/ppermute | solution.py:126
  36.3 6.5 %collective-permute-start.10 = (bf16[128,256]{1,0:T(8,128)(2,1)S(1)}, bf16[128,256]{1,0:T(8,128)(2,1)S(1)}, u32[]{:S(2)}, u32[]{:S(2)}) collective-permute-start(bf16[128,256]{1,0:T(8,128)(2,1)S(1)} %get-tuple-element.61), channel_id=1, source_target_pairs={{0,8},{4,12},{8,0},{12,4},{1,9},{5,13},{9,1},{13,5},{2,10},{6,14},... | collective-permute-start | bytes 196616 | tf_op jit(solution)/shard_map/ppermute | solution.py:126
  36.3 9.1 %collective-permute-start.8 = (bf16[128,256]{1,0:T(8,128)(2,1)S(1)}, bf16[128,256]{1,0:T(8,128)(2,1)S(1)}, u32[]{:S(2)}, u32[]{:S(2)}) collective-permute-start(bf16[128,256]{1,0:T(8,128)(2,1)S(1)} %get-tuple-element.61), channel_id=1, source_target_pairs={{0,4},{4,0},{8,12},{12,8},{1,5},{5,1},{9,13},{13,9},{2,6},{6,2},{1... | collective-permute-start | bytes 196616 | tf_op jit(solution)/shard_map/ppermute | solution.py:126
  38.2 7.5 %collective-permute-start.17 = (bf16[544,128]{1,0:T(8,128)(2,1)S(1)}, bf16[544,128]{1,0:T(8,128)(2,1)S(1)}, u32[]{:S(2)}, u32[]{:S(2)}) collective-permute-start(bf16[544,128]{1,0:T(8,128)(2,1)S(1)} %broadcast_select_fusion), channel_id=1, source_target_pairs={{0,16},{16,0},{1,17},{17,1},{2,18},{18,2},{3,19},{19,3},{4,20},{20... | collective-permute-start | bytes 417800 | tf_op jit(solution)/shard_map/ppermute | solution.py:126
  38.9 6.9 %collective-permute-start.16 = (bf16[256,128]{1,0:T(8,128)(2,1)S(1)}, bf16[256,128]{1,0:T(8,128)(2,1)S(1)}, u32[]{:S(2)}, u32[]{:S(2)}) collective-permute-start(bf16[256,128]{1,0:T(8,128)(2,1)S(1)} %get-tuple-element.64), channel_id=1, source_target_pairs={{0,4},{4,0},{8,12},{12,8},{1,5},{5,1},{9,13},{13,9},{2,6},{6,2},{1... | collective-permute-start | bytes 196616 | tf_op jit(solution)/shard_map/ppermute | solution.py:126
  40.3 5.4 %collective-permute-start.14 = (bf16[256,128]{1,0:T(8,128)(2,1)S(1)}, bf16[256,128]{1,0:T(8,128)(2,1)S(1)}, u32[]{:S(2)}, u32[]{:S(2)}) collective-permute-start(bf16[256,128]{1,0:T(8,128)(2,1)S(1)} %get-tuple-element.65), channel_id=1, source_target_pairs={{0,8},{4,12},{8,0},{12,4},{1,9},{5,13},{9,1},{13,5},{2,10},{6,14},... | collective-permute-start | bytes 196616 | tf_op jit(solution)/shard_map/ppermute | solution.py:126
  42.9 6.1 %collective-permute-start.15 = (bf16[256,128]{1,0:T(8,128)(2,1)S(1)}, bf16[256,128]{1,0:T(8,128)(2,1)S(1)}, u32[]{:S(2)}, u32[]{:S(2)}) collective-permute-start(bf16[256,128]{1,0:T(8,128)(2,1)S(1)} %get-tuple-element.66), channel_id=1, source_target_pairs={{0,12},{4,8},{8,4},{12,0},{1,13},{5,9},{9,5},{13,1},{2,14},{6,10},... | collective-permute-start | bytes 196616 | tf_op jit(solution)/shard_map/ppermute | solution.py:126
  45.5 13.2 %collective-permute-start.12 = (bf16[4,128,256]{2,1,0:T(8,128)(2,1)S(1)}, bf16[4,128,256]{2,1,0:T(8,128)(2,1)S(1)}, u32[]{:S(2)}, u32[]{:S(2)}) collective-permute-start(bf16[4,128,256]{2,1,0:T(8,128)(2,1)S(1)} %pad_maximum_fusion.refs_0_), channel_id=1, source_target_pairs={{0,2},{1,3},{2,0},{3,1},{4,6},{5,7},{6,4},{7,5},{8,10},{9,11},{10,... | collective-permute-start | bytes 786440 | tf_op jit(solution)/shard_map/ppermute | solution.py:126
  51.4 7.3 %collective-permute-start.19 = (bf16[2,256,128]{2,1,0:T(8,128)(2,1)S(1)}, bf16[2,256,128]{2,1,0:T(8,128)(2,1)S(1)}, u32[]{:S(2)}, u32[]{:S(2)}) collective-permute-start(bf16[2,256,128]{2,1,0:T(8,128)(2,1)S(1)} %get-tuple-element.74), channel_id=1, source_target_pairs={{0,16},{16,0},{1,17},{17,1},{2,18},{18,2},{3,19},{19,3},{4,20},{20... | collective-permute-start | bytes 393224 | tf_op jit(solution)/shard_map/ppermute | solution.py:126
  52.5 6.2 %collective-permute-start.21 = (bf16[128,256]{1,0:T(8,128)(2,1)S(1)}, bf16[128,256]{1,0:T(8,128)(2,1)S(1)}, u32[]{:S(2)}, u32[]{:S(2)}) collective-permute-start(bf16[128,256]{1,0:T(8,128)(2,1)S(1)} %get-tuple-element.73), channel_id=1, source_target_pairs={{0,12},{4,8},{8,4},{12,0},{1,13},{5,9},{9,5},{13,1},{2,14},{6,10},... | collective-permute-start | bytes 196616 | tf_op jit(solution)/shard_map/ppermute | solution.py:126
  54.8 5.2 %collective-permute-start.20 = (bf16[128,256]{1,0:T(8,128)(2,1)S(1)}, bf16[128,256]{1,0:T(8,128)(2,1)S(1)}, u32[]{:S(2)}, u32[]{:S(2)}) collective-permute-start(bf16[128,256]{1,0:T(8,128)(2,1)S(1)} %get-tuple-element.73), channel_id=1, source_target_pairs={{0,8},{4,12},{8,0},{12,4},{1,9},{5,13},{9,1},{13,5},{2,10},{6,14},... | collective-permute-start | bytes 196616 | tf_op jit(solution)/shard_map/ppermute | solution.py:126
  54.8 5.2 %collective-permute-start.18 = (bf16[128,256]{1,0:T(8,128)(2,1)S(1)}, bf16[128,256]{1,0:T(8,128)(2,1)S(1)}, u32[]{:S(2)}, u32[]{:S(2)}) collective-permute-start(bf16[128,256]{1,0:T(8,128)(2,1)S(1)} %get-tuple-element.73), channel_id=1, source_target_pairs={{0,4},{4,0},{8,12},{12,8},{1,5},{5,1},{9,13},{13,9},{2,6},{6,2},{1... | collective-permute-start | bytes 196616 | tf_op jit(solution)/shard_map/ppermute | solution.py:126
  58.6 4.1 %collective-permute-start.23 = (bf16[4,128,256]{2,1,0:T(8,128)(2,1)S(1)}, bf16[4,128,256]{2,1,0:T(8,128)(2,1)S(1)}, u32[]{:S(2)}, u32[]{:S(2)}) collective-permute-start(bf16[4,128,256]{2,1,0:T(8,128)(2,1)S(1)} %pad_maximum_fusion.refs_0_), channel_id=1, source_target_pairs={{0,1},{1,0},{2,3},{3,2},{4,5},{5,4},{6,7},{7,6},{8,9},{9,8},{10,11... | collective-permute-start | bytes 786440 | tf_op jit(solution)/shard_map/ppermute | solution.py:126
  60.2 9.9 %collective-permute-start.22 = (bf16[4,128,256]{2,1,0:T(8,128)(2,1)S(1)}, bf16[4,128,256]{2,1,0:T(8,128)(2,1)S(1)}, u32[]{:S(2)}, u32[]{:S(2)}) collective-permute-start(bf16[4,128,256]{2,1,0:T(8,128)(2,1)S(1)} %pad_maximum_fusion.1.refs_2_), channel_id=1, source_target_pairs={{0,2},{1,3},{2,0},{3,1},{4,6},{5,7},{6,4},{7,5},{8,10},{9,11},{10,... | collective-permute-start | bytes 786440 | tf_op jit(solution)/shard_map/ppermute | solution.py:126
  60.8 9.4 %collective-permute-start.25 = (bf16[2,256,128]{2,1,0:T(8,128)(2,1)S(1)}, bf16[2,256,128]{2,1,0:T(8,128)(2,1)S(1)}, u32[]{:S(2)}, u32[]{:S(2)}) collective-permute-start(bf16[2,256,128]{2,1,0:T(8,128)(2,1)S(1)} %broadcast_select_fusion.1), channel_id=1, source_target_pairs={{0,8},{4,12},{8,0},{12,4},{1,9},{5,13},{9,1},{13,5},{2,10},{6,14},... | collective-permute-start | bytes 393224 | tf_op jit(solution)/shard_map/ppermute | solution.py:126
  62.8 7.5 %collective-permute-start.13 = (bf16[4,128,256]{2,1,0:T(8,128)(2,1)S(1)}, bf16[4,128,256]{2,1,0:T(8,128)(2,1)S(1)}, u32[]{:S(2)}, u32[]{:S(2)}) collective-permute-start(bf16[4,128,256]{2,1,0:T(8,128)(2,1)S(1)} %collective-permute-done.12.refs_0_), channel_id=1, source_target_pairs={{0,1},{1,0},{2,3},{3,2},{4,5},{5,4},{6,7},{7,6},{8,9},{9,8},{10,11... | collective-permute-start | bytes 786440 | tf_op jit(solution)/shard_map/ppermute | solution.py:126
  (9 other events, 78.6 us)

commit v5 on v4

--- a/solution.py
+++ b/solution.py
@@ -419,8 +419,10 @@
 
 
 def dot_fine(left, right, dims):
-    return (
-        dot(left[0], right[0], dims) + dot(left[0], right[1], dims) + dot(left[1], right[0], dims)
+    return dot(
+        jnp.concatenate([left[0], left[0], left[1]], axis=1),
+        jnp.concatenate([right[0], right[1], right[0]], axis=1),
+        dims,
     )
 
 

time: 75.7 us -> 75.5 us (level)
  no operation moved by 1% of the time
where the time goes in v5:
time: 75.5 us; the launch traced here: 75.4 us
  starting transfers between devices  32.9 us (44%)
  Pallas kernels  23.8 us (32%)
  waiting for transfers between devices  17.4 us (23%)
  between operations  0.88 us (1%)
    ppermute x27, starting transfers between devices, swap(): lax.ppermute(array, axis, [(i, i ^ bit) for i in range(size)])  32.9 us
    ppermute x27, waiting for transfers between devices, swap(): lax.ppermute(array, axis, [(i, i ^ bit) for i in range(size)])  17.4 us
    pallas_call x2, Pallas kernels, grad_rows(): pl.pallas_call(kernel, name='grad_rows', grid_spec=pltpu.PrefetchScalarGr...  7.56 us
    pallas_call x2, Pallas kernels, streamed_product(): pl.pallas_call(streamed_product_kernel, name='streamed_product', grid_spe...  6.33 us
    pallas_call x2, Pallas kernels, attention(): pl.pallas_call(attention_kernel, name='attention', grid_spec=pltpu.Prefet...  4.66 us
    pallas_call x1, Pallas kernels, load_weights(): pl.pallas_call(load_kernel, name='load_weights', grid_spec=pltpu.Prefetch...  2.86 us
    pallas_call x2, Pallas kernels, half_product(): pl.pallas_call(half_product_kernel, in_specs=[vmem] * 2, out_specs=vmem,...  2.01 us
  transfers between devices with their start and end apart: 27, of which 10 were waited for; matrix products, arithmetic and copies ran while one was open for 0% of the time, Pallas kernels for 22%

profile of v5, /device:TPU:0, one launch (start us, length us, event | category | flops | bytes accessed | tf_op | source)
XLA Modules:
  0.0 75.4 jit_solution(14967243024011142608)
XLA Ops:
  0.6 3.2 %streamed_product.3 = bf16[2,4,256,128]{3,2,1,0:T(8,128)(2,1)S(1)} custom-call(s32[1]{0:T(128)} %bitcast.5.core_ref, bf16[256,1536]{1,0:T(8,128)(2,1)} %refs_4_.3, bf16[2048,1536]{1,0:T(8,128)(2,1)} %weight_ref.4), custom_call_target="tpu_custom_call" | custom-call | flops 805306368 | bytes 3932160 | tf_op jit(solution)/shard_map/streamed_product/pallas_call | solution.py:161
  4.4 2.6 %collective-permute-start.2 = (bf16[256,1536]{1,0:T(8,128)(2,1)S(1)}, bf16[256,1536]{1,0:T(8,128)(2,1)S(1)}, u32[]{:S(2)}, u32[]{:S(2)}) collective-permute-start(bf16[256,1536]{1,0:T(8,128)(2,1)S(1)} %copy-done), channel_id=1, source_target_pairs={{0,16},{16,0},{1,17},{17,1},{2,18},{18,2},{3,19},{19,3},{4,20},{20... | collective-permute-start | bytes 2359304 | tf_op jit(solution)/shard_map/ppermute | solution.py:126
  7.0 3.1 %streamed_product.2.kept_ref = f32[2,4,256,128]{3,2,1,0:T(8,128)S(1)} custom-call(s32[1]{0:T(128)} %bitcast.4.core_ref, bf16[256,1536]{1,0:T(8,128)(2,1)} %refs_4_.3, bf16[2048,1536]{1,0:T(8,128)(2,1)} %weight_ref.4), custom_call_target="tpu_custom_call" | custom-call | flops 805306368 | bytes 3932160 | tf_op jit(solution)/shard_map/streamed_product/pallas_call | solution.py:161
  10.3 1.6 %collective-permute-start.1 = (bf16[4,256,128]{2,1,0:T(8,128)(2,1)S(1)}, bf16[4,256,128]{2,1,0:T(8,128)(2,1)S(1)}, u32[]{:S(2)}, u32[]{:S(2)}) collective-permute-start(bf16[4,256,128]{2,1,0:T(8,128)(2,1)S(1)} %get-tuple-element.45), channel_id=1, source_target_pairs={{0,2},{1,3},{2,0},{3,1},{4,6},{5,7},{6,4},{7,5},{8,10},{9,11},{10,... | collective-permute-start | bytes 786440 | tf_op jit(solution)/shard_map/ppermute | solution.py:126
  12.0 2.7 %collective-permute-start.3 = (bf16[544,128]{1,0:T(8,128)(2,1)S(1)}, bf16[544,128]{1,0:T(8,128)(2,1)S(1)}, u32[]{:S(2)}, u32[]{:S(2)}) collective-permute-start(bf16[544,128]{1,0:T(8,128)(2,1)S(1)} %get-tuple-element.47), channel_id=1, source_target_pairs={{0,8},{4,12},{8,0},{12,4},{1,9},{5,13},{9,1},{13,5},{2,10},{6,14},... | collective-permute-start | bytes 417800 | tf_op jit(solution)/shard_map/ppermute | solution.py:126
  14.6 2.9 %load_weights.1 = (bf16[4,256,1536]{2,1,0:T(8,128)(2,1)S(1)}, bf16[4,256,1536]{2,1,0:T(8,128)(2,1)S(1)}) custom-call(s32[1]{0:T(128)} %bitcast.4.core_ref, bf16[2048,1536]{1,0:T(8,128)(2,1)} %weight_ref.4), custom_call_target="tpu_custom_call" | custom-call | tf_op jit(solution)/shard_map/load_weights/pallas_call | solution.py:209
  18.8 3.7 %collective-permute-start.4 = (bf16[256,128]{1,0:T(8,128)(2,1)S(1)}, bf16[256,128]{1,0:T(8,128)(2,1)S(1)}, u32[]{:S(2)}, u32[]{:S(2)}) collective-permute-start(bf16[256,128]{1,0:T(8,128)(2,1)S(1)} %get-tuple-element.54), channel_id=1, source_target_pairs={{0,12},{4,8},{8,4},{12,0},{1,13},{5,9},{9,5},{13,1},{2,14},{6,10},... | collective-permute-start | bytes 196616 | tf_op jit(solution)/shard_map/ppermute | solution.py:126
  23.2 1.9 %collective-permute-done.2.hidden_ref.refs_5_ = bf16[256,1536]{1,0:T(8,128)(2,1)S(1)} collective-permute-done((bf16[256,1536]{1,0:T(8,128)(2,1)S(1)}, bf16[256,1536]{1,0:T(8,128)(2,1)S(1)}, u32[]{:S(2)}, u32[]{:S(2)}) %collective-permute-start.2) | collective-permute-done | bytes 786464 | tf_op jit(solution)/shard_map/ppermute | solution.py:126
  26.2 1.5 %collective-permute-done.5.mid_ref = bf16[256,128]{1,0:T(8,128)(2,1)S(1)} collective-permute-done((bf16[256,128]{1,0:T(8,128)(2,1)S(1)}, bf16[256,128]{1,0:T(8,128)(2,1)S(1)}, u32[]{:S(2)}, u32[]{:S(2)}) %collective-permute-start.5) | collective-permute-done | bytes 65568 | tf_op jit(solution)/shard_map/ppermute | solution.py:126
  29.7 1.6 %collective-permute-start.9 = (bf16[4,256,128]{2,1,0:T(8,128)(2,1)S(1)}, bf16[4,256,128]{2,1,0:T(8,128)(2,1)S(1)}, u32[]{:S(2)}, u32[]{:S(2)}) collective-permute-start(bf16[4,256,128]{2,1,0:T(8,128)(2,1)S(1)} %get-tuple-element.58), channel_id=1, source_target_pairs={{0,2},{1,3},{2,0},{3,1},{4,6},{5,7},{6,4},{7,5},{8,10},{9,11},{10,... | collective-permute-start | bytes 786440 | tf_op jit(solution)/shard_map/ppermute | solution.py:126
  31.3 2.3 %attention.2 = (bf16[2,256,128]{2,1,0:T(8,128)(2,1)S(1)}, bf16[128,256]{1,0:T(8,128)(2,1)S(1)}) custom-call(s32[1]{0:T(128)} %bitcast.which_ref.home_ref, f32[256,128]{1,0:T(8,128)S(1)} %get-tuple-element.59.kept_ref, bf16[256,128]{1,0:T(8,128)(2,1)S(1)} %collective-permute-done.4.near_ref, bf16[256,128]{1,0:T(8,128)(2,1)S(1)} %collective-permute-done.5.mid_ref, ...), custom_call_target="tpu_custom_call" | custom-call | flops 402653184 | bytes 524288 | tf_op jit(solution)/shard_map/attention/pallas_call | solution.py:520
  33.7 2.6 %collective-permute-start.11 = (bf16[128,256]{1,0:T(8,128)(2,1)S(1)}, bf16[128,256]{1,0:T(8,128)(2,1)S(1)}, u32[]{:S(2)}, u32[]{:S(2)}) collective-permute-start(bf16[128,256]{1,0:T(8,128)(2,1)S(1)} %get-tuple-element.61), channel_id=1, source_target_pairs={{0,12},{4,8},{8,4},{12,0},{1,13},{5,9},{9,5},{13,1},{2,14},{6,10},... | collective-permute-start | bytes 196616 | tf_op jit(solution)/shard_map/ppermute | solution.py:126
  36.2 1.9 %collective-permute-start.8 = (bf16[128,256]{1,0:T(8,128)(2,1)S(1)}, bf16[128,256]{1,0:T(8,128)(2,1)S(1)}, u32[]{:S(2)}, u32[]{:S(2)}) collective-permute-start(bf16[128,256]{1,0:T(8,128)(2,1)S(1)} %get-tuple-element.61), channel_id=1, source_target_pairs={{0,4},{4,0},{8,12},{12,8},{1,5},{5,1},{9,13},{13,9},{2,6},{6,2},{1... | collective-permute-start | bytes 196616 | tf_op jit(solution)/shard_map/ppermute | solution.py:126
  40.2 2.6 %collective-permute-start.14 = (bf16[256,128]{1,0:T(8,128)(2,1)S(1)}, bf16[256,128]{1,0:T(8,128)(2,1)S(1)}, u32[]{:S(2)}, u32[]{:S(2)}) collective-permute-start(bf16[256,128]{1,0:T(8,128)(2,1)S(1)} %get-tuple-element.65), channel_id=1, source_target_pairs={{0,8},{4,12},{8,0},{12,4},{1,9},{5,13},{9,1},{13,5},{2,10},{6,14},... | collective-permute-start | bytes 196616 | tf_op jit(solution)/shard_map/ppermute | solution.py:126
  42.8 2.5 %collective-permute-start.15 = (bf16[256,128]{1,0:T(8,128)(2,1)S(1)}, bf16[256,128]{1,0:T(8,128)(2,1)S(1)}, u32[]{:S(2)}, u32[]{:S(2)}) collective-permute-start(bf16[256,128]{1,0:T(8,128)(2,1)S(1)} %get-tuple-element.66), channel_id=1, source_target_pairs={{0,12},{4,8},{8,4},{12,0},{1,13},{5,9},{9,5},{13,1},{2,14},{6,10},... | collective-permute-start | bytes 196616 | tf_op jit(solution)/shard_map/ppermute | solution.py:126
  45.7 3.2 %collective-permute-done.15.mid_ref = bf16[256,128]{1,0:T(8,128)(2,1)S(1)} collective-permute-done((bf16[256,128]{1,0:T(8,128)(2,1)S(1)}, bf16[256,128]{1,0:T(8,128)(2,1)S(1)}, u32[]{:S(2)}, u32[]{:S(2)}) %collective-permute-start.15) | collective-permute-done | bytes 65568 | tf_op jit(solution)/shard_map/ppermute | solution.py:126
  48.8 2.3 %attention.3 = (bf16[2,256,128]{2,1,0:T(8,128)(2,1)S(1)}, bf16[128,256]{1,0:T(8,128)(2,1)S(1)}) custom-call(s32[1]{0:T(128)} %bitcast.which_ref.home_ref, f32[256,128]{1,0:T(8,128)S(1)} %get-tuple-element.71.kept_ref, bf16[256,128]{1,0:T(8,128)(2,1)S(1)} %collective-permute-done.14.near_ref, bf16[256,128]{1,0:T(8,128)(2,1)S(1)} %collective-permute-done.15.mid_ref, ...), custom_call_target="tpu_custom_call" | custom-call | flops 402653184 | bytes 524288 | tf_op jit(solution)/shard_map/attention/pallas_call | solution.py:520
  52.3 2.3 %collective-permute-start.21 = (bf16[128,256]{1,0:T(8,128)(2,1)S(1)}, bf16[128,256]{1,0:T(8,128)(2,1)S(1)}, u32[]{:S(2)}, u32[]{:S(2)}) collective-permute-start(bf16[128,256]{1,0:T(8,128)(2,1)S(1)} %get-tuple-element.73), channel_id=1, source_target_pairs={{0,12},{4,8},{8,4},{12,0},{1,13},{5,9},{9,5},{13,1},{2,14},{6,10},... | collective-permute-start | bytes 196616 | tf_op jit(solution)/shard_map/ppermute | solution.py:126
  54.6 2.1 %collective-permute-start.18 = (bf16[128,256]{1,0:T(8,128)(2,1)S(1)}, bf16[128,256]{1,0:T(8,128)(2,1)S(1)}, u32[]{:S(2)}, u32[]{:S(2)}) collective-permute-start(bf16[128,256]{1,0:T(8,128)(2,1)S(1)} %get-tuple-element.73), channel_id=1, source_target_pairs={{0,4},{4,0},{8,12},{12,8},{1,5},{5,1},{9,13},{13,9},{2,6},{6,2},{1... | collective-permute-start | bytes 196616 | tf_op jit(solution)/shard_map/ppermute | solution.py:126
  56.7 1.8 %collective-permute-done.21 = bf16[128,256]{1,0:T(8,128)(2,1)S(1)} collective-permute-done((bf16[128,256]{1,0:T(8,128)(2,1)S(1)}, bf16[128,256]{1,0:T(8,128)(2,1)S(1)}, u32[]{:S(2)}, u32[]{:S(2)}) %collective-permute-start.21) | collective-permute-done | bytes 65568 | tf_op jit(solution)/shard_map/ppermute | solution.py:126
  60.5 2.0 %collective-permute-start.25 = (bf16[2,256,128]{2,1,0:T(8,128)(2,1)S(1)}, bf16[2,256,128]{2,1,0:T(8,128)(2,1)S(1)}, u32[]{:S(2)}, u32[]{:S(2)}) collective-permute-start(bf16[2,256,128]{2,1,0:T(8,128)(2,1)S(1)} %broadcast_select_fusion.1), channel_id=1, source_target_pairs={{0,8},{4,12},{8,0},{12,4},{1,9},{5,13},{9,1},{13,5},{2,10},{6,14},... | collective-permute-start | bytes 393224 | tf_op jit(solution)/shard_map/ppermute | solution.py:126
  62.6 3.7 %grad_rows.2 = (f32[2048,1536]{1,0:T(8,128)}, f32[8,128]{1,0:T(8,128)S(1)}) custom-call(s32[8]{0:T(128)S(1)} %pad_add_fusion.1.table_ref, bf16[4,128,256]{2,1,0:T(8,128)(2,1)S(1)} %pad_maximum_fusion.refs_0_, bf16[4,128,256]{2,1,0:T(8,128)(2,1)S(1)} %collective-permute-done.23.refs_1_, bf16[4,128,256]{2,1,0:T(8,128)(2,1)S(1)} %pad_maximum_fusion.1.refs_2_, ...), custom_call_target="tpu_custom_call" | custom-call | flops 1610612736 | bytes 6291456 | tf_op jit(solution)/shard_map/grad_rows/pallas_call | solution.py:303
  66.3 3.7 %collective-permute-done.25.refs_8_ = bf16[2,256,128]{2,1,0:T(8,128)(2,1)S(1)} collective-permute-done((bf16[2,256,128]{2,1,0:T(8,128)(2,1)S(1)}, bf16[2,256,128]{2,1,0:T(8,128)(2,1)S(1)}, u32[]{:S(2)}, u32[]{:S(2)}) %collective-permute-start.25) | collective-permute-done | bytes 131104 | tf_op jit(solution)/shard_map/ppermute | solution.py:126
  71.5 3.9 %grad_rows.3 = (f32[2048,1536]{1,0:T(8,128)}, bf16[2,256,256]{2,1,0:T(8,128)(2,1)}) custom-call(s32[8]{0:T(128)S(1)} %pad_add_fusion.table_ref, s32[1]{0:T(128)} %bitcast.which_ref.home_ref, s32[1]{0:T(128)} %bitcast.1.dp_ref, bf16[4,128,256]{2,1,0:T(8,128)(2,1)S(1)} %collective-permute-done.12.refs_0_, ...), custom_call_target="tpu_custom_call", output_to_operand_aliasing={{0}: (13, {})} | custom-call | flops 1610612736 | bytes 6291456 | tf_op jit(solution)/shard_map/grad_rows/pallas_call | solution.py:303
  (68 shorter events, 13.0 us)
Async XLA Ops:
  3.9 6.2 %collective-permute-start = (bf16[2,4,256,128]{3,2,1,0:T(8,128)(2,1)S(1)}, bf16[2,4,256,128]{3,2,1,0:T(8,128)(2,1)S(1)}, u32[]{:S(2)}, u32[]{:S(2)}) collective-permute-start(bf16[2,4,256,128]{3,2,1,0:T(8,128)(2,1)S(1)} %streamed_product.3), channel_id=1, source_target_pairs={{0,1},{1,0},{2,3},{3,2},{4,5},{5,4},{6,7},{7,6},{8,9},{9,8},{10,11... | collective-permute-start | bytes 1572872 | tf_op jit(solution)/shard_map/ppermute | solution.py:126
  4.4 20.7 %collective-permute-start.2 = (bf16[256,1536]{1,0:T(8,128)(2,1)S(1)}, bf16[256,1536]{1,0:T(8,128)(2,1)S(1)}, u32[]{:S(2)}, u32[]{:S(2)}) collective-permute-start(bf16[256,1536]{1,0:T(8,128)(2,1)S(1)} %copy-done), channel_id=1, source_target_pairs={{0,16},{16,0},{1,17},{17,1},{2,18},{18,2},{3,19},{19,3},{4,20},{20... | collective-permute-start | bytes 2359304 | tf_op jit(solution)/shard_map/ppermute | solution.py:126
  10.3 8.4 %collective-permute-start.1 = (bf16[4,256,128]{2,1,0:T(8,128)(2,1)S(1)}, bf16[4,256,128]{2,1,0:T(8,128)(2,1)S(1)}, u32[]{:S(2)}, u32[]{:S(2)}) collective-permute-start(bf16[4,256,128]{2,1,0:T(8,128)(2,1)S(1)} %get-tuple-element.45), channel_id=1, source_target_pairs={{0,2},{1,3},{2,0},{3,1},{4,6},{5,7},{6,4},{7,5},{8,10},{9,11},{10,... | collective-permute-start | bytes 786440 | tf_op jit(solution)/shard_map/ppermute | solution.py:126
  12.0 11.2 %collective-permute-start.3 = (bf16[544,128]{1,0:T(8,128)(2,1)S(1)}, bf16[544,128]{1,0:T(8,128)(2,1)S(1)}, u32[]{:S(2)}, u32[]{:S(2)}) collective-permute-start(bf16[544,128]{1,0:T(8,128)(2,1)S(1)} %get-tuple-element.47), channel_id=1, source_target_pairs={{0,8},{4,12},{8,0},{12,4},{1,9},{5,13},{9,1},{13,5},{2,10},{6,14},... | collective-permute-start | bytes 417800 | tf_op jit(solution)/shard_map/ppermute | solution.py:126
  18.8 7.4 %collective-permute-start.4 = (bf16[256,128]{1,0:T(8,128)(2,1)S(1)}, bf16[256,128]{1,0:T(8,128)(2,1)S(1)}, u32[]{:S(2)}, u32[]{:S(2)}) collective-permute-start(bf16[256,128]{1,0:T(8,128)(2,1)S(1)} %get-tuple-element.54), channel_id=1, source_target_pairs={{0,12},{4,8},{8,4},{12,0},{1,13},{5,9},{9,5},{13,1},{2,14},{6,10},... | collective-permute-start | bytes 196616 | tf_op jit(solution)/shard_map/ppermute | solution.py:126
  22.4 5.3 %collective-permute-start.5 = (bf16[256,128]{1,0:T(8,128)(2,1)S(1)}, bf16[256,128]{1,0:T(8,128)(2,1)S(1)}, u32[]{:S(2)}, u32[]{:S(2)}) collective-permute-start(bf16[256,128]{1,0:T(8,128)(2,1)S(1)} %get-tuple-element.55), channel_id=1, source_target_pairs={{0,8},{4,12},{8,0},{12,4},{1,9},{5,13},{9,1},{13,5},{2,10},{6,14},... | collective-permute-start | bytes 196616 | tf_op jit(solution)/shard_map/ppermute | solution.py:126
  22.4 5.3 %collective-permute-start.6 = (bf16[256,128]{1,0:T(8,128)(2,1)S(1)}, bf16[256,128]{1,0:T(8,128)(2,1)S(1)}, u32[]{:S(2)}, u32[]{:S(2)}) collective-permute-start(bf16[256,128]{1,0:T(8,128)(2,1)S(1)} %get-tuple-element.56), channel_id=1, source_target_pairs={{0,4},{4,0},{8,12},{12,8},{1,5},{5,1},{9,13},{13,9},{2,6},{6,2},{1... | collective-permute-start | bytes 196616 | tf_op jit(solution)/shard_map/ppermute | solution.py:126
  29.7 9.0 %collective-permute-start.9 = (bf16[4,256,128]{2,1,0:T(8,128)(2,1)S(1)}, bf16[4,256,128]{2,1,0:T(8,128)(2,1)S(1)}, u32[]{:S(2)}, u32[]{:S(2)}) collective-permute-start(bf16[4,256,128]{2,1,0:T(8,128)(2,1)S(1)} %get-tuple-element.58), channel_id=1, source_target_pairs={{0,2},{1,3},{2,0},{3,1},{4,6},{5,7},{6,4},{7,5},{8,10},{9,11},{10,... | collective-permute-start | bytes 786440 | tf_op jit(solution)/shard_map/ppermute | solution.py:126
  33.7 6.5 %collective-permute-start.11 = (bf16[128,256]{1,0:T(8,128)(2,1)S(1)}, bf16[128,256]{1,0:T(8,128)(2,1)S(1)}, u32[]{:S(2)}, u32[]{:S(2)}) collective-permute-start(bf16[128,256]{1,0:T(8,128)(2,1)S(1)} %get-tuple-element.61), channel_id=1, source_target_pairs={{0,12},{4,8},{8,4},{12,0},{1,13},{5,9},{9,5},{13,1},{2,14},{6,10},... | collective-permute-start | bytes 196616 | tf_op jit(solution)/shard_map/ppermute | solution.py:126
  36.2 6.5 %collective-permute-start.10 = (bf16[128,256]{1,0:T(8,128)(2,1)S(1)}, bf16[128,256]{1,0:T(8,128)(2,1)S(1)}, u32[]{:S(2)}, u32[]{:S(2)}) collective-permute-start(bf16[128,256]{1,0:T(8,128)(2,1)S(1)} %get-tuple-element.61), channel_id=1, source_target_pairs={{0,8},{4,12},{8,0},{12,4},{1,9},{5,13},{9,1},{13,5},{2,10},{6,14},... | collective-permute-start | bytes 196616 | tf_op jit(solution)/shard_map/ppermute | solution.py:126
  36.2 9.1 %collective-permute-start.8 = (bf16[128,256]{1,0:T(8,128)(2,1)S(1)}, bf16[128,256]{1,0:T(8,128)(2,1)S(1)}, u32[]{:S(2)}, u32[]{:S(2)}) collective-permute-start(bf16[128,256]{1,0:T(8,128)(2,1)S(1)} %get-tuple-element.61), channel_id=1, source_target_pairs={{0,4},{4,0},{8,12},{12,8},{1,5},{5,1},{9,13},{13,9},{2,6},{6,2},{1... | collective-permute-start | bytes 196616 | tf_op jit(solution)/shard_map/ppermute | solution.py:126
  38.1 7.5 %collective-permute-start.17 = (bf16[544,128]{1,0:T(8,128)(2,1)S(1)}, bf16[544,128]{1,0:T(8,128)(2,1)S(1)}, u32[]{:S(2)}, u32[]{:S(2)}) collective-permute-start(bf16[544,128]{1,0:T(8,128)(2,1)S(1)} %broadcast_select_fusion), channel_id=1, source_target_pairs={{0,16},{16,0},{1,17},{17,1},{2,18},{18,2},{3,19},{19,3},{4,20},{20... | collective-permute-start | bytes 417800 | tf_op jit(solution)/shard_map/ppermute | solution.py:126
  38.8 6.9 %collective-permute-start.16 = (bf16[256,128]{1,0:T(8,128)(2,1)S(1)}, bf16[256,128]{1,0:T(8,128)(2,1)S(1)}, u32[]{:S(2)}, u32[]{:S(2)}) collective-permute-start(bf16[256,128]{1,0:T(8,128)(2,1)S(1)} %get-tuple-element.64), channel_id=1, source_target_pairs={{0,4},{4,0},{8,12},{12,8},{1,5},{5,1},{9,13},{13,9},{2,6},{6,2},{1... | collective-permute-start | bytes 196616 | tf_op jit(solution)/shard_map/ppermute | solution.py:126
  40.2 5.4 %collective-permute-start.14 = (bf16[256,128]{1,0:T(8,128)(2,1)S(1)}, bf16[256,128]{1,0:T(8,128)(2,1)S(1)}, u32[]{:S(2)}, u32[]{:S(2)}) collective-permute-start(bf16[256,128]{1,0:T(8,128)(2,1)S(1)} %get-tuple-element.65), channel_id=1, source_target_pairs={{0,8},{4,12},{8,0},{12,4},{1,9},{5,13},{9,1},{13,5},{2,10},{6,14},... | collective-permute-start | bytes 196616 | tf_op jit(solution)/shard_map/ppermute | solution.py:126
  42.8 6.1 %collective-permute-start.15 = (bf16[256,128]{1,0:T(8,128)(2,1)S(1)}, bf16[256,128]{1,0:T(8,128)(2,1)S(1)}, u32[]{:S(2)}, u32[]{:S(2)}) collective-permute-start(bf16[256,128]{1,0:T(8,128)(2,1)S(1)} %get-tuple-element.66), channel_id=1, source_target_pairs={{0,12},{4,8},{8,4},{12,0},{1,13},{5,9},{9,5},{13,1},{2,14},{6,10},... | collective-permute-start | bytes 196616 | tf_op jit(solution)/shard_map/ppermute | solution.py:126
  45.3 13.1 %collective-permute-start.12 = (bf16[4,128,256]{2,1,0:T(8,128)(2,1)S(1)}, bf16[4,128,256]{2,1,0:T(8,128)(2,1)S(1)}, u32[]{:S(2)}, u32[]{:S(2)}) collective-permute-start(bf16[4,128,256]{2,1,0:T(8,128)(2,1)S(1)} %pad_maximum_fusion.refs_0_), channel_id=1, source_target_pairs={{0,2},{1,3},{2,0},{3,1},{4,6},{5,7},{6,4},{7,5},{8,10},{9,11},{10,... | collective-permute-start | bytes 786440 | tf_op jit(solution)/shard_map/ppermute | solution.py:126
  51.2 7.3 %collective-permute-start.19 = (bf16[2,256,128]{2,1,0:T(8,128)(2,1)S(1)}, bf16[2,256,128]{2,1,0:T(8,128)(2,1)S(1)}, u32[]{:S(2)}, u32[]{:S(2)}) collective-permute-start(bf16[2,256,128]{2,1,0:T(8,128)(2,1)S(1)} %get-tuple-element.74), channel_id=1, source_target_pairs={{0,16},{16,0},{1,17},{17,1},{2,18},{18,2},{3,19},{19,3},{4,20},{20... | collective-permute-start | bytes 393224 | tf_op jit(solution)/shard_map/ppermute | solution.py:126
  52.3 6.2 %collective-permute-start.21 = (bf16[128,256]{1,0:T(8,128)(2,1)S(1)}, bf16[128,256]{1,0:T(8,128)(2,1)S(1)}, u32[]{:S(2)}, u32[]{:S(2)}) collective-permute-start(bf16[128,256]{1,0:T(8,128)(2,1)S(1)} %get-tuple-element.73), channel_id=1, source_target_pairs={{0,12},{4,8},{8,4},{12,0},{1,13},{5,9},{9,5},{13,1},{2,14},{6,10},... | collective-permute-start | bytes 196616 | tf_op jit(solution)/shard_map/ppermute | solution.py:126
  54.6 5.2 %collective-permute-start.20 = (bf16[128,256]{1,0:T(8,128)(2,1)S(1)}, bf16[128,256]{1,0:T(8,128)(2,1)S(1)}, u32[]{:S(2)}, u32[]{:S(2)}) collective-permute-start(bf16[128,256]{1,0:T(8,128)(2,1)S(1)} %get-tuple-element.73), channel_id=1, source_target_pairs={{0,8},{4,12},{8,0},{12,4},{1,9},{5,13},{9,1},{13,5},{2,10},{6,14},... | collective-permute-start | bytes 196616 | tf_op jit(solution)/shard_map/ppermute | solution.py:126
  54.6 5.2 %collective-permute-start.18 = (bf16[128,256]{1,0:T(8,128)(2,1)S(1)}, bf16[128,256]{1,0:T(8,128)(2,1)S(1)}, u32[]{:S(2)}, u32[]{:S(2)}) collective-permute-start(bf16[128,256]{1,0:T(8,128)(2,1)S(1)} %get-tuple-element.73), channel_id=1, source_target_pairs={{0,4},{4,0},{8,12},{12,8},{1,5},{5,1},{9,13},{13,9},{2,6},{6,2},{1... | collective-permute-start | bytes 196616 | tf_op jit(solution)/shard_map/ppermute | solution.py:126
  58.4 4.1 %collective-permute-start.23 = (bf16[4,128,256]{2,1,0:T(8,128)(2,1)S(1)}, bf16[4,128,256]{2,1,0:T(8,128)(2,1)S(1)}, u32[]{:S(2)}, u32[]{:S(2)}) collective-permute-start(bf16[4,128,256]{2,1,0:T(8,128)(2,1)S(1)} %pad_maximum_fusion.refs_0_), channel_id=1, source_target_pairs={{0,1},{1,0},{2,3},{3,2},{4,5},{5,4},{6,7},{7,6},{8,9},{9,8},{10,11... | collective-permute-start | bytes 786440 | tf_op jit(solution)/shard_map/ppermute | solution.py:126
  60.0 9.9 %collective-permute-start.22 = (bf16[4,128,256]{2,1,0:T(8,128)(2,1)S(1)}, bf16[4,128,256]{2,1,0:T(8,128)(2,1)S(1)}, u32[]{:S(2)}, u32[]{:S(2)}) collective-permute-start(bf16[4,128,256]{2,1,0:T(8,128)(2,1)S(1)} %pad_maximum_fusion.1.refs_2_), channel_id=1, source_target_pairs={{0,2},{1,3},{2,0},{3,1},{4,6},{5,7},{6,4},{7,5},{8,10},{9,11},{10,... | collective-permute-start | bytes 786440 | tf_op jit(solution)/shard_map/ppermute | solution.py:126
  60.5 9.4 %collective-permute-start.25 = (bf16[2,256,128]{2,1,0:T(8,128)(2,1)S(1)}, bf16[2,256,128]{2,1,0:T(8,128)(2,1)S(1)}, u32[]{:S(2)}, u32[]{:S(2)}) collective-permute-start(bf16[2,256,128]{2,1,0:T(8,128)(2,1)S(1)} %broadcast_select_fusion.1), channel_id=1, source_target_pairs={{0,8},{4,12},{8,0},{12,4},{1,9},{5,13},{9,1},{13,5},{2,10},{6,14},... | collective-permute-start | bytes 393224 | tf_op jit(solution)/shard_map/ppermute | solution.py:126
  62.6 7.5 %collective-permute-start.13 = (bf16[4,128,256]{2,1,0:T(8,128)(2,1)S(1)}, bf16[4,128,256]{2,1,0:T(8,128)(2,1)S(1)}, u32[]{:S(2)}, u32[]{:S(2)}) collective-permute-start(bf16[4,128,256]{2,1,0:T(8,128)(2,1)S(1)} %collective-permute-done.12.refs_0_), channel_id=1, source_target_pairs={{0,1},{1,0},{2,3},{3,2},{4,5},{5,4},{6,7},{7,6},{8,9},{9,8},{10,11... | collective-permute-start | bytes 786440 | tf_op jit(solution)/shard_map/ppermute | solution.py:126
  (9 other events, 78.4 us)
